TPU v7x, 128 devices: a whole 4x4x4 slice. The times are simulated.
128 devices in a mesh: leaf: 4 (over y), row: 8 (over z, core), col: 4 (over x).
Axes of the slice: x: 4, y: 4, z: 4, core: 2. Of those that a mesh axis runs over, the one named last changes fastest.
Arguments:
- sigma_top: float32 [1024, 1024], P(('leaf', 'row'), 'col')
- panels: float32 [4, 7, 1024, 512], P('leaf', None, 'row', 'col'), may hold values from -0.1875 to 0.1875
- inverse_diag: float32 [4, 7, 512, 512], P('leaf', None, 'col')
- slot_lists: int32 [4, 6, 8], P('leaf'), may hold values from -1 to 11, as said below
- parent_links: int32 [4, 4], P('leaf'), may hold values from 1 to 2
Outputs:
- ancestor_block: float32 [4, 7, 1024, 512], P('leaf', None, 'row', 'col')
- diagonal_block: float32 [4, 7, 512, 512], P('leaf', None, None, 'col')
Inputs may be any that keep to these rules, and one draw needn't show every extreme that they name: `slot_lists`: in every row, entries 0 to 3 are 8 to 11 in order (the parent's own tiles); then come 1 to 3 distinct parent ancestor slots, below 8 for supernodes 1 and 2 and below 4 for supernodes 3 to 6; the rest are -1, so every row has padding. `parent_links`: each supernode 3 to 6 has supernode 1 or 2 as its parent. `sigma_top`: symmetric.
All inputs are finite; a program needn't handle non-finite values.
Results may differ from a plain program's by a relative error of at most 0.0001.
Values sent between devices are 32-bit elements; how exact they have to be, the bound alone decides.
A program may use at most 128 MiB of HBM per device.

v0:
```python
import jax
import jax.numpy as jnp
from jax import lax
from jax.sharding import PartitionSpec as P

TILE = 128


def child_blocks(ancestors, products, diagonals, parent_ids, picks, tile):
    count_parents = ancestors.shape[0]
    slot_count = ancestors.shape[1] // tile
    own_width = diagonals.shape[1]
    own_tiles = own_width // tile
    tail = picks[:, own_tiles:]
    living = tail >= 0
    indices = jnp.maximum(tail, 0)
    child_count = tail.shape[0]
    tail_count = tail.shape[1]
    a_tiles = ancestors.reshape(count_parents, slot_count, tile, slot_count, tile)
    corner = a_tiles[parent_ids[:, None, None], indices[:, :, None], :, indices[:, None, :], :]
    corner = jnp.transpose(corner, (0, 1, 3, 2, 4))
    weights = (living[:, :, None] & living[:, None, :]).astype(jnp.float32)
    corner = corner * weights[:, :, None, :, None]
    corner = corner.reshape(child_count, tail_count * tile, tail_count * tile)
    p_tiles = products.reshape(count_parents, slot_count, tile, own_width)
    side = p_tiles[parent_ids[:, None], indices]
    side = side * living.astype(jnp.float32)[:, :, None, None]
    side = side.reshape(child_count, tail_count * tile, own_width)
    top_left = jnp.take(diagonals, parent_ids, axis=0)
    upper = jnp.concatenate([top_left, -jnp.transpose(side, (0, 2, 1))], axis=2)
    lower = jnp.concatenate([-side, corner], axis=2)
    return jnp.concatenate([upper, lower], axis=1)


def body(sigma_top, panels, inverse_diag, slot_lists, parent_links):
    highest = lax.Precision.HIGHEST
    row_count = lax.axis_size("row")
    col_count = lax.axis_size("col")
    row_index = lax.axis_index("row")
    col_index = lax.axis_index("col")
    panel_local = panels[0]
    inverse_local = inverse_diag[0]
    picks_all = slot_lists[0]
    parents = parent_links[0]
    block_rows = panel_local.shape[1]
    block_cols = panel_local.shape[2]
    diag_width = inverse_local.shape[2]
    diag_rows = diag_width // row_count
    tile = TILE
    top_rows = lax.all_gather(sigma_top, ("leaf", "row"), axis=0, tiled=True)
    top_full = lax.all_gather(top_rows, "col", axis=1, tiled=True)
    partial_factor = jnp.einsum("vrk,vkj->vrj", panel_local, inverse_local, precision=highest)
    inverse_band = lax.dynamic_slice_in_dim(inverse_local, row_index * diag_rows, diag_rows, 2)
    partial_gram = jnp.einsum("vki,vkj->vij", inverse_band, inverse_local, precision=highest)
    factor_rows = lax.psum(partial_factor, "col")
    gram_mine = lax.psum_scatter(partial_gram, "col", scatter_dimension=2, tiled=True)
    slots_here = block_rows // tile
    slot_ids = row_index * slots_here + jnp.arange(slots_here, dtype=jnp.int32)
    listed = jnp.take(picks_all, slot_ids, axis=1) >= 0
    living = jnp.concatenate([jnp.ones((1, slots_here), jnp.bool_), listed], axis=0)
    row_weight = jnp.repeat(living.astype(jnp.float32), tile, axis=1)
    factor_rows = factor_rows * row_weight[:, :, None]
    factor_mine = lax.dynamic_slice_in_dim(factor_rows, col_index * block_cols, block_cols, 2)
    ancestors = top_full[None]
    ancestor_parts = []
    diagonal_parts = []
    bounds = ((0, 1), (1, 3), (3, 7))
    for level_id, (first_node, last_node) in enumerate(bounds):
        factor_level = factor_mine[first_node:last_node]

        def contribute(start, count, ancestors=ancestors, factor_level=factor_level):
            strip = ancestors
            strip = lax.dynamic_slice_in_dim(strip, row_index * block_rows, block_rows, 2)
            return jnp.einsum("vrs,vsc->rvc", strip, factor_level, precision=highest)

        summed = lax.psum_scatter(
            contribute(jnp.int32(0), block_rows * lax.axis_size("row")),
            "row",
            scatter_dimension=0,
            tiled=True,
        )
        product_mine = jnp.transpose(summed, (1, 0, 2))
        partial_diag = jnp.einsum(
            "vrj,vrc->vjc", factor_rows[first_node:last_node], product_mine, precision=highest
        )
        diag_piece = lax.psum_scatter(partial_diag, "row", scatter_dimension=1, tiled=True)
        diag_piece = diag_piece + gram_mine[first_node:last_node]
        ancestor_parts.append(-product_mine)
        if level_id == 2:
            diag_cols = lax.all_gather(diag_piece, "row", axis=1, tiled=True)
        else:
            width_nodes = last_node - first_node
            product_all, diag_all = (
                lax.all_gather(product_mine[:, None], ("row", "col"), axis=1, tiled=True),
                lax.all_gather(diag_piece[:, None], ("row", "col"), axis=1, tiled=True),
            )
            product_full = product_all.reshape(
                width_nodes, row_count, col_count, block_rows, block_cols
            )
            product_full = product_full.transpose(0, 1, 3, 2, 4).reshape(
                width_nodes, row_count * block_rows, col_count * block_cols
            )
            diag_full = diag_all.reshape(width_nodes, row_count, col_count, diag_rows, block_cols)
            diag_full = diag_full.transpose(0, 1, 3, 2, 4).reshape(
                width_nodes, row_count * diag_rows, col_count * block_cols
            )
            diag_cols = lax.dynamic_slice_in_dim(diag_full, col_index * block_cols, block_cols, 2)
            if level_id == 0:
                parent_ids = jnp.zeros((2,), jnp.int32)
                picks_level = picks_all[0:2]
            else:
                parent_ids = parents - 1
                picks_level = picks_all[2:6]
            ancestors = child_blocks(
                ancestors, product_full, diag_full, parent_ids, picks_level, tile
            )
        diagonal_parts.append(diag_cols)
    ancestor_block = jnp.concatenate(ancestor_parts, axis=0)[None]
    diagonal_block = jnp.concatenate(diagonal_parts, axis=0)[None]
    return (ancestor_block, diagonal_block)


def solution(mesh):
    return jax.shard_map(
        body,
        mesh=mesh,
        in_specs=(
            P(("leaf", "row"), "col"),
            P("leaf", None, "row", "col"),
            P("leaf", None, "col", None),
            P("leaf", None, None),
            P("leaf", None),
        ),
        out_specs=(P("leaf", None, "row", "col"), P("leaf", None, None, "col")),
        check_vma=False,
    )
```

profile of v0, /device:TPU:1, one launch (start us, length us, event | category | flops | bytes accessed | tf_op | source)
XLA Modules:
  0.0 642.9 jit_solution(15466048117871456007)
XLA Ops:
  13.4 44.3 %all-gather.12.cloned.1.call-done = f32[1024,256]{1,0:T(8,128)} async-done(((f32[32,256]{1,0:T(8,128)}), f32[1024,256]{1,0:T(8,128)}) %all-gather.12.cloned.1.call-update) | async-done | bytes 1048592 | tf_op jit(solution)/shard_map/all_gather | solution.py:50
  58.1 12.6 %all-reduce.3.cloned.1.call-done = f32[7,128,512]{2,1,0:T(8,128)} async-done(((f32[7,128,512]{2,1,0:T(8,128)}), f32[7,128,512]{2,1,0:T(8,128)}) %all-reduce.3.cloned.1.call-update) | async-done | bytes 1835024 | tf_op jit(solution)/shard_map/psum | solution.py:55
  73.9 46.3 %all-gather.14.cloned.1.call-done = f32[1024,1024]{1,0:T(8,128)} async-done(((f32[1024,256]{1,0:T(8,128)}), f32[1024,1024]{1,0:T(8,128)}) %all-gather.14.cloned.1.call-update) | async-done | bytes 4194320 | tf_op jit(solution)/shard_map/all_gather | solution.py:51
  125.1 26.5 %reduce-scatter.8.cloned.1.call-done = f32[128,1,128]{0,2,1:T(8,128)} async-done(((f32[1024,1,128]{0,2,1:T(8,128)}), f32[128,1,128]{0,2,1:T(8,128)}) %reduce-scatter.8.cloned.1.call-update) | async-done | bytes 65552 | tf_op jit(solution)/shard_map/reduce_scatter | solution.py:76
  154.0 23.1 %reduce-scatter.12.cloned.1.call-done = f32[7,64,128]{2,1,0:T(8,128)} async-done(((f32[7,64,512]{2,1,0:T(8,128)}), f32[7,64,128]{2,1,0:T(8,128)}) %reduce-scatter.12.cloned.1.call-update) | async-done | bytes 229392 | tf_op jit(solution)/shard_map/reduce_scatter | solution.py:56
  177.1 32.2 %reduce-scatter.10.cloned.1.call-done = f32[1,64,128]{2,1,0:T(8,128)} async-done(((f32[1,512,128]{2,1,0:T(8,128)}), f32[1,64,128]{2,1,0:T(8,128)}) %reduce-scatter.10.cloned.1.call-update) | async-done | bytes 32784 | tf_op jit(solution)/shard_map/reduce_scatter | solution.py:86
  230.0 26.9 %all-gather.18.cloned.1.call-done = f32[32,64,128]{2,1,0:T(8,128)} async-done(((f32[1,64,128]{2,1,0:T(8,128)}), f32[32,64,128]{2,1,0:T(8,128)}) %all-gather.18.cloned.1.call-update) | async-done | bytes 1048592 | tf_op jit(solution)/shard_map/all_gather | solution.py:95
  261.4 41.7 %all-gather.20.cloned.1.call-done = f32[4096,1,128]{0,2,1:T(8,128)} async-done(((f32[128,1,128]{0,2,1:T(8,128)}), f32[4096,1,128]{0,2,1:T(8,128)}) %all-gather.20.cloned.1.call-update) | async-done | bytes 2097168 | tf_op jit(solution)/shard_map/all_gather | solution.py:94
  323.8 5.4 copy.67
  338.5 28.2 %reduce-scatter.14.cloned.1.call-done = f32[128,2,128]{0,2,1:T(8,128)} async-done(((f32[1024,2,128]{0,2,1:T(8,128)}), f32[128,2,128]{0,2,1:T(8,128)}) %reduce-scatter.14.cloned.1.call-update) | async-done | bytes 131088 | tf_op jit(solution)/shard_map/reduce_scatter | solution.py:76
  369.4 30.1 %reduce-scatter.16.cloned.1.call-done = f32[2,64,128]{2,1,0:T(8,128)} async-done(((f32[2,512,128]{2,1,0:T(8,128)}), f32[2,64,128]{2,1,0:T(8,128)}) %reduce-scatter.16.cloned.1.call-update) | async-done | bytes 65552 | tf_op jit(solution)/shard_map/reduce_scatter | solution.py:86
  402.9 5.5 copy.91
  413.2 6.2 gather_fusion.4
  426.7 5.6 reshape.199
  432.3 16.3 %all-gather.22.cloned.1.call-done = f32[2,2048,128]{2,1,0:T(8,128)} async-done(((f32[2,64,128]{2,1,0:T(8,128)}), f32[2,2048,128]{2,1,0:T(8,128)}) %all-gather.22.cloned.1.call-update) | async-done | bytes 2097168 | tf_op jit(solution)/shard_map/all_gather | solution.py:95
  460.5 39.1 %all-gather.24.cloned.1.call-done = f32[2,4096,128]{1,2,0:T(8,128)} async-done(((f32[2,128,128]{1,2,0:T(8,128)}), f32[2,4096,128]{1,2,0:T(8,128)}) %all-gather.24.cloned.1.call-update) | async-done | bytes 4194320 | tf_op jit(solution)/shard_map/all_gather | solution.py:94
  499.6 6.0 reshape.197
  505.6 6.6 %copy.72 = f32[2,8,4,128,128]{3,4,2,1,0:T(8,128)} copy(f32[2,8,4,128,128]{3,2,1,4,0:T(4,128)} %reshape.197) | data formatting | bytes 8388608 | tf_op jit(solution)/shard_map/reshape | solution.py:97
  517.2 5.3 copy.73
  522.5 7.1 %fusion = (f32[4,512,512]{2,1,0:T(8,128)}, f32[4,512,512]{2,1,0:T(8,128)}) fusion(f32[4,512]{1,0:T(4,128)S(1)} %bitcast.161, f32[4,512,512]{2,1,0:T(8,128)} %gather_fusion.2, pred[4]{0:T(512)(128)(4,1)S(1)} %compare_and_fusion, f32[4,512,512]{2,1,0:T(8,128)} %bitcast.145), kind=kLoop, calls=%fused_computation.12 | loop fusion | flops 3145728 | bytes 16785412 | tf_op jit(solution)/shard_map/neg | solution.py:30
  529.6 5.2 copy.74
  540.4 29.7 %reduce-scatter.18.cloned.1.call-done = f32[128,4,128]{0,2,1:T(8,128)} async-done(((f32[1024,4,128]{0,2,1:T(8,128)}), f32[128,4,128]{0,2,1:T(8,128)}) %reduce-scatter.18.cloned.1.call-update) | async-done | bytes 262160 | tf_op jit(solution)/shard_map/reduce_scatter | solution.py:76
  573.9 31.0 %reduce-scatter.20.cloned.1.call-done = f32[4,64,128]{2,1,0:T(8,128)} async-done(((f32[4,512,128]{2,1,0:T(8,128)}), f32[4,64,128]{2,1,0:T(8,128)}) %reduce-scatter.20.cloned.1.call-update) | async-done | bytes 131088 | tf_op jit(solution)/shard_map/reduce_scatter | solution.py:86
  609.2 23.9 %all-gather.16.cloned.1.call-done = f32[4,512,128]{2,1,0:T(8,128)} async-done(((f32[4,64,128]{2,1,0:T(8,128)}), f32[4,512,128]{2,1,0:T(8,128)}) %all-gather.16.cloned.1.call-update) | async-done | bytes 1048592 | tf_op jit(solution)/shard_map/all_gather | solution.py:90
  (123 shorter events, 122.1 us)
Async XLA Ops:
  8.0 49.7 %all-gather.12.cloned.1.call-start = ((), (), s32[]{:S(2)}) async-start(), calls=%async_computation.8 | async-start | bytes 1081344 | tf_op jit(solution)/shard_map/all_gather | solution.py:50
  8.7 62.0 %all-reduce.3.cloned.1.call-start = ((), (), s32[]{:S(2)}) async-start(), calls=%async_computation.7 | async-start | bytes 3670016 | tf_op jit(solution)/shard_map/psum | solution.py:55
  13.4 44.4 %copy-start.9 = (s32[1,6,8]{2,0,1:T(1,128)S(1)}, s32[1,6,8]{2,0,1:T(1,128)}, u32[]{:S(2)}) copy-start(s32[1,6,8]{2,0,1:T(1,128)} %param.8) | copy-start | bytes 580
  13.4 106.8 %all-gather.14.cloned.1.call-start = ((), (), s32[]{:S(2)}) async-start(), calls=%async_computation.9 | async-start | bytes 5242880 | tf_op jit(solution)/shard_map/all_gather | solution.py:51
  57.7 93.9 %reduce-scatter.8.cloned.1.call-start = ((), (), s32[]{:S(2)}) async-start(), calls=%async_computation.10 | async-start | bytes 589824 | tf_op jit(solution)/shard_map/reduce_scatter | solution.py:76
  122.7 54.4 %reduce-scatter.12.cloned.1.call-start = ((), (), s32[]{:S(2)}) async-start(), calls=%async_computation.12 | async-start | bytes 1146880 | tf_op jit(solution)/shard_map/reduce_scatter | solution.py:56
  125.1 84.3 %reduce-scatter.10.cloned.1.call-start = ((), (), s32[]{:S(2)}) async-start(), calls=%async_computation.11 | async-start | bytes 294912 | tf_op jit(solution)/shard_map/reduce_scatter | solution.py:86
  153.9 103.0 %all-gather.18.cloned.1.call-start = ((), (), s32[]{:S(2)}) async-start(), calls=%async_computation.18 | async-start | bytes 1081344 | tf_op jit(solution)/shard_map/all_gather | solution.py:95
  210.8 92.3 %all-gather.20.cloned.1.call-start = ((), (), s32[]{:S(2)}) async-start(), calls=%async_computation.19 | async-start | bytes 2162688 | tf_op jit(solution)/shard_map/all_gather | solution.py:94
  211.3 155.3 %reduce-scatter.14.cloned.1.call-start = ((), (), s32[]{:S(2)}) async-start(), calls=%async_computation.13 | async-start | bytes 1179648 | tf_op jit(solution)/shard_map/reduce_scatter | solution.py:76
  317.5 3.3 copy-start.4
  329.1 7.2 %copy-start.3 = (f32[7,128,512]{2,1,0:T(8,128)S(1)}, f32[7,128,512]{2,1,0:T(8,128)}, u32[]{:S(2)}) copy-start(f32[7,128,512]{2,1,0:T(8,128)} %broadcast_multiply_fusion) | copy-start | bytes 5505028
  333.1 3.3 copy-start.2
  338.4 61.1 %copy-start.8 = (f32[7,64,128]{2,1,0:T(8,128)S(1)}, f32[7,64,128]{2,1,0:T(8,128)}, u32[]{:S(2)}) copy-start(f32[7,64,128]{2,1,0:T(8,128)} %reduce-scatter.12.cloned.1.call-done) | copy-start | bytes 688132
  338.4 63.8 %copy-start.10 = (s32[1,4]{1,0:T(1,128)S(1)}, s32[1,4]{1,0:T(1,128)}, u32[]{:S(2)}) copy-start(s32[1,4]{1,0:T(1,128)} %param.9) | copy-start | bytes 52
  338.4 61.1 %reduce-scatter.16.cloned.1.call-start = ((), (), s32[]{:S(2)}) async-start(), calls=%async_computation.14 | async-start | bytes 589824 | tf_op jit(solution)/shard_map/reduce_scatter | solution.py:86
  369.4 79.3 %all-gather.22.cloned.1.call-start = ((), (), s32[]{:S(2)}) async-start(), calls=%async_computation.20 | async-start | bytes 2162688 | tf_op jit(solution)/shard_map/all_gather | solution.py:95
  401.1 98.5 %all-gather.24.cloned.1.call-start = ((), (), s32[]{:S(2)}) async-start(), calls=%async_computation.21 | async-start | bytes 4325376 | tf_op jit(solution)/shard_map/all_gather | solution.py:94
  401.7 168.4 %reduce-scatter.18.cloned.1.call-start = ((), (), s32[]{:S(2)}) async-start(), calls=%async_computation.15 | async-start | bytes 2359296 | tf_op jit(solution)/shard_map/reduce_scatter | solution.py:76
  540.1 66.4 %copy-start.7 = (f32[128,1,128]{0,2,1:T(8,128)S(1)}, f32[128,1,128]{0,2,1:T(8,128)}, u32[]{:S(2)}) copy-start(f32[128,1,128]{0,2,1:T(8,128)} %reduce-scatter.8.cloned.1.call-done) | copy-start | bytes 196612
  540.1 64.8 %reduce-scatter.20.cloned.1.call-start = ((), (), s32[]{:S(2)}) async-start(), calls=%async_computation.16 | async-start | bytes 1179648 | tf_op jit(solution)/shard_map/reduce_scatter | solution.py:86
  573.8 33.2 %copy-start.5 = (f32[128,2,128]{0,2,1:T(8,128)S(1)}, f32[128,2,128]{0,2,1:T(8,128)}, u32[]{:S(2)}) copy-start(f32[128,2,128]{0,2,1:T(8,128)} %reduce-scatter.14.cloned.1.call-done) | copy-start | bytes 393220
  573.8 59.2 %all-gather.16.cloned.1.call-start = ((), (), s32[]{:S(2)}) async-start(), calls=%async_computation.17 | async-start | bytes 1179648 | tf_op jit(solution)/shard_map/all_gather | solution.py:90
  608.1 27.5 %copy-start.1 = (f32[1,7,128,512]{3,2,1,0:T(8,128)S(1)}, f32[1,7,128,512]{3,2,1,0:T(8,128)}, u32[]{:S(2)}) copy-start(f32[1,7,128,512]{3,2,1,0:T(8,128)} %param.7) | copy-start | bytes 5505028
  (2 other events, 3.2 us)
Sparse Core Ops, SparseCore 0:
  11.1 46.5 all-gather.11
  122.9 28.7 reduce-scatter.7
  154.2 22.8 reduce-scatter.11
  180.0 29.2 reduce-scatter.9
  212.0 44.8 all-gather.17
  259.0 44.0 all-gather.19
  338.6 28.0 reduce-scatter.13
  369.6 29.9 reduce-scatter.15
  402.7 45.9 all-gather.21
  450.9 48.6 all-gather.23
  540.2 29.8 reduce-scatter.17
  574.0 30.8 reduce-scatter.19
  607.2 25.7 all-gather.15
Sparse Core Ops, SparseCore 1:
  13.5 57.2 all-reduce.2
  72.3 47.8 all-gather.13
where the time goes:
time: 649 us; the launch traced here: 643 us
  waiting for transfers between devices  454 us (70%)
  local copies, waits for them, and re-layouts  114 us (18%)
  other arithmetic  32.6 us (5%)
  matrix products  24.6 us (4%)
  between operations  15.8 us (2%)
    reduce_scatter x3, waiting for transfers between devices, body(): lax.psum_scatter(partial_diag, 'row', scatter_dimension=1, tiled=True)  93.3 us
    reduce_scatter x3, waiting for transfers between devices, body(): lax.psum_scatter(contribute(jnp.int32(0), block_rows * lax.axis_size('row...  84.4 us
    all_gather x2, waiting for transfers between devices, body(): lax.all_gather(product_mine[:, None], ('row', 'col'), axis=1, tiled=True)  80.8 us
    all_gather x1, waiting for transfers between devices, body(): top_full = lax.all_gather(top_rows, 'col', axis=1, tiled=True)  46.3 us
    all_gather x1, waiting for transfers between devices, body(): top_rows = lax.all_gather(sigma_top, ('leaf', 'row'), axis=0, tiled=True)  44.3 us
    all_gather x2, waiting for transfers between devices, body(): lax.all_gather(diag_piece[:, None], ('row', 'col'), axis=1, tiled=True)  43.2 us
    all_gather x1, waiting for transfers between devices, body(): diag_cols = lax.all_gather(diag_piece, 'row', axis=1, tiled=True)  23.9 us
    reduce_scatter x1, waiting for transfers between devices, body(): lax.psum_scatter(partial_gram, 'col', scatter_dimension=2, tiled=True)  23.1 us
  transfers between devices with their start and end apart: 15, of which 15 were waited for; matrix products, arithmetic and copies ran while one was open for 12% of the time, Pallas kernels for 0%

commit v1 on v0

v1 whole, which is shorter than its diff:
```python
import jax
import jax.numpy as jnp
from jax import lax
from jax.sharding import PartitionSpec as P

TILE = 128
HIGHEST = lax.Precision.HIGHEST


def mm(a, b):
    return jnp.matmul(a, b, precision=HIGHEST, preferred_element_type=jnp.float32)


def tile_rows(matrix, index, tile):
    return lax.dynamic_slice_in_dim(matrix, index * tile, tile, 0)


def tile_cols(matrix, index, tile):
    return lax.dynamic_slice_in_dim(matrix, index * tile, tile, 1)


def scatter_factor(factor_col, slots, positions, tile):
    tiles = factor_col.reshape(slots.shape[0], tile, factor_col.shape[1])
    hits = slots[:, None] == jnp.arange(positions, dtype=slots.dtype)[None, :]
    present = jnp.any(hits, axis=0)
    source = jnp.argmax(hits, axis=0)
    moved = jnp.take(tiles, source, axis=0)
    moved = jnp.where(present[:, None, None], moved, 0.0)
    return moved.reshape(positions * tile, factor_col.shape[1])


def pick_transposed(column_block, picks, tile):
    tiles = column_block.reshape(-1, tile, tile)
    chosen = jnp.take(tiles, jnp.maximum(picks, 0), axis=0)
    chosen = jnp.where((picks >= 0)[:, None, None], chosen, 0.0)
    return jnp.transpose(chosen, (2, 0, 1)).reshape(tile, picks.shape[0] * tile)


def body(sigma_top, panels, inverse_diag, slot_lists, parent_links):
    tile = TILE
    row_count = lax.axis_size("row")
    col_count = lax.axis_size("col")
    leaf_count = lax.axis_size("leaf")
    r = lax.axis_index("row")
    c = lax.axis_index("col")
    panel = panels[0]
    inverse = inverse_diag[0]
    picks_all = slot_lists[0]
    parents = parent_links[0]
    nodes = panel.shape[0]
    width = inverse.shape[2]
    own_tiles = width // tile
    slot_count = picks_all.shape[1]
    positions = slot_count + own_tiles
    band = width // row_count

    partial_factor = mm(panel, inverse)
    factor_rows = lax.psum(partial_factor, "col")
    living = jnp.concatenate([jnp.ones((1, slot_count), jnp.bool_), picks_all >= 0], axis=0)
    live_here = jnp.take(living, r, axis=1).astype(jnp.float32)
    factor_rows = factor_rows * live_here[:, None, None]
    factor_tile = lax.dynamic_slice_in_dim(factor_rows, c * tile, tile, 2)
    factor_cols = lax.all_gather(factor_tile, "row", axis=1, tiled=True)

    inverse_band = lax.dynamic_slice_in_dim(inverse, r * band, band, 2)
    partial_gram = mm(jnp.transpose(inverse_band, (0, 2, 1)), inverse)
    gram_piece = lax.psum_scatter(partial_gram, "col", scatter_dimension=2, tiled=True)

    local_rows, local_cols = sigma_top.shape
    gathered = lax.all_gather(sigma_top, ("leaf", "row", "col"), axis=0)
    sigma = gathered.reshape(leaf_count * row_count, col_count, local_rows, local_cols)
    sigma = jnp.transpose(sigma, (0, 2, 1, 3)).reshape(
        leaf_count * row_count * local_rows, col_count * local_cols
    )

    def diag_partial(first, products):
        rows = factor_rows[first:first + products.shape[0]]
        return mm(jnp.transpose(rows, (0, 2, 1)), products)

    def reduce_and_gather(first, products):
        count = products.shape[0]
        piece = lax.psum_scatter(diag_partial(first, products), "row", scatter_dimension=1, tiled=True)
        piece = piece + gram_piece[first:first + count]
        both = jnp.concatenate([products, piece], axis=1)
        everything = lax.all_gather(both, ("row", "col"), axis=0)
        everything = everything.reshape(row_count, col_count, count, tile + band, tile)
        product_full = jnp.transpose(everything[:, :, :, :tile], (2, 0, 3, 1, 4)).reshape(
            count, row_count * tile, col_count * tile
        )
        diag_full = jnp.transpose(everything[:, :, :, tile:], (2, 0, 3, 1, 4)).reshape(
            count, row_count * band, col_count * tile
        )
        return product_full, diag_full

    own_row = jnp.minimum(r, own_tiles - 1)
    upper = r < own_tiles

    product_0 = mm(tile_rows(sigma, r, tile), factor_cols[0])
    product_full_0, diag_full_0 = reduce_and_gather(0, product_0[None])
    product_full_0 = product_full_0[0]
    diag_full_0 = diag_full_0[0]

    level_1 = []
    for node in (1, 2):
        slots = picks_all[node - 1]
        spread = scatter_factor(factor_cols[node], slots, positions, tile)
        top_row = jnp.concatenate(
            [-jnp.transpose(tile_cols(product_full_0, own_row, tile)), tile_rows(diag_full_0, own_row, tile)],
            axis=1,
        )
        source = slots[jnp.maximum(r, own_tiles)]
        source_row = jnp.maximum(source, 0)
        low_row = jnp.concatenate(
            [tile_rows(sigma, source_row, tile), -tile_rows(product_full_0, source_row, tile)], axis=1
        )
        low_row = jnp.where(source >= 0, low_row, 0.0)
        row = jnp.where(upper, top_row, low_row)
        level_1.append(mm(row, spread))
    product_1 = jnp.stack(level_1)
    product_full_1, diag_full_1 = reduce_and_gather(1, product_1)

    level_2 = []
    for node in range(3, nodes):
        slots = picks_all[node - 1]
        parent = parents[node - 3] - 1
        parent_slots = jnp.take(picks_all, parent, axis=0)
        product_p = jnp.take(product_full_1, parent, axis=0)
        diag_p = jnp.take(diag_full_1, parent, axis=0)
        spread = scatter_factor(factor_cols[node], slots, positions, tile)
        top_row = jnp.concatenate(
            [-jnp.transpose(tile_cols(product_p, own_row, tile)), tile_rows(diag_p, own_row, tile)], axis=1
        )
        source = slots[jnp.maximum(r, own_tiles)]
        source_row = jnp.clip(source, 0, own_tiles - 1)
        corner = pick_transposed(
            -tile_cols(product_full_0, source_row, tile), parent_slots[own_tiles:], tile
        )
        low_row = jnp.concatenate(
            [
                tile_rows(diag_full_0, source_row, tile),
                corner,
                -tile_rows(product_p, source_row, tile),
            ],
            axis=1,
        )
        low_row = jnp.where(source >= 0, low_row, 0.0)
        row = jnp.where(upper, top_row, low_row)
        level_2.append(mm(row, spread))
    product_2 = jnp.stack(level_2)
    first_2 = 3
    count_2 = product_2.shape[0]
    gram_rows = jnp.zeros((count_2, width, tile), jnp.float32)
    gram_rows = lax.dynamic_update_slice_in_dim(gram_rows, gram_piece[first_2:first_2 + count_2], r * band, 1)
    diag_2 = lax.psum(diag_partial(first_2, product_2) + gram_rows, "row")

    products = jnp.concatenate([product_0[None], product_1, product_2], axis=0)
    diag_cols = jnp.concatenate(
        [
            tile_cols(diag_full_0, c, tile)[None],
            lax.dynamic_slice_in_dim(diag_full_1, c * tile, tile, 2),
            diag_2,
        ],
        axis=0,
    )
    return (-products)[None], diag_cols[None]


def solution(mesh):
    return jax.shard_map(
        body,
        mesh=mesh,
        in_specs=(
            P(("leaf", "row"), "col"),
            P("leaf", None, "row", "col"),
            P("leaf", None, "col", None),
            P("leaf", None, None),
            P("leaf", None),
        ),
        out_specs=(P("leaf", None, "row", "col"), P("leaf", None, None, "col")),
        check_vma=False,
    )
```

time: 649 us -> 461 us (0.71)
  waiting for transfers between devices: 454 us -> 251 us
  other arithmetic: 32.6 us -> 53.4 us
  local copies, waits for them, and re-layouts: 114 us -> 100 us
  between operations: 15.8 us -> 26.5 us
    all_gather x7 -> x4, waiting for transfers between devices: 238 us -> 81.8 us  [the longest x2 43.1 us: reduce_and_gather(): everything = lax.all_gather(both, ('row', 'col'), axis=0)]
    reduce_scatter x6 -> x2, waiting for transfers between devices: 178 us -> 54.5 us  [reduce_and_gather(): lax.psum_scatter(diag_partial(first, products), 'row', scatter_dimension=...]
    psum x0 -> x1, waiting for transfers between devices: none -> 55.5 us  [body(): diag_2 = lax.psum(diag_partial(first_2, product_2) + gram_rows, 'row')]
    psum x1, waiting for transfers between devices: 12.6 us -> 58.4 us  [body(): factor_rows = lax.psum(partial_factor, 'col')]
    reshape x11 -> x6, local copies, waits for them, and re-layouts: 43.7 us -> 16.3 us  [the longest x1 5.81 us: body(): gathered.reshape(leaf_count * row_count, col_count, local_rows, local_cols)]
    select_n x1 -> x19, other arithmetic: 0.01 us -> 27.3 us  [the longest x4 13.2 us: body(): product_p = jnp.take(product_full_1, parent, axis=0)]
    reduce_scatter x1, waiting for transfers between devices: 23.1 us -> 0.02 us  [body(): lax.psum_scatter(partial_gram, 'col', scatter_dimension=2, tiled=True)]
    unnamed x30 -> x92, local copies, waits for them, and re-layouts: 14.8 us -> 35.4 us
  transfers between devices with their start and end apart: 15 -> 9, of which waited for: 15 -> 8; matrix products, arithmetic and copies ran while one was open for 12% -> 15% of each run, Pallas kernels for 0% -> 0%
where the time goes in v1:
time: 461 us; the launch traced here: 458 us
  waiting for transfers between devices  251 us (54%)
  local copies, waits for them, and re-layouts  100 us (22%)
  other arithmetic  53.4 us (12%)
  between operations  26.5 us (6%)
  matrix products  26 us (6%)
    psum x1, waiting for transfers between devices, body(): factor_rows = lax.psum(partial_factor, 'col')  58.4 us
    psum x1, waiting for transfers between devices, body(): diag_2 = lax.psum(diag_partial(first_2, product_2) + gram_rows, 'row')  55.5 us
    reduce_scatter x2, waiting for transfers between devices, reduce_and_gather(): lax.psum_scatter(diag_partial(first, products), 'row', scatter_dimension=...  54.5 us
    all_gather x2, waiting for transfers between devices, reduce_and_gather(): everything = lax.all_gather(both, ('row', 'col'), axis=0)  43.1 us
    unnamed x92, local copies, waits for them, and re-layouts  35.4 us
    dot_general x12, matrix products, mm(): jnp.matmul(a, b, precision=HIGHEST, preferred_element_type=jnp.float32)  26 us
    all_gather x1, waiting for transfers between devices, body(): factor_cols = lax.all_gather(factor_tile, 'row', axis=1, tiled=True)  20.2 us
    all_gather x1, waiting for transfers between devices, body(): gathered = lax.all_gather(sigma_top, ('leaf', 'row', 'col'), axis=0)  18.5 us
  transfers between devices with their start and end apart: 9, of which 8 were waited for; matrix products, arithmetic and copies ran while one was open for 15% of the time, Pallas kernels for 0%

profile of v1, /device:TPU:1, one launch (start us, length us, event | category | flops | bytes accessed | tf_op | source)
XLA Modules:
  0.0 457.8 jit_solution(14943117877159287603)
XLA Ops:
  9.5 3.9 fusion.2
  14.3 58.4 %all-reduce.4.cloned.1.call-done = f32[7,128,512]{2,1,0:T(8,128)} async-done(((f32[7,128,512]{2,1,0:T(8,128)}), f32[7,128,512]{2,1,0:T(8,128)}) %all-reduce.4.cloned.1.call-update) | async-done | bytes 1835024 | tf_op jit(solution)/shard_map/psum | solution.py:58
  79.0 18.5 %all-gather.10.cloned.1.call-done = f32[4096,256]{1,0:T(8,128)} async-done(((f32[32,256]{1,0:T(8,128)}), f32[4096,256]{1,0:T(8,128)}) %all-gather.10.cloned.1.call-update) | async-done | bytes 4194320 | tf_op jit(solution)/shard_map/all_gather | solution.py:70
  97.5 5.8 %copy.83 = f32[32,4,32,256]{3,1,2,0:T(4,128)S(1)} copy(f32[32,4,32,256]{3,2,1,0:T(8,128)} %bitcast.194) | data formatting | bytes 8388608 | tf_op jit(solution)/shard_map/reshape | solution.py:71
  103.3 3.0 copy.124
  106.3 20.2 %all-gather.8.cloned.1.call-done = f32[7,1024,128]{2,1,0:T(8,128)} async-done(((f32[7,128,128]{2,1,0:T(8,128)}), f32[7,1024,128]{2,1,0:T(8,128)}) %all-gather.8.cloned.1.call-update) | async-done | bytes 3670032 | tf_op jit(solution)/shard_map/all_gather | solution.py:63
  130.3 27.3 %reduce-scatter.4.cloned.1.call-done = f32[1,64,128]{2,1,0:T(8,128)} async-done(((f32[1,512,128]{2,1,0:T(8,128)}), f32[1,64,128]{2,1,0:T(8,128)}) %reduce-scatter.4.cloned.1.call-update) | async-done | bytes 32784 | tf_op jit(solution)/shard_map/reduce_scatter | solution.py:82
  168.3 3.1 fusion.102
  179.9 27.3 %all-gather.12.cloned.1.call-done = f32[32,192,128]{2,1,0:T(8,128)} async-done(((f32[1,192,128]{2,1,0:T(8,128)}), f32[32,192,128]{2,1,0:T(8,128)}) %all-gather.12.cloned.1.call-update) | async-done | bytes 3145744 | tf_op jit(solution)/shard_map/all_gather | solution.py:85
  208.4 3.2 slice.189
  232.4 27.2 %reduce-scatter.8.cloned.1.call-done = f32[2,64,128]{2,1,0:T(8,128)} async-done(((f32[2,512,128]{2,1,0:T(8,128)}), f32[2,64,128]{2,1,0:T(8,128)}) %reduce-scatter.8.cloned.1.call-update) | async-done | bytes 65552 | tf_op jit(solution)/shard_map/reduce_scatter | solution.py:82
  297.2 15.8 %all-gather.14.cloned.1.call-done = f32[64,192,128]{2,1,0:T(8,128)} async-done(((f32[2,192,128]{2,1,0:T(8,128)}), f32[64,192,128]{2,1,0:T(8,128)}) %all-gather.14.cloned.1.call-update) | async-done | bytes 6291472 | tf_op jit(solution)/shard_map/all_gather | solution.py:85
  313.0 3.2 slice.195
  316.2 4.7 %slice.194 = f32[8,4,2,128,128]{4,3,2,1,0:T(8,128)} slice(f32[8,4,2,192,128]{4,3,2,1,0:T(8,128)} %bitcast.193), slice={[0:8], [0:4], [0:2], [0:128], [0:128]} | slice | bytes 8388608 | tf_op jit(solution)/shard_map/slice | solution.py:87
  320.9 5.3 %copy.118 = f32[8,4,2,128,128]{3,0,4,1,2:T(8,128)} copy(f32[8,4,2,128,128]{4,3,2,1,0:T(8,128)} %slice.194) | data formatting | bytes 8388608
  326.2 4.9 %reshape.293 = f32[2,1024,512]{1,2,0:T(8,128)} reshape(f32[2,8,128,4,128]{2,1,4,3,0:T(8,128)} %bitcast.183) | data formatting | bytes 8388608 | tf_op jit(solution)/shard_map/reshape | solution.py:87
  331.1 4.3 copy.134
  335.4 3.1 reshape.294
  338.5 3.9 select_bitcast_fusion.4
  346.7 7.6 %select_bitcast_fusion = (f32[1024,512]{0,1:T(8,128)}, f32[1,1024,512]{1,2,0:T(8,128)}, f32[1,1024,512]{1,2,0:T(8,128)}, f32[1,1024,512]{1,2,0:T(8,128)}) fusion(f32[2,1024,512]{1,2,0:T(8,128)} %reshape.293, s32[]{:T(128)S(6)} %select_n.346, pred[]{:T(512)S(6)} %and.78, s32[]{:T(128)S(6)} %select_n.326, s32[]{:T(128)S(6)} %select_n.316, s32[]{:T(128)S(6)} %select_n.336), kind=kLoop, calls=%fused_computation.12 | loop fusion | flops 524288 | bytes 16777232 | tf_op jit(solution)/shard_map/jit(_take)/select_n | solution.py:127
  364.4 3.0 copy.119
  371.2 2.9 copy.122
  378.1 3.3 bitcast_dynamic-update-slice_fusion.3
  392.1 55.5 %all-reduce.6.cloned.1.call-done = f32[4,512,128]{2,1,0:T(8,128)} async-done(((f32[4,512,128]{2,1,0:T(8,128)}), f32[4,512,128]{2,1,0:T(8,128)}) %all-reduce.6.cloned.1.call-update) | async-done | bytes 1048592 | tf_op jit(solution)/shard_map/psum | solution.py:154
  (225 shorter events, 116.1 us)
Async XLA Ops:
  8.0 6.0 %copy-start.37 = (s32[1,6,8]{2,0,1:T(1,128)S(1)}, s32[1,6,8]{2,0,1:T(1,128)}, u32[]{:S(2)}) copy-start(s32[1,6,8]{2,0,1:T(1,128)} %param.18) | copy-start | bytes 580
  8.0 64.7 %all-reduce.4.cloned.1.call-start = ((), (), s32[]{:S(2)}) async-start(), calls=%async_computation.3 | async-start | bytes 3670016 | tf_op jit(solution)/shard_map/psum | solution.py:58
  13.4 84.1 %all-gather.10.cloned.1.call-start = ((), (), s32[]{:S(2)}) async-start(), calls=%async_computation.9 | async-start | bytes 4227072 | tf_op jit(solution)/shard_map/all_gather | solution.py:70
  14.0 112.5 %all-gather.8.cloned.1.call-start = ((), (), s32[]{:S(2)}) async-start(), calls=%async_computation.4 | async-start | bytes 4128768 | tf_op jit(solution)/shard_map/all_gather | solution.py:63
  76.6 53.8 %reduce-scatter.6.cloned.1.call-start = ((), (), s32[]{:S(2)}) async-start(), calls=%async_computation.6 | async-start | bytes 1146880 | tf_op jit(solution)/shard_map/reduce_scatter | solution.py:67
  79.0 78.7 %reduce-scatter.4.cloned.1.call-start = ((), (), s32[]{:S(2)}) async-start(), calls=%async_computation.5 | async-start | bytes 294912 | tf_op jit(solution)/shard_map/reduce_scatter | solution.py:82
  103.3 25.6 %copy-start.3 = (f32[7,128,512]{2,1,0:T(8,128)S(1)}, f32[7,128,512]{2,1,0:T(8,128)}, u32[]{:S(2)}) copy-start(f32[7,128,512]{2,1,0:T(8,128)} %copy-done.2) | copy-start | bytes 5505028
  130.3 76.9 %all-gather.12.cloned.1.call-start = ((), (), s32[]{:S(2)}) async-start(), calls=%async_computation.10 | async-start | bytes 3244032 | tf_op jit(solution)/shard_map/all_gather | solution.py:85
  159.0 100.6 %reduce-scatter.8.cloned.1.call-start = ((), (), s32[]{:S(2)}) async-start(), calls=%async_computation.7 | async-start | bytes 589824 | tf_op jit(solution)/shard_map/reduce_scatter | solution.py:82
  230.5 31.0 %copy-start.38 = (s32[1,4]{1,0:T(1,128)S(1)}, s32[1,4]{1,0:T(1,128)}, u32[]{:S(2)}) copy-start(s32[1,4]{1,0:T(1,128)} %param.19) | copy-start | bytes 52
  230.5 44.2 %copy-start.7 = (f32[1,1024,128]{2,1,0:T(8,128)S(1)}, f32[1,1024,128]{2,1,0:T(8,128)}, u32[]{:S(2)}) copy-start(f32[1,1024,128]{2,1,0:T(8,128)} %get-tuple-element.69) | copy-start | bytes 1572868
  232.3 43.9 %copy-start.6 = (f32[1,1024,128]{2,1,0:T(8,128)S(1)}, f32[1,1024,128]{2,1,0:T(8,128)}, u32[]{:S(2)}) copy-start(f32[1,1024,128]{2,1,0:T(8,128)} %get-tuple-element.71) | copy-start | bytes 1572868
  232.3 80.7 %all-gather.14.cloned.1.call-start = ((), (), s32[]{:S(2)}) async-start(), calls=%async_computation.11 | async-start | bytes 6488064 | tf_op jit(solution)/shard_map/all_gather | solution.py:85
  261.2 186.4 %all-reduce.6.cloned.1.call-start = ((), (), s32[]{:S(2)}) async-start(), calls=%async_computation.8 | async-start | bytes 2097152 | tf_op jit(solution)/shard_map/psum | solution.py:154
  281.7 6.0 %copy-start.19 = (f32[1024,128]{0,1:T(8,128)S(1)}, f32[1024,128]{0,1:T(8,128)}, u32[]{:S(2)}) copy-start(f32[1024,128]{0,1:T(8,128)} %get-tuple-element.76) | copy-start | bytes 1572868
  283.8 7.6 %copy-start.18 = (f32[1024,128]{0,1:T(8,128)S(1)}, f32[1024,128]{0,1:T(8,128)}, u32[]{:S(2)}) copy-start(f32[1024,128]{0,1:T(8,128)} %get-tuple-element.77) | copy-start | bytes 1572868
  288.8 6.0 %copy-start.17 = (f32[1024,128]{0,1:T(8,128)S(1)}, f32[1024,128]{0,1:T(8,128)}, u32[]{:S(2)}) copy-start(f32[1024,128]{0,1:T(8,128)} %get-tuple-element.78) | copy-start | bytes 1572868
  291.6 4.9 %copy-start.22 = (f32[1024,128]{1,0:T(8,128)S(1)}, f32[1024,128]{1,0:T(8,128)}, u32[]{:S(2)}) copy-start(f32[1024,128]{1,0:T(8,128)} %copy.108) | copy-start | bytes 1572868
  378.1 5.0 %copy-start.9 = (f32[128,1536]{1,0:T(8,128)S(1)}, f32[128,1536]{1,0:T(8,128)}, u32[]{:S(2)}) copy-start(f32[128,1536]{1,0:T(8,128)} %copy.106) | copy-start | bytes 2359300
  378.1 5.0 %copy-start.14 = (f32[12,128,128]{2,1,0:T(8,128)S(1)}, f32[12,128,128]{2,1,0:T(8,128)}, u32[]{:S(2)}) copy-start(f32[12,128,128]{2,1,0:T(8,128)} %select_select_fusion.1) | copy-start | bytes 2359300
  378.1 5.0 %copy-start.23 = (f32[128,512]{1,0:T(8,128)S(1)}, f32[128,512]{1,0:T(8,128)}, u32[]{:S(2)}) copy-start(f32[128,512]{1,0:T(8,128)} %get-tuple-element.87) | copy-start | bytes 786436
  378.1 5.0 %copy-start.27 = (f32[128,512]{1,0:T(8,128)S(1)}, f32[128,512]{1,0:T(8,128)}, u32[]{:S(2)}) copy-start(f32[128,512]{1,0:T(8,128)} %dynamic-slice_negate_fusion.5) | copy-start | bytes 786436
  378.1 5.0 %copy-start.28 = (f32[128,512]{1,0:T(8,128)S(1)}, f32[128,512]{1,0:T(8,128)}, u32[]{:S(2)}) copy-start(f32[128,512]{1,0:T(8,128)} %copy.105) | copy-start | bytes 786436
  390.9 59.3 %copy-start.1 = (f32[1,7,128,512]{3,2,1,0:T(8,128)S(1)}, f32[1,7,128,512]{3,2,1,0:T(8,128)}, u32[]{:S(2)}) copy-start(f32[1,7,128,512]{3,2,1,0:T(8,128)} %param.17) | copy-start | bytes 5505028
  (24 other events, 68.5 us)
Sparse Core Ops, SparseCore 0:
  13.5 59.1 all-reduce.3
  79.8 21.3 reduce-scatter.5
  130.4 27.1 reduce-scatter.3
  160.0 47.1 all-gather.11
  232.5 27.0 reduce-scatter.7
  261.7 51.2 all-gather.13
Sparse Core Ops, SparseCore 1:
  17.0 80.4 all-gather.9
  99.6 26.8 all-gather.7
  389.2 58.4 all-reduce.5

commit v2 on v1

--- a/solution.py
+++ b/solution.py
@@ -27,13 +27,6 @@
     moved = jnp.take(tiles, source, axis=0)
     moved = jnp.where(present[:, None, None], moved, 0.0)
     return moved.reshape(positions * tile, factor_col.shape[1])
-
-
-def pick_transposed(column_block, picks, tile):
-    tiles = column_block.reshape(-1, tile, tile)
-    chosen = jnp.take(tiles, jnp.maximum(picks, 0), axis=0)
-    chosen = jnp.where((picks >= 0)[:, None, None], chosen, 0.0)
-    return jnp.transpose(chosen, (2, 0, 1)).reshape(tile, picks.shape[0] * tile)
 
 
 def body(sigma_top, panels, inverse_diag, slot_lists, parent_links):
@@ -83,64 +76,70 @@
         piece = piece + gram_piece[first:first + count]
         both = jnp.concatenate([products, piece], axis=1)
         everything = lax.all_gather(both, ("row", "col"), axis=0)
-        everything = everything.reshape(row_count, col_count, count, tile + band, tile)
-        product_full = jnp.transpose(everything[:, :, :, :tile], (2, 0, 3, 1, 4)).reshape(
-            count, row_count * tile, col_count * tile
-        )
-        diag_full = jnp.transpose(everything[:, :, :, tile:], (2, 0, 3, 1, 4)).reshape(
-            count, row_count * band, col_count * tile
-        )
-        return product_full, diag_full
+        return everything.reshape(row_count, col_count, count, tile + band, tile)
+
+    bands_per_tile = tile // band
+
+    def product_col_t(gathered, node, m):
+        tiles = lax.dynamic_index_in_dim(gathered[:, :, :, :tile], m, 1, keepdims=False)
+        tiles = lax.dynamic_index_in_dim(tiles, node, 1, keepdims=False)
+        return jnp.transpose(tiles, (2, 0, 1)).reshape(tile, -1)
+
+    def product_row(gathered, node, q):
+        tiles = lax.dynamic_index_in_dim(gathered[:, :, :, :tile], q, 0, keepdims=False)
+        tiles = lax.dynamic_index_in_dim(tiles, node, 1, keepdims=False)
+        return jnp.transpose(tiles, (1, 0, 2)).reshape(tile, -1)
+
+    def diag_row(gathered, node, m):
+        pieces = lax.dynamic_slice_in_dim(gathered[:, :, :, tile:], m * bands_per_tile, bands_per_tile, 0)
+        pieces = lax.dynamic_index_in_dim(pieces, node, 2, keepdims=False)
+        return jnp.transpose(pieces, (0, 2, 1, 3)).reshape(tile, -1)
+
+    def diag_col(gathered, m):
+        pieces = lax.dynamic_index_in_dim(gathered[:, :, :, tile:], m, 1, keepdims=False)
+        return jnp.transpose(pieces, (1, 0, 2, 3)).reshape(pieces.shape[1], -1, tile)
 
     own_row = jnp.minimum(r, own_tiles - 1)
     upper = r < own_tiles
 
     product_0 = mm(tile_rows(sigma, r, tile), factor_cols[0])
-    product_full_0, diag_full_0 = reduce_and_gather(0, product_0[None])
-    product_full_0 = product_full_0[0]
-    diag_full_0 = diag_full_0[0]
+    gathered_0 = reduce_and_gather(0, product_0[None])
 
+    top_row_1 = jnp.concatenate(
+        [-product_col_t(gathered_0, 0, own_row), diag_row(gathered_0, 0, own_row)], axis=1
+    )
     level_1 = []
     for node in (1, 2):
         slots = picks_all[node - 1]
         spread = scatter_factor(factor_cols[node], slots, positions, tile)
-        top_row = jnp.concatenate(
-            [-jnp.transpose(tile_cols(product_full_0, own_row, tile)), tile_rows(diag_full_0, own_row, tile)],
-            axis=1,
-        )
         source = slots[jnp.maximum(r, own_tiles)]
         source_row = jnp.maximum(source, 0)
         low_row = jnp.concatenate(
-            [tile_rows(sigma, source_row, tile), -tile_rows(product_full_0, source_row, tile)], axis=1
+            [tile_rows(sigma, source_row, tile), -product_row(gathered_0, 0, source_row)], axis=1
         )
         low_row = jnp.where(source >= 0, low_row, 0.0)
-        row = jnp.where(upper, top_row, low_row)
+        row = jnp.where(upper, top_row_1, low_row)
         level_1.append(mm(row, spread))
     product_1 = jnp.stack(level_1)
-    product_full_1, diag_full_1 = reduce_and_gather(1, product_1)
+    gathered_1 = reduce_and_gather(1, product_1)
 
     level_2 = []
     for node in range(3, nodes):
         slots = picks_all[node - 1]
         parent = parents[node - 3] - 1
         parent_slots = jnp.take(picks_all, parent, axis=0)
-        product_p = jnp.take(product_full_1, parent, axis=0)
-        diag_p = jnp.take(diag_full_1, parent, axis=0)
         spread = scatter_factor(factor_cols[node], slots, positions, tile)
         top_row = jnp.concatenate(
-            [-jnp.transpose(tile_cols(product_p, own_row, tile)), tile_rows(diag_p, own_row, tile)], axis=1
+            [-product_col_t(gathered_1, parent, own_row), diag_row(gathered_1, parent, own_row)], axis=1
         )
         source = slots[jnp.maximum(r, own_tiles)]
         source_row = jnp.clip(source, 0, own_tiles - 1)
-        corner = pick_transposed(
-            -tile_cols(product_full_0, source_row, tile), parent_slots[own_tiles:], tile
-        )
+        corner_tiles = product_col_t(gathered_0, 0, source_row).reshape(tile, slot_count, tile)
+        corner_picks = parent_slots[own_tiles:]
+        corner = jnp.take(corner_tiles, jnp.maximum(corner_picks, 0), axis=1)
+        corner = jnp.where((corner_picks >= 0)[None, :, None], -corner, 0.0).reshape(tile, -1)
         low_row = jnp.concatenate(
-            [
-                tile_rows(diag_full_0, source_row, tile),
-                corner,
-                -tile_rows(product_p, source_row, tile),
-            ],
+            [diag_row(gathered_0, 0, source_row), corner, -product_row(gathered_1, parent, source_row)],
             axis=1,
         )
         low_row = jnp.where(source >= 0, low_row, 0.0)
@@ -154,14 +153,7 @@
     diag_2 = lax.psum(diag_partial(first_2, product_2) + gram_rows, "row")
 
     products = jnp.concatenate([product_0[None], product_1, product_2], axis=0)
-    diag_cols = jnp.concatenate(
-        [
-            tile_cols(diag_full_0, c, tile)[None],
-            lax.dynamic_slice_in_dim(diag_full_1, c * tile, tile, 2),
-            diag_2,
-        ],
-        axis=0,
-    )
+    diag_cols = jnp.concatenate([diag_col(gathered_0, c), diag_col(gathered_1, c), diag_2], axis=0)
     return (-products)[None], diag_cols[None]
 
 

time: 461 us -> 446 us (0.967)
  other arithmetic: 53.4 us -> 39 us
  waiting for transfers between devices: 251 us -> 237 us
  local copies, waits for them, and re-layouts: 100 us -> 110 us
    neg x4 -> x17, local copies, waits for them, and re-layouts: 3.46 us -> 27.3 us  [the longest x8 14.3 us: body(): -product_row(gathered_1, parent, source_row)]
    unnamed x92 -> x95, local copies, waits for them, and re-layouts: 35.4 us -> 13.6 us
    all_gather x2, waiting for transfers between devices: 43.1 us -> 26 us  [reduce_and_gather(): everything = lax.all_gather(both, ('row', 'col'), axis=0)]
    select_n x9 -> x4, other arithmetic: 18.5 us -> 7.19 us  [body(): jnp.where((corner_picks >= 0)[None, :, None], -corner, 0.0)]
    dynamic_slice x1 -> x5, local copies, waits for them, and re-layouts: 1.21 us -> 9.22 us  [the longest x4 8.24 us: product_col_t(): lax.dynamic_index_in_dim(gathered[:, :, :, :tile], m, 1, keepdims=False)]
    select_n x0 -> x4, local copies, waits for them, and re-layouts: none -> 7.16 us  [body(): jnp.where((corner_picks >= 0)[None, :, None], -corner, 0.0)]
    dynamic_slice x10 -> x1, local copies, waits for them, and re-layouts: 8.46 us -> 2.31 us  [tile_rows(): return lax.dynamic_slice_in_dim(matrix, index * tile, tile, 0)]
    gather x4, local copies, waits for them, and re-layouts: 4.06 us -> 9.37 us  [body(): corner = jnp.take(corner_tiles, jnp.maximum(corner_picks, 0), axis=1)]
  transfers between devices with their start and end apart: 9 -> 9, of which waited for: 8 -> 7; matrix products, arithmetic and copies ran while one was open for 15% -> 22% of each run, Pallas kernels for 0% -> 0%
where the time goes in v2:
time: 446 us; the launch traced here: 443 us
  waiting for transfers between devices  237 us (53%)
  local copies, waits for them, and re-layouts  110 us (25%)
  other arithmetic  39 us (9%)
  between operations  29.3 us (7%)
  matrix products  26.3 us (6%)
    psum x1, waiting for transfers between devices, body(): diag_2 = lax.psum(diag_partial(first_2, product_2) + gram_rows, 'row')  58.8 us
    psum x1, waiting for transfers between devices, body(): factor_rows = lax.psum(partial_factor, 'col')  58.4 us
    reduce_scatter x2, waiting for transfers between devices, reduce_and_gather(): lax.psum_scatter(diag_partial(first, products), 'row', scatter_dimension=...  54.4 us
    dot_general x12, matrix products, mm(): jnp.matmul(a, b, precision=HIGHEST, preferred_element_type=jnp.float32)  26.3 us
    all_gather x2, waiting for transfers between devices, reduce_and_gather(): everything = lax.all_gather(both, ('row', 'col'), axis=0)  26 us
    all_gather x1, waiting for transfers between devices, body(): factor_cols = lax.all_gather(factor_tile, 'row', axis=1, tiled=True)  20.2 us
    all_gather x1, waiting for transfers between devices, body(): gathered = lax.all_gather(sigma_top, ('leaf', 'row', 'col'), axis=0)  18.5 us
    neg x8, local copies, waits for them, and re-layouts, body(): -product_row(gathered_1, parent, source_row)  14.3 us
  transfers between devices with their start and end apart: 9, of which 7 were waited for; matrix products, arithmetic and copies ran while one was open for 22% of the time, Pallas kernels for 0%

profile of v2, /device:TPU:1, one launch (start us, length us, event | category | flops | bytes accessed | tf_op | source)
XLA Modules:
  0.0 442.5 jit_solution(9169907735359701775)
XLA Ops:
  9.5 3.9 fusion.2
  14.3 58.4 %all-reduce.4.cloned.1.call-done = f32[7,128,512]{2,1,0:T(8,128)} async-done(((f32[7,128,512]{2,1,0:T(8,128)}), f32[7,128,512]{2,1,0:T(8,128)}) %all-reduce.4.cloned.1.call-update) | async-done | bytes 1835024 | tf_op jit(solution)/shard_map/psum | solution.py:51
  76.6 2.3 fusion
  79.0 18.5 %all-gather.10.cloned.1.call-done = f32[4096,256]{1,0:T(8,128)} async-done(((f32[32,256]{1,0:T(8,128)}), f32[4096,256]{1,0:T(8,128)}) %all-gather.10.cloned.1.call-update) | async-done | bytes 4194320 | tf_op jit(solution)/shard_map/all_gather | solution.py:63
  97.5 5.8 %copy.183 = f32[32,4,32,256]{3,1,2,0:T(4,128)S(1)} copy(f32[32,4,32,256]{3,2,1,0:T(8,128)} %bitcast.299) | data formatting | bytes 8388608 | tf_op jit(solution)/shard_map/reshape | solution.py:64
  103.3 3.0 copy.234
  106.3 20.2 %all-gather.8.cloned.1.call-done = f32[7,1024,128]{2,1,0:T(8,128)} async-done(((f32[7,128,128]{2,1,0:T(8,128)}), f32[7,1024,128]{2,1,0:T(8,128)}) %all-gather.8.cloned.1.call-update) | async-done | bytes 3670032 | tf_op jit(solution)/shard_map/all_gather | solution.py:56
  126.5 2.5 bitcast_dynamic-update-slice_fusion.6
  130.3 27.3 %reduce-scatter.4.cloned.1.call-done = f32[1,64,128]{2,1,0:T(8,128)} async-done(((f32[1,512,128]{2,1,0:T(8,128)}), f32[1,64,128]{2,1,0:T(8,128)}) %reduce-scatter.4.cloned.1.call-update) | async-done | bytes 32784 | tf_op jit(solution)/shard_map/reduce_scatter | solution.py:75
  168.6 3.0 fusion.109
  171.6 2.5 gather_fusion.1
  181.2 26.0 %all-gather.12.cloned.1.call-done = f32[32,192,128]{2,1,0:T(8,128)} async-done(((f32[1,192,128]{2,1,0:T(8,128)}), f32[32,192,128]{2,1,0:T(8,128)}) %all-gather.12.cloned.1.call-update) | async-done | bytes 3145744 | tf_op jit(solution)/shard_map/all_gather | solution.py:78
  217.6 3.2 constant_dynamic-slice_fusion.6
  222.1 3.1 bitcast_dynamic-update-slice_fusion.5
  228.7 27.2 %reduce-scatter.8.cloned.1.call-done = f32[2,64,128]{2,1,0:T(8,128)} async-done(((f32[2,512,128]{2,1,0:T(8,128)}), f32[2,64,128]{2,1,0:T(8,128)}) %reduce-scatter.8.cloned.1.call-update) | async-done | bytes 65552 | tf_op jit(solution)/shard_map/reduce_scatter | solution.py:75
  270.8 2.5 gather_fusion.7
  287.3 2.3 gather_fusion.8
  297.1 2.4 gather_fusion.6
  307.0 2.3 gather_fusion.4
  316.7 2.3 gather_fusion.2
  326.1 3.2 slice.198
  359.4 3.3 bitcast_dynamic-update-slice_fusion.3
  373.4 58.8 %all-reduce.6.cloned.1.call-done = f32[4,512,128]{2,1,0:T(8,128)} async-done(((f32[4,512,128]{2,1,0:T(8,128)}), f32[4,512,128]{2,1,0:T(8,128)}) %all-reduce.6.cloned.1.call-update) | async-done | bytes 1048592 | tf_op jit(solution)/shard_map/psum | solution.py:153
  432.2 2.7 maximum_bitcast_fusion
  (231 shorter events, 126.6 us)
Async XLA Ops:
  8.0 64.7 %all-reduce.4.cloned.1.call-start = ((), (), s32[]{:S(2)}) async-start(), calls=%async_computation.3 | async-start | bytes 3670016 | tf_op jit(solution)/shard_map/psum | solution.py:51
  13.4 84.1 %all-gather.10.cloned.1.call-start = ((), (), s32[]{:S(2)}) async-start(), calls=%async_computation.9 | async-start | bytes 4227072 | tf_op jit(solution)/shard_map/all_gather | solution.py:63
  14.0 112.5 %all-gather.8.cloned.1.call-start = ((), (), s32[]{:S(2)}) async-start(), calls=%async_computation.4 | async-start | bytes 4128768 | tf_op jit(solution)/shard_map/all_gather | solution.py:56
  76.6 53.8 %reduce-scatter.6.cloned.1.call-start = ((), (), s32[]{:S(2)}) async-start(), calls=%async_computation.6 | async-start | bytes 1146880 | tf_op jit(solution)/shard_map/reduce_scatter | solution.py:60
  79.0 78.6 %reduce-scatter.4.cloned.1.call-start = ((), (), s32[]{:S(2)}) async-start(), calls=%async_computation.5 | async-start | bytes 294912 | tf_op jit(solution)/shard_map/reduce_scatter | solution.py:75
  103.3 25.6 %copy-start.3 = (f32[7,128,512]{2,1,0:T(8,128)S(1)}, f32[7,128,512]{2,1,0:T(8,128)}, u32[]{:S(2)}) copy-start(f32[7,128,512]{2,1,0:T(8,128)} %copy-done.2) | copy-start | bytes 5505028
  130.3 76.9 %all-gather.12.cloned.1.call-start = ((), (), s32[]{:S(2)}) async-start(), calls=%async_computation.10 | async-start | bytes 3244032 | tf_op jit(solution)/shard_map/all_gather | solution.py:78
  159.1 96.8 %reduce-scatter.8.cloned.1.call-start = ((), (), s32[]{:S(2)}) async-start(), calls=%async_computation.7 | async-start | bytes 589824 | tf_op jit(solution)/shard_map/reduce_scatter | solution.py:75
  222.1 3.2 copy-start.15
  222.1 3.2 copy-start.16
  222.1 3.2 copy-start.20
  222.1 3.2 copy-start.36
  226.8 30.7 %copy-start.41 = (s32[1,4]{1,0:T(1,128)S(1)}, s32[1,4]{1,0:T(1,128)}, u32[]{:S(2)}) copy-start(s32[1,4]{1,0:T(1,128)} %param.15) | copy-start | bytes 52
  228.6 44.7 %copy-start.9 = (f32[1,1024,128]{2,1,0:T(8,128)S(1)}, f32[1,1024,128]{2,1,0:T(8,128)}, u32[]{:S(2)}) copy-start(f32[1,1024,128]{2,1,0:T(8,128)} %get-tuple-element.49) | copy-start | bytes 1572868
  228.6 95.7 %all-gather.14.cloned.1.call-start = ((), (), s32[]{:S(2)}) async-start(), calls=%async_computation.11 | async-start | bytes 6488064 | tf_op jit(solution)/shard_map/all_gather | solution.py:78
  257.5 174.8 %all-reduce.6.cloned.1.call-start = ((), (), s32[]{:S(2)}) async-start(), calls=%async_computation.8 | async-start | bytes 2097152 | tf_op jit(solution)/shard_map/psum | solution.py:153
  326.1 3.2 copy-start.8
  329.4 4.0 copy-start.5
  359.4 3.4 copy-start.14
  359.4 3.4 copy-start.19
  359.4 3.4 copy-start.28
  359.4 3.4 copy-start.30
  359.4 3.4 copy-start.33
  359.4 3.4 copy-start.37
  (27 other events, 50.4 us)
Sparse Core Ops, SparseCore 0:
  13.5 59.1 all-reduce.3
  79.8 21.3 reduce-scatter.5
  130.4 27.1 reduce-scatter.3
  160.0 47.1 all-gather.11
  228.8 27.0 reduce-scatter.7
  258.0 51.3 all-gather.13
Sparse Core Ops, SparseCore 1:
  17.0 80.4 all-gather.9
  99.6 26.8 all-gather.7
  370.6 61.6 all-reduce.5

commit v3 on v2

--- a/solution.py
+++ b/solution.py
@@ -1,6 +1,10 @@
+import functools
+
 import jax
 import jax.numpy as jnp
 from jax import lax
+from jax.experimental import pallas as pl
+from jax.experimental.pallas import tpu as pltpu
 from jax.sharding import PartitionSpec as P
 
 TILE = 128
@@ -27,6 +31,82 @@
     moved = jnp.take(tiles, source, axis=0)
     moved = jnp.where(present[:, None, None], moved, 0.0)
     return moved.reshape(positions * tile, factor_col.shape[1])
+
+
+def dot_hi(a, b):
+    return jnp.dot(a, b, precision=HIGHEST, preferred_element_type=jnp.float32)
+
+
+def dot_t_hi(a, b):
+    return lax.dot_general(
+        a, b, (((0,), (0,)), ((), ())), precision=HIGHEST, preferred_element_type=jnp.float32
+    )
+
+
+def level_kernel(info_ref, par_ref, low_ref, fac_ref, out_ref, *, level, tile, band, own_tiles, slot_count):
+    count = out_ref.shape[0]
+    split = tile // band
+    r = info_ref[0]
+    own = jnp.minimum(r, own_tiles - 1)
+
+    def p_tile(ref, node, q, m):
+        return ref[q, m, node, 0:tile, :]
+
+    def d_tile(ref, node, a, m):
+        return jnp.concatenate([ref[a * split + h, m, node, tile:tile + band, :] for h in range(split)], axis=0)
+
+    for i in range(count):
+        base = 1 + i * slot_count
+        parent = info_ref[1 + count * slot_count + i]
+        factor = [fac_ref[i, k * tile:(k + 1) * tile, :] for k in range(slot_count)]
+        picks = [jnp.clip(info_ref[base + k], 0, slot_count - 1) for k in range(slot_count)]
+        source = info_ref[base + jnp.maximum(r, own_tiles)]
+
+        @pl.when(r < own_tiles)
+        def _():
+            acc = dot_hi(d_tile(par_ref, parent, own, 0), factor[0])
+            for k in range(1, own_tiles):
+                acc += dot_hi(d_tile(par_ref, parent, own, k), factor[k])
+            for k in range(own_tiles, slot_count):
+                acc -= dot_t_hi(p_tile(par_ref, parent, picks[k], own), factor[k])
+            out_ref[i] = acc
+
+        @pl.when(jnp.logical_and(r >= own_tiles, source >= 0))
+        def _():
+            if level == 1:
+                s = jnp.clip(source, 0, slot_count - 1)
+                start = pl.multiple_of(s * tile, tile)
+                acc = -dot_hi(p_tile(par_ref, parent, s, 0), factor[0])
+                for k in range(1, own_tiles):
+                    acc -= dot_hi(p_tile(par_ref, parent, s, k), factor[k])
+                for k in range(own_tiles, slot_count):
+                    acc += dot_hi(low_ref[picks[k], pl.ds(start, tile), :], factor[k])
+            else:
+                s = jnp.clip(source, 0, own_tiles - 1)
+                acc = -dot_hi(p_tile(par_ref, parent, s, 0), factor[0])
+                for k in range(1, own_tiles):
+                    acc -= dot_hi(p_tile(par_ref, parent, s, k), factor[k])
+                for k in range(own_tiles, slot_count):
+                    q = jnp.minimum(picks[k], own_tiles - 1)
+                    acc += dot_hi(d_tile(low_ref, 0, s, q), factor[k])
+            out_ref[i] = acc
+
+        @pl.when(jnp.logical_and(r >= own_tiles, source < 0))
+        def _():
+            out_ref[i] = jnp.zeros((tile, tile), jnp.float32)
+
+
+def level_products(info, parent_data, low_data, factors, level, tile, band, own_tiles, slot_count):
+    kernel = functools.partial(
+        level_kernel, level=level, tile=tile, band=band, own_tiles=own_tiles, slot_count=slot_count
+    )
+    vmem = pl.BlockSpec(memory_space=pltpu.VMEM)
+    return pl.pallas_call(
+        kernel,
+        out_shape=jax.ShapeDtypeStruct((factors.shape[0], tile, tile), jnp.float32),
+        in_specs=[pl.BlockSpec(memory_space=pltpu.SMEM), vmem, vmem, vmem],
+        out_specs=vmem,
+    )(info, parent_data, low_data, factors)
 
 
 def body(sigma_top, panels, inverse_diag, slot_lists, parent_links):
@@ -105,47 +185,19 @@
     product_0 = mm(tile_rows(sigma, r, tile), factor_cols[0])
     gathered_0 = reduce_and_gather(0, product_0[None])
 
-    top_row_1 = jnp.concatenate(
-        [-product_col_t(gathered_0, 0, own_row), diag_row(gathered_0, 0, own_row)], axis=1
-    )
-    level_1 = []
-    for node in (1, 2):
-        slots = picks_all[node - 1]
-        spread = scatter_factor(factor_cols[node], slots, positions, tile)
-        source = slots[jnp.maximum(r, own_tiles)]
-        source_row = jnp.maximum(source, 0)
-        low_row = jnp.concatenate(
-            [tile_rows(sigma, source_row, tile), -product_row(gathered_0, 0, source_row)], axis=1
-        )
-        low_row = jnp.where(source >= 0, low_row, 0.0)
-        row = jnp.where(upper, top_row_1, low_row)
-        level_1.append(mm(row, spread))
-    product_1 = jnp.stack(level_1)
+    sigma_tiles = jnp.transpose(sigma.reshape(sigma.shape[0], slot_count, tile), (1, 0, 2))
+    info_1 = jnp.concatenate([r.astype(jnp.int32)[None], picks_all[0:2].reshape(-1), jnp.zeros((2,), jnp.int32)])
+    product_1 = level_products(
+        info_1, gathered_0, sigma_tiles, factor_cols[1:3], 1, tile, band, own_tiles, slot_count
+    )
     gathered_1 = reduce_and_gather(1, product_1)
 
-    level_2 = []
-    for node in range(3, nodes):
-        slots = picks_all[node - 1]
-        parent = parents[node - 3] - 1
-        parent_slots = jnp.take(picks_all, parent, axis=0)
-        spread = scatter_factor(factor_cols[node], slots, positions, tile)
-        top_row = jnp.concatenate(
-            [-product_col_t(gathered_1, parent, own_row), diag_row(gathered_1, parent, own_row)], axis=1
-        )
-        source = slots[jnp.maximum(r, own_tiles)]
-        source_row = jnp.clip(source, 0, own_tiles - 1)
-        corner_tiles = product_col_t(gathered_0, 0, source_row).reshape(tile, slot_count, tile)
-        corner_picks = parent_slots[own_tiles:]
-        corner = jnp.take(corner_tiles, jnp.maximum(corner_picks, 0), axis=1)
-        corner = jnp.where((corner_picks >= 0)[None, :, None], -corner, 0.0).reshape(tile, -1)
-        low_row = jnp.concatenate(
-            [diag_row(gathered_0, 0, source_row), corner, -product_row(gathered_1, parent, source_row)],
-            axis=1,
-        )
-        low_row = jnp.where(source >= 0, low_row, 0.0)
-        row = jnp.where(upper, top_row, low_row)
-        level_2.append(mm(row, spread))
-    product_2 = jnp.stack(level_2)
+    info_2 = jnp.concatenate(
+        [r.astype(jnp.int32)[None], picks_all[2:nodes - 1].reshape(-1), (parents - 1).astype(jnp.int32)]
+    )
+    product_2 = level_products(
+        info_2, gathered_1, gathered_0, factor_cols[3:nodes], 2, tile, band, own_tiles, slot_count
+    )
     first_2 = 3
     count_2 = product_2.shape[0]
     gram_rows = jnp.zeros((count_2, width, tile), jnp.float32)

time: 446 us -> 381 us (0.85)
  local copies, waits for them, and re-layouts: 110 us -> 35.3 us
  waiting for transfers between devices: 237 us -> 287 us
  other arithmetic: 39 us -> 9.85 us
  between operations: 29.3 us -> 15.9 us
  Pallas kernels: 0 us -> 13.3 us
  matrix products: 26.3 us -> 16.2 us
    all_gather x2, waiting for transfers between devices: 26 us -> 83.5 us  [reduce_and_gather(): everything = lax.all_gather(both, ('row', 'col'), axis=0)]
    neg x17 -> x0, local copies, waits for them, and re-layouts: 27.3 us -> none  [the longest x8 14.3 us: body(): -product_row(gathered_1, parent, source_row)]
    gather x11 -> x0, local copies, waits for them, and re-layouts: 20.6 us -> none  [the longest x6 11 us: scatter_factor(): moved = jnp.take(tiles, source, axis=0)]
    select_n x14 -> x0, other arithmetic: 14.2 us -> none  [the longest x4 7.19 us: body(): jnp.where((corner_picks >= 0)[None, :, None], -corner, 0.0)]
    pallas_call x0 -> x2, Pallas kernels: none -> 13.3 us  [level_products(): pl.pallas_call(kernel, out_shape=jax.ShapeDtypeStruct((factors.shape[0],...]
    dynamic_slice x5 -> x0, local copies, waits for them, and re-layouts: 10.5 us -> none  [the longest x4 8.24 us: product_col_t(): lax.dynamic_index_in_dim(gathered[:, :, :, :tile], m, 1, keepdims=False)]
    another operation x0 -> x3, local copies, waits for them, and re-layouts: none -> 10.4 us  [the longest x2 10.4 us: body(): sigma.reshape(sigma.shape[0], slot_count, tile)]
    dot_general x12 -> x6, matrix products: 26.3 us -> 16.2 us  [mm(): jnp.matmul(a, b, precision=HIGHEST, preferred_element_type=jnp.float32)]
  transfers between devices with their start and end apart: 9 -> 9, of which waited for: 7 -> 8; matrix products, arithmetic and copies ran while one was open for 22% -> 10% of each run, Pallas kernels for 0% -> 0%
where the time goes in v3:
time: 381 us; the launch traced here: 378 us
  waiting for transfers between devices  287 us (75%)
  local copies, waits for them, and re-layouts  35.3 us (9%)
  matrix products  16.2 us (4%)
  between operations  15.9 us (4%)
  Pallas kernels  13.3 us (3%)
  other arithmetic  9.85 us (3%)
    all_gather x2, waiting for transfers between devices, reduce_and_gather(): everything = lax.all_gather(both, ('row', 'col'), axis=0)  83.5 us
    psum x1, waiting for transfers between devices, body(): factor_rows = lax.psum(partial_factor, 'col')  58.3 us
    reduce_scatter x2, waiting for transfers between devices, reduce_and_gather(): lax.psum_scatter(diag_partial(first, products), 'row', scatter_dimension=...  54.4 us
    psum x1, waiting for transfers between devices, body(): diag_2 = lax.psum(diag_partial(first_2, product_2) + gram_rows, 'row')  53.8 us
    all_gather x1, waiting for transfers between devices, body(): gathered = lax.all_gather(sigma_top, ('leaf', 'row', 'col'), axis=0)  18.6 us
    all_gather x1, waiting for transfers between devices, body(): factor_cols = lax.all_gather(factor_tile, 'row', axis=1, tiled=True)  18.2 us
    dot_general x6, matrix products, mm(): jnp.matmul(a, b, precision=HIGHEST, preferred_element_type=jnp.float32)  16.2 us
    pallas_call x2, Pallas kernels, level_products(): pl.pallas_call(kernel, out_shape=jax.ShapeDtypeStruct((factors.shape[0],...  13.3 us
  transfers between devices with their start and end apart: 9, of which 8 were waited for; matrix products, arithmetic and copies ran while one was open for 10% of the time, Pallas kernels for 0%

profile of v3, /device:TPU:1, one launch (start us, length us, event | category | flops | bytes accessed | tf_op | source)
XLA Modules:
  0.0 378.3 jit_solution(619960571446674216)
XLA Ops:
  9.5 3.9 %fusion.2 = f32[7,128,512]{2,1,0:T(8,128)} fusion(f32[1,7,128,512]{3,2,1,0:T(8,128)S(1)} %copy-done, f32[1,7,128,128]{3,2,1,0:T(8,128)} %param.6), kind=kOutput, calls=%fused_computation.4 | convolution fusion | flops 704643072 | bytes 4128768 | tf_op jit(solution)/shard_map/dot_general | solution.py:15
  14.4 58.3 %all-reduce.4.cloned.1.call-done = f32[7,128,512]{2,1,0:T(8,128)} async-done(((f32[7,128,512]{2,1,0:T(8,128)}), f32[7,128,512]{2,1,0:T(8,128)}) %all-reduce.4.cloned.1.call-update) | async-done | bytes 1835024 | tf_op jit(solution)/shard_map/psum | solution.py:131
  76.6 2.3 fusion
  78.9 18.6 %all-gather.10.cloned.1.call-done = f32[4096,256]{1,0:T(8,128)} async-done(((f32[32,256]{1,0:T(8,128)}), f32[4096,256]{1,0:T(8,128)}) %all-gather.10.cloned.1.call-update) | async-done | bytes 4194320 | tf_op jit(solution)/shard_map/all_gather | solution.py:143
  97.5 5.8 %copy.29 = f32[32,4,32,256]{3,1,2,0:T(4,128)S(1)} copy(f32[32,4,32,256]{3,2,1,0:T(8,128)} %bitcast.63) | data formatting | bytes 8388608 | tf_op jit(solution)/shard_map/reshape | solution.py:144
  103.3 1.9 copy-done.1
  105.3 3.0 copy.24
  108.2 18.2 %all-gather.8.cloned.1.call-done = f32[7,1024,128]{2,1,0:T(8,128)} async-done(((f32[7,128,128]{2,1,0:T(8,128)}), f32[7,1024,128]{2,1,0:T(8,128)}) %all-gather.8.cloned.1.call-update) | async-done | bytes 3670032 | tf_op jit(solution)/shard_map/all_gather | solution.py:136
  126.5 1.8 fusion.4
  128.3 2.2 convolution_bitcast_fusion
  130.7 27.3 %reduce-scatter.4.cloned.1.call-done = f32[1,64,128]{2,1,0:T(8,128)} async-done(((f32[1,512,128]{2,1,0:T(8,128)}), f32[1,64,128]{2,1,0:T(8,128)}) %reduce-scatter.4.cloned.1.call-update) | async-done | bytes 32784 | tf_op jit(solution)/shard_map/reduce_scatter | solution.py:155
  160.2 2.3 slice.64.fac_ref
  162.5 5.5 %reshape_reshape.3 = f32[1024,8,128]{2,1,0:T(8,128)} reshape(f32[32,32,4,256]{3,2,1,0:T(4,128)} %bitcast.55) | data formatting | bytes 8388608 | tf_op jit(solution)/shard_map/reshape;reshape | solution.py:188
  168.0 4.9 %copy.28 = f32[1024,8,128]{2,0,1:T(8,128)} copy(f32[1024,8,128]{2,1,0:T(8,128)} %reshape_reshape.3) | data formatting | bytes 8388608 | tf_op jit(solution)/shard_map/reshape;reshape | solution.py:188
  173.0 35.1 %all-gather.12.cloned.1.call-done = f32[32,192,128]{2,1,0:T(8,128)} async-done(((f32[1,192,128]{2,1,0:T(8,128)}), f32[32,192,128]{2,1,0:T(8,128)}) %all-gather.12.cloned.1.call-update) | async-done | bytes 3145744 | tf_op jit(solution)/shard_map/all_gather | solution.py:158
  208.0 5.6 %shard_map.68 = f32[2,128,128]{2,1,0:T(8,128)} custom-call(s32[19]{0:T(128)} %pad_add_fusion.info_ref, f32[8,4,1,192,128]{4,3,2,1,0:T(8,128)} %bitcast.56, f32[8,1024,128]{2,1,0:T(8,128)} %bitcast.59, f32[2,1024,128]{2,1,0:T(8,128)} %slice.64.fac_ref), custom_call_target="tpu_custom_call" | custom-call | tf_op jit(solution)/shard_map/pallas_call | solution.py:104
  213.6 2.9 fusion.12
  216.6 27.2 %reduce-scatter.8.cloned.1.call-done = f32[2,64,128]{2,1,0:T(8,128)} async-done(((f32[2,512,128]{2,1,0:T(8,128)}), f32[2,64,128]{2,1,0:T(8,128)}) %reduce-scatter.8.cloned.1.call-update) | async-done | bytes 65552 | tf_op jit(solution)/shard_map/reduce_scatter | solution.py:155
  246.2 3.1 slice.66.fac_ref
  249.2 48.4 %all-gather.14.cloned.1.call-done = f32[64,192,128]{2,1,0:T(8,128)} async-done(((f32[2,192,128]{2,1,0:T(8,128)}), f32[64,192,128]{2,1,0:T(8,128)}) %all-gather.14.cloned.1.call-update) | async-done | bytes 6291472 | tf_op jit(solution)/shard_map/all_gather | solution.py:158
  297.6 7.7 %shard_map.69 = f32[4,128,128]{2,1,0:T(8,128)} custom-call(s32[37]{0:T(128)} %pad_add_fusion.1.info_ref, f32[8,4,2,192,128]{4,3,2,1,0:T(8,128)} %bitcast.60, f32[8,4,1,192,128]{4,3,2,1,0:T(8,128)} %bitcast.57, f32[4,1024,128]{2,1,0:T(8,128)} %slice.66.fac_ref), custom_call_target="tpu_custom_call" | custom-call | tf_op jit(solution)/shard_map/pallas_call | solution.py:104
  305.3 3.1 fusion.13
  314.4 53.8 %all-reduce.6.cloned.1.call-done = f32[4,512,128]{2,1,0:T(8,128)} async-done(((f32[4,512,128]{2,1,0:T(8,128)}), f32[4,512,128]{2,1,0:T(8,128)}) %all-reduce.6.cloned.1.call-update) | async-done | bytes 1048592 | tf_op jit(solution)/shard_map/psum | solution.py:205
  368.2 2.6 maximum_bitcast_fusion
  (59 shorter events, 17.1 us)
Async XLA Ops:
  8.0 1.5 copy-start
  8.0 64.7 %all-reduce.4.cloned.1.call-start = ((), (), s32[]{:S(2)}) async-start(), calls=%async_computation.3 | async-start | bytes 3670016 | tf_op jit(solution)/shard_map/psum | solution.py:131
  13.4 0.7 copy-start.7
  13.4 84.1 %all-gather.10.cloned.1.call-start = ((), (), s32[]{:S(2)}) async-start(), calls=%async_computation.9 | async-start | bytes 4227072 | tf_op jit(solution)/shard_map/all_gather | solution.py:143
  14.0 112.5 %all-gather.8.cloned.1.call-start = ((), (), s32[]{:S(2)}) async-start(), calls=%async_computation.4 | async-start | bytes 4128768 | tf_op jit(solution)/shard_map/all_gather | solution.py:136
  74.5 1.2 copy-start.2
  76.6 54.1 %reduce-scatter.6.cloned.1.call-start = ((), (), s32[]{:S(2)}) async-start(), calls=%async_computation.6 | async-start | bytes 1146880 | tf_op jit(solution)/shard_map/reduce_scatter | solution.py:140
  78.9 79.0 %reduce-scatter.4.cloned.1.call-start = ((), (), s32[]{:S(2)}) async-start(), calls=%async_computation.5 | async-start | bytes 294912 | tf_op jit(solution)/shard_map/reduce_scatter | solution.py:155
  103.3 2.0 copy-start.1
  130.6 77.4 %all-gather.12.cloned.1.call-start = ((), (), s32[]{:S(2)}) async-start(), calls=%async_computation.10 | async-start | bytes 3244032 | tf_op jit(solution)/shard_map/all_gather | solution.py:158
  159.4 84.3 %reduce-scatter.8.cloned.1.call-start = ((), (), s32[]{:S(2)}) async-start(), calls=%async_computation.7 | async-start | bytes 589824 | tf_op jit(solution)/shard_map/reduce_scatter | solution.py:155
  213.6 31.0 %copy-start.5 = (f32[2,128,128]{2,1,0:T(8,128)S(1)}, f32[2,128,128]{2,1,0:T(8,128)}, u32[]{:S(2)}) copy-start(f32[2,128,128]{2,1,0:T(8,128)} %shard_map.68) | copy-start | bytes 393220
  213.6 31.9 %copy-start.8 = (s32[1,4]{1,0:T(1,128)S(1)}, s32[1,4]{1,0:T(1,128)}, u32[]{:S(2)}) copy-start(s32[1,4]{1,0:T(1,128)} %param.9) | copy-start | bytes 52
  216.5 81.1 %all-gather.14.cloned.1.call-start = ((), (), s32[]{:S(2)}) async-start(), calls=%async_computation.11 | async-start | bytes 6488064 | tf_op jit(solution)/shard_map/all_gather | solution.py:158
  245.3 122.8 %all-reduce.6.cloned.1.call-start = ((), (), s32[]{:S(2)}) async-start(), calls=%async_computation.8 | async-start | bytes 2097152 | tf_op jit(solution)/shard_map/psum | solution.py:205
  305.3 3.1 copy-start.6
  308.5 1.0 copy-start.3
  312.6 1.0 copy-start.4
Sparse Core Ops, SparseCore 0:
  13.5 59.1 all-reduce.3
  79.8 21.3 reduce-scatter.5
  130.7 27.1 reduce-scatter.3
  160.9 47.1 all-gather.11
  216.6 27.0 reduce-scatter.7
  246.4 51.1 all-gather.13
Sparse Core Ops, SparseCore 1:
  17.0 80.4 all-gather.9
  99.6 26.8 all-gather.7
  309.6 58.5 all-reduce.5

commit v4 on v3

--- a/solution.py
+++ b/solution.py
@@ -109,6 +109,96 @@
     )(info, parent_data, low_data, factors)
 
 
+def reduce_kernel(x_ref, out_ref, recv_ref, send_sem, recv_sem, back_send, back_recv, *, axis, count, band, gather):
+    me = lax.axis_index(axis)
+    ids = {name: lax.axis_index(name) for name in ("leaf", "row", "col")}
+
+    def device(peer):
+        where = dict(ids)
+        where[axis] = peer
+        return (where["leaf"], where["row"], where["col"])
+
+    mesh_ids = pl.DeviceIdType.MESH
+    barrier = pltpu.get_barrier_semaphore()
+    for d in range(1, count):
+        pl.semaphore_signal(barrier, inc=1, device_id=device(lax.rem(me + d, count)), device_id_type=mesh_ids)
+    pl.semaphore_wait(barrier, count - 1)
+
+    sends = []
+    for d in range(1, count):
+        peer = lax.rem(me + d, count)
+        copy = pltpu.make_async_remote_copy(
+            src_ref=x_ref.at[:, pl.ds(pl.multiple_of(peer * band, band), band), :],
+            dst_ref=recv_ref.at[d - 1],
+            send_sem=send_sem.at[d - 1],
+            recv_sem=recv_sem.at[d - 1],
+            device_id=device(peer),
+            device_id_type=mesh_ids,
+        )
+        copy.start()
+        sends.append(copy)
+    for copy in sends:
+        copy.wait_recv()
+    for copy in sends:
+        copy.wait_send()
+    own = pl.ds(pl.multiple_of(me * band, band), band)
+    total = x_ref[:, own, :]
+    for d in range(1, count):
+        total = total + recv_ref[d - 1]
+    if not gather:
+        out_ref[...] = total
+        return
+    out_ref[:, own, :] = total
+    backs = []
+    for d in range(1, count):
+        peer = lax.rem(me + d, count)
+        copy = pltpu.make_async_remote_copy(
+            src_ref=out_ref.at[:, own, :],
+            dst_ref=out_ref.at[:, own, :],
+            send_sem=back_send.at[d - 1],
+            recv_sem=back_recv.at[d - 1],
+            device_id=device(peer),
+            device_id_type=mesh_ids,
+        )
+        copy.start()
+        backs.append(copy)
+    for d in range(1, count):
+        source = lax.rem(me + count - d, count)
+        part = pl.ds(pl.multiple_of(source * band, band), band)
+        pltpu.make_async_remote_copy(
+            src_ref=out_ref.at[:, part, :],
+            dst_ref=out_ref.at[:, part, :],
+            send_sem=back_send.at[d - 1],
+            recv_sem=back_recv.at[d - 1],
+            device_id=device(source),
+            device_id_type=mesh_ids,
+        ).wait_recv()
+    for copy in backs:
+        copy.wait_send()
+
+
+def axis_reduce(x, axis, count, gather, collective_id):
+    lead, rows, last = x.shape
+    band = rows // count
+    kernel = functools.partial(reduce_kernel, axis=axis, count=count, band=band, gather=gather)
+    out_rows = rows if gather else band
+    vmem = pl.BlockSpec(memory_space=pltpu.VMEM)
+    return pl.pallas_call(
+        kernel,
+        out_shape=jax.ShapeDtypeStruct((lead, out_rows, last), x.dtype),
+        in_specs=[vmem],
+        out_specs=vmem,
+        scratch_shapes=[
+            pltpu.VMEM((count - 1, lead, band, last), x.dtype),
+            pltpu.SemaphoreType.DMA((count - 1,)),
+            pltpu.SemaphoreType.DMA((count - 1,)),
+            pltpu.SemaphoreType.DMA((count - 1,)),
+            pltpu.SemaphoreType.DMA((count - 1,)),
+        ],
+        compiler_params=pltpu.CompilerParams(collective_id=collective_id, has_side_effects=True),
+    )(x)
+
+
 def body(sigma_top, panels, inverse_diag, slot_lists, parent_links):
     tile = TILE
     row_count = lax.axis_size("row")
@@ -152,7 +242,7 @@
 
     def reduce_and_gather(first, products):
         count = products.shape[0]
-        piece = lax.psum_scatter(diag_partial(first, products), "row", scatter_dimension=1, tiled=True)
+        piece = axis_reduce(diag_partial(first, products), "row", row_count, False, first)
         piece = piece + gram_piece[first:first + count]
         both = jnp.concatenate([products, piece], axis=1)
         everything = lax.all_gather(both, ("row", "col"), axis=0)
@@ -202,7 +292,7 @@
     count_2 = product_2.shape[0]
     gram_rows = jnp.zeros((count_2, width, tile), jnp.float32)
     gram_rows = lax.dynamic_update_slice_in_dim(gram_rows, gram_piece[first_2:first_2 + count_2], r * band, 1)
-    diag_2 = lax.psum(diag_partial(first_2, product_2) + gram_rows, "row")
+    diag_2 = axis_reduce(diag_partial(first_2, product_2) + gram_rows, "row", row_count, True, 2)
 
     products = jnp.concatenate([product_0[None], product_1, product_2], axis=0)
     diag_cols = jnp.concatenate([diag_col(gathered_0, c), diag_col(gathered_1, c), diag_2], axis=0)

time: 381 us -> 313 us (0.82)
  waiting for transfers between devices: 287 us -> 170 us
  Pallas kernels: 13.3 us -> 64.2 us
    reduce_scatter x2 -> x0, waiting for transfers between devices: 54.4 us -> none  [reduce_and_gather(): lax.psum_scatter(diag_partial(first, products), 'row', scatter_dimension=...]
    psum x1 -> x0, waiting for transfers between devices: 53.8 us -> none  [body(): diag_2 = lax.psum(diag_partial(first_2, product_2) + gram_rows, 'row')]
    pallas_call x0 -> x3, Pallas kernels: none -> 50.9 us  [axis_reduce(): pl.pallas_call(kernel, out_shape=jax.ShapeDtypeStruct((lead, out_rows, la...]
    all_gather x2, waiting for transfers between devices: 83.5 us -> 74.6 us  [reduce_and_gather(): everything = lax.all_gather(both, ('row', 'col'), axis=0)]
    unnamed x19 -> x25, local copies, waits for them, and re-layouts: 9.42 us -> 8.6 us
  transfers between devices with their start and end apart: 9 -> 6, of which waited for: 8 -> 5; matrix products, arithmetic and copies ran while one was open for 10% -> 12% of each run, Pallas kernels for 0% -> 3%
where the time goes in v4:
time: 313 us; the launch traced here: 312 us
  waiting for transfers between devices  170 us (54%)
  Pallas kernels  64.2 us (21%)
  local copies, waits for them, and re-layouts  37.1 us (12%)
  matrix products  16.2 us (5%)
  between operations  15.4 us (5%)
  other arithmetic  8.47 us (3%)
    all_gather x2, waiting for transfers between devices, reduce_and_gather(): everything = lax.all_gather(both, ('row', 'col'), axis=0)  74.6 us
    psum x1, waiting for transfers between devices, body(): factor_rows = lax.psum(partial_factor, 'col')  58.3 us
    pallas_call x3, Pallas kernels, axis_reduce(): pl.pallas_call(kernel, out_shape=jax.ShapeDtypeStruct((lead, out_rows, la...  50.9 us
    all_gather x1, waiting for transfers between devices, body(): gathered = lax.all_gather(sigma_top, ('leaf', 'row', 'col'), axis=0)  18.5 us
    all_gather x1, waiting for transfers between devices, body(): factor_cols = lax.all_gather(factor_tile, 'row', axis=1, tiled=True)  18.2 us
    dot_general x6, matrix products, mm(): jnp.matmul(a, b, precision=HIGHEST, preferred_element_type=jnp.float32)  16.2 us
    pallas_call x2, Pallas kernels, level_products(): pl.pallas_call(kernel, out_shape=jax.ShapeDtypeStruct((factors.shape[0],...  13.3 us
    another operation x2, local copies, waits for them, and re-layouts, body(): sigma.reshape(sigma.shape[0], slot_count, tile)  10.5 us
  transfers between devices with their start and end apart: 6, of which 5 were waited for; matrix products, arithmetic and copies ran while one was open for 12% of the time, Pallas kernels for 3%

profile of v4, /device:TPU:1, one launch (start us, length us, event | category | flops | bytes accessed | tf_op | source)
XLA Modules:
  0.0 312.0 jit_solution(1235583436446362819)
XLA Ops:
  9.5 3.9 %fusion.2 = f32[7,128,512]{2,1,0:T(8,128)} fusion(f32[1,7,128,512]{3,2,1,0:T(8,128)S(1)} %copy-done, f32[1,7,128,128]{3,2,1,0:T(8,128)} %param.6), kind=kOutput, calls=%fused_computation.4 | convolution fusion | flops 704643072 | bytes 4128768 | tf_op jit(solution)/shard_map/dot_general | solution.py:15
  14.4 58.3 %all-reduce.3.cloned.1.call-done = f32[7,128,512]{2,1,0:T(8,128)} async-done(((f32[7,128,512]{2,1,0:T(8,128)}), f32[7,128,512]{2,1,0:T(8,128)}) %all-reduce.3.cloned.1.call-update) | async-done | bytes 1835024 | tf_op jit(solution)/shard_map/psum | solution.py:221
  76.6 2.3 fusion
  79.0 18.5 %all-gather.10.cloned.1.call-done = f32[4096,256]{1,0:T(8,128)} async-done(((f32[32,256]{1,0:T(8,128)}), f32[4096,256]{1,0:T(8,128)}) %all-gather.10.cloned.1.call-update) | async-done | bytes 4194320 | tf_op jit(solution)/shard_map/all_gather | solution.py:233
  97.5 5.8 %copy.29 = f32[32,4,32,256]{3,1,2,0:T(4,128)S(1)} copy(f32[32,4,32,256]{3,2,1,0:T(8,128)} %bitcast.63) | data formatting | bytes 8388608 | tf_op jit(solution)/shard_map/reshape | solution.py:234
  103.3 1.9 copy-done.1
  105.3 3.0 copy.24
  108.2 18.2 %all-gather.8.cloned.1.call-done = f32[7,1024,128]{2,1,0:T(8,128)} async-done(((f32[7,128,128]{2,1,0:T(8,128)}), f32[7,1024,128]{2,1,0:T(8,128)}) %all-gather.8.cloned.1.call-update) | async-done | bytes 3670032 | tf_op jit(solution)/shard_map/all_gather | solution.py:226
  126.5 1.8 fusion.4
  128.3 2.3 convolution_bitcast_fusion.x_ref
  130.6 8.7 %shard_map.68 = f32[1,64,128]{2,1,0:T(8,128)} custom-call(f32[1,512,128]{2,1,0:T(8,128)} %convolution_bitcast_fusion.x_ref), custom_call_target="tpu_custom_call" | custom-call | tf_op jit(solution)/shard_map/pallas_call | solution.py:186
  141.6 2.3 slice.64.fac_ref
  143.9 5.5 %reshape_reshape.3 = f32[1024,8,128]{2,1,0:T(8,128)} reshape(f32[32,32,4,256]{3,2,1,0:T(4,128)} %bitcast.55) | data formatting | bytes 8388608 | tf_op jit(solution)/shard_map/reshape;reshape | solution.py:278
  149.4 5.0 %copy.28 = f32[1024,8,128]{2,0,1:T(8,128)} copy(f32[1024,8,128]{2,1,0:T(8,128)} %reshape_reshape.3) | data formatting | bytes 8388608 | tf_op jit(solution)/shard_map/reshape;reshape | solution.py:278
  154.4 31.6 %all-gather.12.cloned.1.call-done = f32[32,192,128]{2,1,0:T(8,128)} async-done(((f32[1,192,128]{2,1,0:T(8,128)}), f32[32,192,128]{2,1,0:T(8,128)}) %all-gather.12.cloned.1.call-update) | async-done | bytes 3145744 | tf_op jit(solution)/shard_map/all_gather | solution.py:248
  186.0 5.6 %shard_map.69 = f32[2,128,128]{2,1,0:T(8,128)} custom-call(s32[19]{0:T(128)} %pad_add_fusion.info_ref, f32[8,4,1,192,128]{4,3,2,1,0:T(8,128)} %bitcast.56, f32[8,1024,128]{2,1,0:T(8,128)} %bitcast.59, f32[2,1024,128]{2,1,0:T(8,128)} %slice.64.fac_ref), custom_call_target="tpu_custom_call" | custom-call | tf_op jit(solution)/shard_map/pallas_call | solution.py:104
  191.6 2.9 fusion.12.x_ref
  194.5 12.0 %shard_map.70 = f32[2,64,128]{2,1,0:T(8,128)} custom-call(f32[2,512,128]{2,1,0:T(8,128)} %fusion.12.x_ref), custom_call_target="tpu_custom_call" | custom-call | tf_op jit(solution)/shard_map/pallas_call | solution.py:186
  208.7 3.1 slice.66.fac_ref
  213.2 43.1 %all-gather.14.cloned.1.call-done = f32[64,192,128]{2,1,0:T(8,128)} async-done(((f32[2,192,128]{2,1,0:T(8,128)}), f32[64,192,128]{2,1,0:T(8,128)}) %all-gather.14.cloned.1.call-update) | async-done | bytes 6291472 | tf_op jit(solution)/shard_map/all_gather | solution.py:248
  256.2 3.2 %slice.68 = f32[8,4,2,64,128]{4,3,2,1,0:T(8,128)} slice(f32[8,4,2,192,128]{4,3,2,1,0:T(8,128)} %bitcast.60), slice={[0:8], [0:4], [0:2], [128:192], [0:128]} | slice | bytes 4194304 | tf_op jit(solution)/shard_map/slice | solution.py:269
  259.5 7.7 %shard_map.71 = f32[4,128,128]{2,1,0:T(8,128)} custom-call(s32[37]{0:T(128)} %pad_add_fusion.1.info_ref, f32[8,4,2,192,128]{4,3,2,1,0:T(8,128)} %bitcast.61, f32[8,4,1,192,128]{4,3,2,1,0:T(8,128)} %bitcast.58, f32[4,1024,128]{2,1,0:T(8,128)} %slice.66.fac_ref), custom_call_target="tpu_custom_call" | custom-call | tf_op jit(solution)/shard_map/pallas_call | solution.py:104
  267.2 3.1 fusion.13
  271.2 30.2 %shard_map.72 = f32[4,512,128]{2,1,0:T(8,128)} custom-call(f32[4,512,128]{2,1,0:T(8,128)} %copy-done.3), custom_call_target="tpu_custom_call" | custom-call | tf_op jit(solution)/shard_map/pallas_call | solution.py:186
  (59 shorter events, 16.6 us)
Async XLA Ops:
  8.0 1.5 copy-start
  8.0 64.7 %all-reduce.3.cloned.1.call-start = ((), (), s32[]{:S(2)}) async-start(), calls=%async_computation.1 | async-start | bytes 3670016 | tf_op jit(solution)/shard_map/psum | solution.py:221
  13.4 0.7 copy-start.10
  13.4 84.1 %all-gather.10.cloned.1.call-start = ((), (), s32[]{:S(2)}) async-start(), calls=%async_computation.4 | async-start | bytes 4227072 | tf_op jit(solution)/shard_map/all_gather | solution.py:233
  14.0 112.5 %all-gather.8.cloned.1.call-start = ((), (), s32[]{:S(2)}) async-start(), calls=%async_computation.2 | async-start | bytes 4128768 | tf_op jit(solution)/shard_map/all_gather | solution.py:226
  74.5 1.2 copy-start.2
  76.6 62.8 %reduce-scatter.2.cloned.1.call-start = ((), (), s32[]{:S(2)}) async-start(), calls=%async_computation.3 | async-start | bytes 1146880 | tf_op jit(solution)/shard_map/reduce_scatter | solution.py:230
  78.9 107.1 %all-gather.12.cloned.1.call-start = ((), (), s32[]{:S(2)}) async-start(), calls=%async_computation.5 | async-start | bytes 3244032 | tf_op jit(solution)/shard_map/all_gather | solution.py:248
  103.3 2.0 copy-start.1
  128.3 21.1 %copy-start.7 = (f32[128,128]{1,0:T(8,128)}, f32[128,128]{1,0:T(8,128)S(1)}, u32[]{:S(2)}) copy-start(f32[128,128]{1,0:T(8,128)S(1)} %fusion.4) | copy-start | bytes 196612
  140.8 115.4 %all-gather.14.cloned.1.call-start = ((), (), s32[]{:S(2)}) async-start(), calls=%async_computation.6 | async-start | bytes 6488064 | tf_op jit(solution)/shard_map/all_gather | solution.py:248
  191.6 14.9 %copy-start.9 = (f32[7,64,128]{2,1,0:T(8,128)S(1)}, f32[7,64,128]{2,1,0:T(8,128)}, u32[]{:S(2)}) copy-start(f32[7,64,128]{2,1,0:T(8,128)} %reduce-scatter.2.cloned.1.call-done) | copy-start | bytes 688132
  191.6 15.7 %copy-start.6 = (f32[2,128,128]{2,1,0:T(8,128)S(1)}, f32[2,128,128]{2,1,0:T(8,128)}, u32[]{:S(2)}) copy-start(f32[2,128,128]{2,1,0:T(8,128)} %shard_map.69) | copy-start | bytes 393220
  191.6 16.6 %copy-start.11 = (s32[1,4]{1,0:T(1,128)S(1)}, s32[1,4]{1,0:T(1,128)}, u32[]{:S(2)}) copy-start(s32[1,4]{1,0:T(1,128)} %param.9) | copy-start | bytes 52
  270.3 1.0 copy-start.3
  271.2 31.5 %copy-start.5 = (f32[4,128,128]{2,1,0:T(8,128)S(1)}, f32[4,128,128]{2,1,0:T(8,128)}, u32[]{:S(2)}) copy-start(f32[4,128,128]{2,1,0:T(8,128)} %shard_map.71) | copy-start | bytes 786436
  301.5 1.3 copy-start.8
  301.5 2.1 copy-start.4
Sparse Core Ops, SparseCore 0:
  13.5 59.1 all-reduce.2
  79.8 21.3 reduce-scatter.1
  140.9 45.0 all-gather.11
  208.1 48.0 all-gather.13
Sparse Core Ops, SparseCore 1:
  17.0 80.4 all-gather.9
  99.6 26.8 all-gather.7

commit v5 on v4

--- a/solution.py
+++ b/solution.py
@@ -218,7 +218,7 @@
     band = width // row_count
 
     partial_factor = mm(panel, inverse)
-    factor_rows = lax.psum(partial_factor, "col")
+    factor_rows = axis_reduce(partial_factor, "col", col_count, True, 3)
     living = jnp.concatenate([jnp.ones((1, slot_count), jnp.bool_), picks_all >= 0], axis=0)
     live_here = jnp.take(living, r, axis=1).astype(jnp.float32)
     factor_rows = factor_rows * live_here[:, None, None]

time: 313 us -> 309 us (0.987)
  waiting for transfers between devices: 170 us -> 116 us
  Pallas kernels: 64.2 us -> 114 us
    psum x1 -> x0, waiting for transfers between devices: 58.3 us -> none  [body(): factor_rows = lax.psum(partial_factor, 'col')]
    pallas_call x3 -> x4, Pallas kernels: 50.9 us -> 101 us  [axis_reduce(): pl.pallas_call(kernel, out_shape=jax.ShapeDtypeStruct((lead, out_rows, la...]
    all_gather x1, waiting for transfers between devices: 18.5 us -> 21.8 us  [body(): gathered = lax.all_gather(sigma_top, ('leaf', 'row', 'col'), axis=0)]
  transfers between devices with their start and end apart: 6 -> 5, of which waited for: 5 -> 4; matrix products, arithmetic and copies ran while one was open for 12% -> 13% of each run, Pallas kernels for 3% -> 19%
where the time goes in v5:
time: 309 us; the launch traced here: 308 us
  waiting for transfers between devices  116 us (38%)
  Pallas kernels  114 us (37%)
  local copies, waits for them, and re-layouts  36.4 us (12%)
  matrix products  16.2 us (5%)
  between operations  15.9 us (5%)
  other arithmetic  8.48 us (3%)
    pallas_call x4, Pallas kernels, axis_reduce(): pl.pallas_call(kernel, out_shape=jax.ShapeDtypeStruct((lead, out_rows, la...  101 us
    all_gather x2, waiting for transfers between devices, reduce_and_gather(): everything = lax.all_gather(both, ('row', 'col'), axis=0)  74.4 us
    all_gather x1, waiting for transfers between devices, body(): gathered = lax.all_gather(sigma_top, ('leaf', 'row', 'col'), axis=0)  21.8 us
    all_gather x1, waiting for transfers between devices, body(): factor_cols = lax.all_gather(factor_tile, 'row', axis=1, tiled=True)  19.4 us
    dot_general x6, matrix products, mm(): jnp.matmul(a, b, precision=HIGHEST, preferred_element_type=jnp.float32)  16.2 us
    pallas_call x2, Pallas kernels, level_products(): pl.pallas_call(kernel, out_shape=jax.ShapeDtypeStruct((factors.shape[0],...  13.3 us
    another operation x2, local copies, waits for them, and re-layouts, body(): sigma.reshape(sigma.shape[0], slot_count, tile)  10.5 us
    unnamed x25, local copies, waits for them, and re-layouts  7.84 us
  transfers between devices with their start and end apart: 5, of which 4 were waited for; matrix products, arithmetic and copies ran while one was open for 13% of the time, Pallas kernels for 19%

profile of v5, /device:TPU:1, one launch (start us, length us, event | category | flops | bytes accessed | tf_op | source)
XLA Modules:
  0.0 307.8 jit_solution(6377526484037687438)
XLA Ops:
  9.5 3.9 %fusion.2.x_ref = f32[7,128,512]{2,1,0:T(8,128)} fusion(f32[1,7,128,512]{3,2,1,0:T(8,128)S(1)} %copy-done, f32[1,7,128,128]{3,2,1,0:T(8,128)} %param.6), kind=kOutput, calls=%fused_computation.4 | convolution fusion | flops 704643072 | bytes 4128768 | tf_op jit(solution)/shard_map/dot_general | solution.py:15
  13.4 49.8 %shard_map.68 = f32[7,128,512]{2,1,0:T(8,128)} custom-call(f32[7,128,512]{2,1,0:T(8,128)} %fusion.2.x_ref), custom_call_target="tpu_custom_call" | custom-call | tf_op jit(solution)/shard_map/pallas_call | solution.py:186
  67.5 2.3 fusion
  69.9 21.8 %all-gather.10.cloned.1.call-done = f32[4096,256]{1,0:T(8,128)} async-done(((f32[32,256]{1,0:T(8,128)}), f32[4096,256]{1,0:T(8,128)}) %all-gather.10.cloned.1.call-update) | async-done | bytes 4194320 | tf_op jit(solution)/shard_map/all_gather | solution.py:233
  91.7 5.8 %copy.29 = f32[32,4,32,256]{3,1,2,0:T(4,128)S(1)} copy(f32[32,4,32,256]{3,2,1,0:T(8,128)} %bitcast.63) | data formatting | bytes 8388608 | tf_op jit(solution)/shard_map/reshape | solution.py:234
  97.5 1.9 copy-done.1
  99.5 3.0 copy.24
  102.4 19.4 %all-gather.8.cloned.1.call-done = f32[7,1024,128]{2,1,0:T(8,128)} async-done(((f32[7,128,128]{2,1,0:T(8,128)}), f32[7,1024,128]{2,1,0:T(8,128)}) %all-gather.8.cloned.1.call-update) | async-done | bytes 3670032 | tf_op jit(solution)/shard_map/all_gather | solution.py:226
  121.9 1.8 fusion.4
  123.7 2.3 convolution_bitcast_fusion.x_ref
  126.0 8.7 %shard_map.69 = f32[1,64,128]{2,1,0:T(8,128)} custom-call(f32[1,512,128]{2,1,0:T(8,128)} %convolution_bitcast_fusion.x_ref), custom_call_target="tpu_custom_call" | custom-call | tf_op jit(solution)/shard_map/pallas_call | solution.py:186
  137.2 2.3 slice.64.fac_ref
  139.5 5.5 %reshape_reshape.3 = f32[1024,8,128]{2,1,0:T(8,128)} reshape(f32[32,32,4,256]{3,2,1,0:T(4,128)} %bitcast.55) | data formatting | bytes 8388608 | tf_op jit(solution)/shard_map/reshape;reshape | solution.py:278
  145.0 5.0 %copy.28 = f32[1024,8,128]{2,0,1:T(8,128)} copy(f32[1024,8,128]{2,1,0:T(8,128)} %reshape_reshape.3) | data formatting | bytes 8388608 | tf_op jit(solution)/shard_map/reshape;reshape | solution.py:278
  150.0 31.4 %all-gather.12.cloned.1.call-done = f32[32,192,128]{2,1,0:T(8,128)} async-done(((f32[1,192,128]{2,1,0:T(8,128)}), f32[32,192,128]{2,1,0:T(8,128)}) %all-gather.12.cloned.1.call-update) | async-done | bytes 3145744 | tf_op jit(solution)/shard_map/all_gather | solution.py:248
  181.4 5.4 %shard_map.70 = f32[2,128,128]{2,1,0:T(8,128)} custom-call(s32[19]{0:T(128)} %pad_add_fusion.info_ref, f32[8,4,1,192,128]{4,3,2,1,0:T(8,128)} %bitcast.56, f32[8,1024,128]{2,1,0:T(8,128)} %bitcast.59, f32[2,1024,128]{2,1,0:T(8,128)} %slice.64.fac_ref), custom_call_target="tpu_custom_call" | custom-call | tf_op jit(solution)/shard_map/pallas_call | solution.py:104
  186.8 2.9 fusion.12.x_ref
  189.7 12.0 %shard_map.71 = f32[2,64,128]{2,1,0:T(8,128)} custom-call(f32[2,512,128]{2,1,0:T(8,128)} %fusion.12.x_ref), custom_call_target="tpu_custom_call" | custom-call | tf_op jit(solution)/shard_map/pallas_call | solution.py:186
  203.9 3.1 slice.66.fac_ref
  208.4 43.0 %all-gather.14.cloned.1.call-done = f32[64,192,128]{2,1,0:T(8,128)} async-done(((f32[2,192,128]{2,1,0:T(8,128)}), f32[64,192,128]{2,1,0:T(8,128)}) %all-gather.14.cloned.1.call-update) | async-done | bytes 6291472 | tf_op jit(solution)/shard_map/all_gather | solution.py:248
  251.4 3.2 %slice.68 = f32[8,4,2,64,128]{4,3,2,1,0:T(8,128)} slice(f32[8,4,2,192,128]{4,3,2,1,0:T(8,128)} %bitcast.60), slice={[0:8], [0:4], [0:2], [128:192], [0:128]} | slice | bytes 4194304 | tf_op jit(solution)/shard_map/slice | solution.py:269
  254.6 7.9 %shard_map.72 = f32[4,128,128]{2,1,0:T(8,128)} custom-call(s32[37]{0:T(128)} %pad_add_fusion.1.info_ref, f32[8,4,2,192,128]{4,3,2,1,0:T(8,128)} %bitcast.61, f32[8,4,1,192,128]{4,3,2,1,0:T(8,128)} %bitcast.58, f32[4,1024,128]{2,1,0:T(8,128)} %slice.66.fac_ref), custom_call_target="tpu_custom_call" | custom-call | tf_op jit(solution)/shard_map/pallas_call | solution.py:104
  262.5 3.1 fusion.13
  266.6 30.2 %shard_map.73 = f32[4,512,128]{2,1,0:T(8,128)} custom-call(f32[4,512,128]{2,1,0:T(8,128)} %copy-done.3), custom_call_target="tpu_custom_call" | custom-call | tf_op jit(solution)/shard_map/pallas_call | solution.py:186
  (57 shorter events, 16.2 us)
Async XLA Ops:
  8.0 1.5 copy-start
  8.0 83.7 %all-gather.10.cloned.1.call-start = ((), (), s32[]{:S(2)}) async-start(), calls=%async_computation.3 | async-start | bytes 4227072 | tf_op jit(solution)/shard_map/all_gather | solution.py:233
  8.7 113.1 %all-gather.8.cloned.1.call-start = ((), (), s32[]{:S(2)}) async-start(), calls=%async_computation.1 | async-start | bytes 4128768 | tf_op jit(solution)/shard_map/all_gather | solution.py:226
  13.4 49.9 %copy-start.10 = (s32[1,6,8]{2,0,1:T(1,128)S(1)}, s32[1,6,8]{2,0,1:T(1,128)}, u32[]{:S(2)}) copy-start(s32[1,6,8]{2,0,1:T(1,128)} %param.8) | copy-start | bytes 580
  65.4 1.2 copy-start.2
  67.5 67.3 %reduce-scatter.2.cloned.1.call-start = ((), (), s32[]{:S(2)}) async-start(), calls=%async_computation.2 | async-start | bytes 1146880 | tf_op jit(solution)/shard_map/reduce_scatter | solution.py:230
  69.8 111.6 %all-gather.12.cloned.1.call-start = ((), (), s32[]{:S(2)}) async-start(), calls=%async_computation.4 | async-start | bytes 3244032 | tf_op jit(solution)/shard_map/all_gather | solution.py:248
  97.5 2.0 copy-start.1
  123.7 21.3 %copy-start.7 = (f32[128,128]{1,0:T(8,128)}, f32[128,128]{1,0:T(8,128)S(1)}, u32[]{:S(2)}) copy-start(f32[128,128]{1,0:T(8,128)S(1)} %fusion.4) | copy-start | bytes 196612
  136.2 115.1 %all-gather.14.cloned.1.call-start = ((), (), s32[]{:S(2)}) async-start(), calls=%async_computation.5 | async-start | bytes 6488064 | tf_op jit(solution)/shard_map/all_gather | solution.py:248
  186.8 14.9 %copy-start.9 = (f32[7,64,128]{2,1,0:T(8,128)S(1)}, f32[7,64,128]{2,1,0:T(8,128)}, u32[]{:S(2)}) copy-start(f32[7,64,128]{2,1,0:T(8,128)} %reduce-scatter.2.cloned.1.call-done) | copy-start | bytes 688132
  186.8 15.7 %copy-start.6 = (f32[2,128,128]{2,1,0:T(8,128)S(1)}, f32[2,128,128]{2,1,0:T(8,128)}, u32[]{:S(2)}) copy-start(f32[2,128,128]{2,1,0:T(8,128)} %shard_map.70) | copy-start | bytes 393220
  186.8 16.6 %copy-start.11 = (s32[1,4]{1,0:T(1,128)S(1)}, s32[1,4]{1,0:T(1,128)}, u32[]{:S(2)}) copy-start(s32[1,4]{1,0:T(1,128)} %param.9) | copy-start | bytes 52
  265.6 1.0 copy-start.3
  266.6 31.5 %copy-start.5 = (f32[4,128,128]{2,1,0:T(8,128)S(1)}, f32[4,128,128]{2,1,0:T(8,128)}, u32[]{:S(2)}) copy-start(f32[4,128,128]{2,1,0:T(8,128)} %shard_map.72) | copy-start | bytes 786436
  296.8 1.3 copy-start.8
  296.8 2.1 copy-start.4
Sparse Core Ops, SparseCore 0:
  12.0 79.6 all-gather.9
  93.9 27.8 all-gather.7
Sparse Core Ops, SparseCore 1:
  70.4 25.3 reduce-scatter.1
  136.3 45.0 all-gather.11
  203.3 48.0 all-gather.13

commit v6 on v5

--- a/solution.py
+++ b/solution.py
@@ -43,17 +43,21 @@
     )
 
 
-def level_kernel(info_ref, par_ref, low_ref, fac_ref, out_ref, *, level, tile, band, own_tiles, slot_count):
+def level_kernel(info_ref, par_ref, low_ref, fac_ref, out_ref, *rest, level, tile, band, own_tiles, slot_count,
+                 par_prow, low_prow, halves):
     count = out_ref.shape[0]
     split = tile // band
     r = info_ref[0]
-    own = jnp.minimum(r, own_tiles - 1)
-
-    def p_tile(ref, node, q, m):
-        return ref[q, m, node, 0:tile, :]
-
-    def d_tile(ref, node, a, m):
-        return jnp.concatenate([ref[a * split + h, m, node, tile:tile + band, :] for h in range(split)], axis=0)
+    own = lax.rem(r, own_tiles)
+
+    def p_tile(ref, prow, node, q, m):
+        if prow == tile:
+            return ref[q, m, node, 0:tile, :]
+        parts = tile // prow
+        return jnp.concatenate([ref[q + j * own_tiles, m, node, 0:prow, :] for j in range(parts)], axis=0)
+
+    def d_tile(ref, prow, node, a, m):
+        return jnp.concatenate([ref[a * split + h, m, node, prow:prow + band, :] for h in range(split)], axis=0)
 
     for i in range(count):
         base = 1 + i * slot_count
@@ -62,33 +66,44 @@
         picks = [jnp.clip(info_ref[base + k], 0, slot_count - 1) for k in range(slot_count)]
         source = info_ref[base + jnp.maximum(r, own_tiles)]
 
+        upper = dot_hi(d_tile(par_ref, par_prow, parent, own, 0), factor[0])
+        for k in range(1, own_tiles):
+            upper += dot_hi(d_tile(par_ref, par_prow, parent, own, k), factor[k])
+        for k in range(own_tiles, slot_count):
+            pick = picks[k] if par_prow == tile else jnp.minimum(picks[k], own_tiles - 1)
+            upper -= dot_t_hi(p_tile(par_ref, par_prow, parent, pick, own), factor[k])
+
+        if halves:
+            half_ref = rest[0]
+            rows = tile // halves
+            which = r // own_tiles
+            half = upper[0:rows]
+            for j in range(1, halves):
+                half = jnp.where(which == j, upper[j * rows:(j + 1) * rows], half)
+            half_ref[i] = half
+
         @pl.when(r < own_tiles)
         def _():
-            acc = dot_hi(d_tile(par_ref, parent, own, 0), factor[0])
-            for k in range(1, own_tiles):
-                acc += dot_hi(d_tile(par_ref, parent, own, k), factor[k])
-            for k in range(own_tiles, slot_count):
-                acc -= dot_t_hi(p_tile(par_ref, parent, picks[k], own), factor[k])
-            out_ref[i] = acc
+            out_ref[i] = upper
 
         @pl.when(jnp.logical_and(r >= own_tiles, source >= 0))
         def _():
             if level == 1:
                 s = jnp.clip(source, 0, slot_count - 1)
                 start = pl.multiple_of(s * tile, tile)
-                acc = -dot_hi(p_tile(par_ref, parent, s, 0), factor[0])
+                acc = -dot_hi(p_tile(par_ref, par_prow, parent, s, 0), factor[0])
                 for k in range(1, own_tiles):
-                    acc -= dot_hi(p_tile(par_ref, parent, s, k), factor[k])
+                    acc -= dot_hi(p_tile(par_ref, par_prow, parent, s, k), factor[k])
                 for k in range(own_tiles, slot_count):
                     acc += dot_hi(low_ref[picks[k], pl.ds(start, tile), :], factor[k])
             else:
                 s = jnp.clip(source, 0, own_tiles - 1)
-                acc = -dot_hi(p_tile(par_ref, parent, s, 0), factor[0])
+                acc = -dot_hi(p_tile(par_ref, par_prow, parent, s, 0), factor[0])
                 for k in range(1, own_tiles):
-                    acc -= dot_hi(p_tile(par_ref, parent, s, k), factor[k])
+                    acc -= dot_hi(p_tile(par_ref, par_prow, parent, s, k), factor[k])
                 for k in range(own_tiles, slot_count):
                     q = jnp.minimum(picks[k], own_tiles - 1)
-                    acc += dot_hi(d_tile(low_ref, 0, s, q), factor[k])
+                    acc += dot_hi(d_tile(low_ref, low_prow, 0, s, q), factor[k])
             out_ref[i] = acc
 
         @pl.when(jnp.logical_and(r >= own_tiles, source < 0))
@@ -96,16 +111,22 @@
             out_ref[i] = jnp.zeros((tile, tile), jnp.float32)
 
 
-def level_products(info, parent_data, low_data, factors, level, tile, band, own_tiles, slot_count):
+def level_products(info, parent_data, low_data, factors, level, tile, band, own_tiles, slot_count,
+                   par_prow, low_prow, halves):
     kernel = functools.partial(
-        level_kernel, level=level, tile=tile, band=band, own_tiles=own_tiles, slot_count=slot_count
+        level_kernel, level=level, tile=tile, band=band, own_tiles=own_tiles, slot_count=slot_count,
+        par_prow=par_prow, low_prow=low_prow, halves=halves,
     )
     vmem = pl.BlockSpec(memory_space=pltpu.VMEM)
+    count = factors.shape[0]
+    shapes = [jax.ShapeDtypeStruct((count, tile, tile), jnp.float32)]
+    if halves:
+        shapes.append(jax.ShapeDtypeStruct((count, tile // halves, tile), jnp.float32))
     return pl.pallas_call(
         kernel,
-        out_shape=jax.ShapeDtypeStruct((factors.shape[0], tile, tile), jnp.float32),
+        out_shape=tuple(shapes),
         in_specs=[pl.BlockSpec(memory_space=pltpu.SMEM), vmem, vmem, vmem],
-        out_specs=vmem,
+        out_specs=tuple([vmem] * len(shapes)),
     )(info, parent_data, low_data, factors)
 
 
@@ -240,13 +261,13 @@
         rows = factor_rows[first:first + products.shape[0]]
         return mm(jnp.transpose(rows, (0, 2, 1)), products)
 
-    def reduce_and_gather(first, products):
+    def reduce_and_gather(first, products, sent):
         count = products.shape[0]
         piece = axis_reduce(diag_partial(first, products), "row", row_count, False, first)
         piece = piece + gram_piece[first:first + count]
-        both = jnp.concatenate([products, piece], axis=1)
+        both = jnp.concatenate([sent, piece], axis=1)
         everything = lax.all_gather(both, ("row", "col"), axis=0)
-        return everything.reshape(row_count, col_count, count, tile + band, tile)
+        return everything.reshape(row_count, col_count, count, sent.shape[1] + band, tile)
 
     bands_per_tile = tile // band
 
@@ -266,27 +287,30 @@
         return jnp.transpose(pieces, (0, 2, 1, 3)).reshape(tile, -1)
 
     def diag_col(gathered, m):
-        pieces = lax.dynamic_index_in_dim(gathered[:, :, :, tile:], m, 1, keepdims=False)
+        pieces = lax.dynamic_index_in_dim(gathered[:, :, :, -band:], m, 1, keepdims=False)
         return jnp.transpose(pieces, (1, 0, 2, 3)).reshape(pieces.shape[1], -1, tile)
 
     own_row = jnp.minimum(r, own_tiles - 1)
     upper = r < own_tiles
 
     product_0 = mm(tile_rows(sigma, r, tile), factor_cols[0])
-    gathered_0 = reduce_and_gather(0, product_0[None])
+    gathered_0 = reduce_and_gather(0, product_0[None], product_0[None])
 
     sigma_tiles = jnp.transpose(sigma.reshape(sigma.shape[0], slot_count, tile), (1, 0, 2))
     info_1 = jnp.concatenate([r.astype(jnp.int32)[None], picks_all[0:2].reshape(-1), jnp.zeros((2,), jnp.int32)])
-    product_1 = level_products(
-        info_1, gathered_0, sigma_tiles, factor_cols[1:3], 1, tile, band, own_tiles, slot_count
-    )
-    gathered_1 = reduce_and_gather(1, product_1)
+    halves = row_count // own_tiles
+    product_1, upper_half = level_products(
+        info_1, gathered_0, sigma_tiles, factor_cols[1:3], 1, tile, band, own_tiles, slot_count,
+        tile, tile, halves,
+    )
+    gathered_1 = reduce_and_gather(1, product_1, upper_half)
 
     info_2 = jnp.concatenate(
         [r.astype(jnp.int32)[None], picks_all[2:nodes - 1].reshape(-1), (parents - 1).astype(jnp.int32)]
     )
-    product_2 = level_products(
-        info_2, gathered_1, gathered_0, factor_cols[3:nodes], 2, tile, band, own_tiles, slot_count
+    (product_2,) = level_products(
+        info_2, gathered_1, gathered_0, factor_cols[3:nodes], 2, tile, band, own_tiles, slot_count,
+        tile // halves, tile, 0,
     )
     first_2 = 3
     count_2 = product_2.shape[0]

time: 309 us -> 309 us (level)
    unnamed x25 -> x23, local copies, waits for them, and re-layouts: 7.84 us -> 7.84 us
where the time goes in v6:
time: 309 us; the launch traced here: 308 us
  Pallas kernels  116 us (38%)
  waiting for transfers between devices  115 us (37%)
  local copies, waits for them, and re-layouts  36.3 us (12%)
  matrix products  16.2 us (5%)
  between operations  15.9 us (5%)
  other arithmetic  8.43 us (3%)
    pallas_call x4, Pallas kernels, axis_reduce(): pl.pallas_call(kernel, out_shape=jax.ShapeDtypeStruct((lead, out_rows, la...  103 us
    all_gather x2, waiting for transfers between devices, reduce_and_gather(): everything = lax.all_gather(both, ('row', 'col'), axis=0)  72.7 us
    all_gather x1, waiting for transfers between devices, body(): gathered = lax.all_gather(sigma_top, ('leaf', 'row', 'col'), axis=0)  21.8 us
    all_gather x1, waiting for transfers between devices, body(): factor_cols = lax.all_gather(factor_tile, 'row', axis=1, tiled=True)  19.4 us
    dot_general x6, matrix products, mm(): jnp.matmul(a, b, precision=HIGHEST, preferred_element_type=jnp.float32)  16.2 us
    pallas_call x2, Pallas kernels, level_products(): pl.pallas_call(kernel, out_shape=tuple(shapes), in_specs=[pl.BlockSpec(me...  12.6 us
    another operation x2, local copies, waits for them, and re-layouts, body(): sigma.reshape(sigma.shape[0], slot_count, tile)  10.5 us
    unnamed x23, local copies, waits for them, and re-layouts  7.84 us
  transfers between devices with their start and end apart: 5, of which 4 were waited for; matrix products, arithmetic and copies ran while one was open for 13% of the time, Pallas kernels for 19%

profile of v6, /device:TPU:1, one launch (start us, length us, event | category | flops | bytes accessed | tf_op | source)
XLA Modules:
  0.0 307.7 jit_solution(6723025156336579371)
XLA Ops:
  9.5 3.9 %fusion.2.x_ref = f32[7,128,512]{2,1,0:T(8,128)} fusion(f32[1,7,128,512]{3,2,1,0:T(8,128)S(1)} %copy-done, f32[1,7,128,128]{3,2,1,0:T(8,128)} %param.6), kind=kOutput, calls=%fused_computation.4 | convolution fusion | flops 704643072 | bytes 4128768 | tf_op jit(solution)/shard_map/dot_general | solution.py:15
  13.4 49.8 %shard_map.68 = f32[7,128,512]{2,1,0:T(8,128)} custom-call(f32[7,128,512]{2,1,0:T(8,128)} %fusion.2.x_ref), custom_call_target="tpu_custom_call" | custom-call | tf_op jit(solution)/shard_map/pallas_call | solution.py:207
  67.5 2.3 fusion
  69.9 21.8 %all-gather.10.cloned.1.call-done = f32[4096,256]{1,0:T(8,128)} async-done(((f32[32,256]{1,0:T(8,128)}), f32[4096,256]{1,0:T(8,128)}) %all-gather.10.cloned.1.call-update) | async-done | bytes 4194320 | tf_op jit(solution)/shard_map/all_gather | solution.py:254
  91.7 5.8 %copy.29 = f32[32,4,32,256]{3,1,2,0:T(4,128)S(1)} copy(f32[32,4,32,256]{3,2,1,0:T(8,128)} %bitcast.63) | data formatting | bytes 8388608 | tf_op jit(solution)/shard_map/reshape | solution.py:255
  97.5 1.9 copy-done.1
  99.5 3.0 copy.24
  102.4 19.4 %all-gather.8.cloned.1.call-done = f32[7,1024,128]{2,1,0:T(8,128)} async-done(((f32[7,128,128]{2,1,0:T(8,128)}), f32[7,1024,128]{2,1,0:T(8,128)}) %all-gather.8.cloned.1.call-update) | async-done | bytes 3670032 | tf_op jit(solution)/shard_map/all_gather | solution.py:247
  121.9 1.8 fusion.4
  123.7 2.2 convolution_bitcast_fusion.x_ref
  125.9 8.7 %shard_map.69 = f32[1,64,128]{2,1,0:T(8,128)} custom-call(f32[1,512,128]{2,1,0:T(8,128)} %convolution_bitcast_fusion.x_ref), custom_call_target="tpu_custom_call" | custom-call | tf_op jit(solution)/shard_map/pallas_call | solution.py:207
  137.1 2.3 slice.64.fac_ref
  139.4 5.5 %reshape_reshape.3 = f32[1024,8,128]{2,1,0:T(8,128)} reshape(f32[32,32,4,256]{3,2,1,0:T(4,128)} %bitcast.55) | data formatting | bytes 8388608 | tf_op jit(solution)/shard_map/reshape;reshape | solution.py:299
  144.9 5.0 %copy.28 = f32[1024,8,128]{2,0,1:T(8,128)} copy(f32[1024,8,128]{2,1,0:T(8,128)} %reshape_reshape.3) | data formatting | bytes 8388608 | tf_op jit(solution)/shard_map/reshape;reshape | solution.py:299
  149.9 31.4 %all-gather.12.cloned.1.call-done = f32[32,192,128]{2,1,0:T(8,128)} async-done(((f32[1,192,128]{2,1,0:T(8,128)}), f32[32,192,128]{2,1,0:T(8,128)}) %all-gather.12.cloned.1.call-update) | async-done | bytes 3145744 | tf_op jit(solution)/shard_map/all_gather | solution.py:269
  181.4 5.4 %shard_map.70 = (f32[2,128,128]{2,1,0:T(8,128)}, f32[2,64,128]{2,1,0:T(8,128)}) custom-call(s32[19]{0:T(128)} %pad_add_fusion.info_ref, f32[8,4,1,192,128]{4,3,2,1,0:T(8,128)} %bitcast.56, f32[8,1024,128]{2,1,0:T(8,128)} %bitcast.59, f32[2,1024,128]{2,1,0:T(8,128)} %slice.64.fac_ref), custom_call_target="tpu_custom_call" | custom-call | tf_op jit(solution)/shard_map/pallas_call | solution.py:125
  186.7 2.9 fusion.12.x_ref
  189.6 12.0 %shard_map.71 = f32[2,64,128]{2,1,0:T(8,128)} custom-call(f32[2,512,128]{2,1,0:T(8,128)} %fusion.12.x_ref), custom_call_target="tpu_custom_call" | custom-call | tf_op jit(solution)/shard_map/pallas_call | solution.py:207
  203.9 3.1 slice.66.fac_ref
  208.3 41.3 %all-gather.14.cloned.1.call-done = f32[64,128,128]{2,1,0:T(8,128)} async-done(((f32[2,128,128]{2,1,0:T(8,128)}), f32[64,128,128]{2,1,0:T(8,128)}) %all-gather.14.cloned.1.call-update) | async-done | bytes 4194320 | tf_op jit(solution)/shard_map/all_gather | solution.py:269
  249.6 3.2 %slice.68 = f32[8,4,2,64,128]{4,3,2,1,0:T(8,128)} slice(f32[8,4,2,128,128]{4,3,2,1,0:T(8,128)} %bitcast.60), slice={[0:8], [0:4], [0:2], [64:128], [0:128]} | slice | bytes 4194304 | tf_op jit(solution)/shard_map/slice | solution.py:290
  252.8 7.3 %shard_map.72 = f32[4,128,128]{2,1,0:T(8,128)} custom-call(s32[37]{0:T(128)} %pad_add_fusion.1.info_ref, f32[8,4,2,128,128]{4,3,2,1,0:T(8,128)} %bitcast.61, f32[8,4,1,192,128]{4,3,2,1,0:T(8,128)} %bitcast.58, f32[4,1024,128]{2,1,0:T(8,128)} %slice.66.fac_ref), custom_call_target="tpu_custom_call" | custom-call | tf_op jit(solution)/shard_map/pallas_call | solution.py:125
  260.0 3.1 fusion.13
  264.1 32.6 %shard_map.73 = f32[4,512,128]{2,1,0:T(8,128)} custom-call(f32[4,512,128]{2,1,0:T(8,128)} %copy-done.3), custom_call_target="tpu_custom_call" | custom-call | tf_op jit(solution)/shard_map/pallas_call | solution.py:207
  (55 shorter events, 16.1 us)
Async XLA Ops:
  8.0 1.5 copy-start
  8.0 83.7 %all-gather.10.cloned.1.call-start = ((), (), s32[]{:S(2)}) async-start(), calls=%async_computation.3 | async-start | bytes 4227072 | tf_op jit(solution)/shard_map/all_gather | solution.py:254
  8.7 113.1 %all-gather.8.cloned.1.call-start = ((), (), s32[]{:S(2)}) async-start(), calls=%async_computation.1 | async-start | bytes 4128768 | tf_op jit(solution)/shard_map/all_gather | solution.py:247
  13.4 49.9 %copy-start.9 = (s32[1,6,8]{2,0,1:T(1,128)S(1)}, s32[1,6,8]{2,0,1:T(1,128)}, u32[]{:S(2)}) copy-start(s32[1,6,8]{2,0,1:T(1,128)} %param.8) | copy-start | bytes 580
  65.4 1.2 copy-start.2
  67.5 67.3 %reduce-scatter.2.cloned.1.call-start = ((), (), s32[]{:S(2)}) async-start(), calls=%async_computation.2 | async-start | bytes 1146880 | tf_op jit(solution)/shard_map/reduce_scatter | solution.py:251
  69.8 111.5 %all-gather.12.cloned.1.call-start = ((), (), s32[]{:S(2)}) async-start(), calls=%async_computation.4 | async-start | bytes 3244032 | tf_op jit(solution)/shard_map/all_gather | solution.py:269
  97.5 2.0 copy-start.1
  136.2 113.4 %all-gather.14.cloned.1.call-start = ((), (), s32[]{:S(2)}) async-start(), calls=%async_computation.5 | async-start | bytes 4325376 | tf_op jit(solution)/shard_map/all_gather | solution.py:269
  186.7 14.9 %copy-start.7 = (f32[7,64,128]{2,1,0:T(8,128)S(1)}, f32[7,64,128]{2,1,0:T(8,128)}, u32[]{:S(2)}) copy-start(f32[7,64,128]{2,1,0:T(8,128)} %reduce-scatter.2.cloned.1.call-done) | copy-start | bytes 688132
  186.7 15.7 %copy-start.8 = (f32[2,64,128]{2,1,0:T(8,128)S(1)}, f32[2,64,128]{2,1,0:T(8,128)}, u32[]{:S(2)}) copy-start(f32[2,64,128]{2,1,0:T(8,128)} %get-tuple-element.5) | copy-start | bytes 196612
  186.7 16.5 %copy-start.10 = (s32[1,4]{1,0:T(1,128)S(1)}, s32[1,4]{1,0:T(1,128)}, u32[]{:S(2)}) copy-start(s32[1,4]{1,0:T(1,128)} %param.9) | copy-start | bytes 52
  263.1 1.0 copy-start.3
  264.1 33.8 %copy-start.5 = (f32[4,128,128]{2,1,0:T(8,128)S(1)}, f32[4,128,128]{2,1,0:T(8,128)}, u32[]{:S(2)}) copy-start(f32[4,128,128]{2,1,0:T(8,128)} %shard_map.72) | copy-start | bytes 786436
  296.7 1.3 copy-start.6
  296.7 2.1 copy-start.4
Sparse Core Ops, SparseCore 0:
  12.0 79.6 all-gather.9
  93.9 27.8 all-gather.7
Sparse Core Ops, SparseCore 1:
  70.4 25.3 reduce-scatter.1
  136.3 45.0 all-gather.11
  203.2 46.3 all-gather.13

commit v7 on v6

--- a/solution.py
+++ b/solution.py
@@ -220,6 +220,115 @@
     )(x)
 
 
+def factor_kernel(x_ref, rows_ref, cols_ref, recv_ref, sems, *, tile):
+    r = lax.axis_index("row")
+    c = lax.axis_index("col")
+    leaf = lax.axis_index("leaf")
+    row_count = lax.axis_size("row")
+    col_count = lax.axis_size("col")
+    mesh_ids = pl.DeviceIdType.MESH
+    col_peers = [lax.rem(c + d, col_count) for d in range(1, col_count)]
+    row_peers = [lax.rem(r + d, row_count) for d in range(1, row_count)]
+
+    barrier = pltpu.get_barrier_semaphore()
+    for peer in col_peers:
+        pl.semaphore_signal(barrier, inc=1, device_id=(leaf, r, peer), device_id_type=mesh_ids)
+    for peer in row_peers:
+        pl.semaphore_signal(barrier, inc=1, device_id=(leaf, peer, c), device_id_type=mesh_ids)
+    pl.semaphore_wait(barrier, len(col_peers) + len(row_peers))
+
+    def col_slice(index):
+        return pl.ds(pl.multiple_of(index * tile, tile), tile)
+
+    sends = []
+    for d, peer in enumerate(col_peers):
+        copy = pltpu.make_async_remote_copy(
+            src_ref=x_ref.at[:, :, col_slice(peer)],
+            dst_ref=recv_ref.at[d],
+            send_sem=sems.at[0, d],
+            recv_sem=sems.at[1, d],
+            device_id=(leaf, r, peer),
+            device_id_type=mesh_ids,
+        )
+        copy.start()
+        sends.append(copy)
+    for copy in sends:
+        copy.wait_recv()
+    for copy in sends:
+        copy.wait_send()
+    total = x_ref[:, :, col_slice(c)]
+    for d in range(len(col_peers)):
+        total = total + recv_ref[d]
+    rows_ref[:, :, col_slice(c)] = total
+    cols_ref[:, col_slice(r), :] = total
+
+    sends = []
+    for d, peer in enumerate(row_peers):
+        copy = pltpu.make_async_remote_copy(
+            src_ref=cols_ref.at[:, col_slice(r), :],
+            dst_ref=cols_ref.at[:, col_slice(r), :],
+            send_sem=sems.at[2, d],
+            recv_sem=sems.at[3, d],
+            device_id=(leaf, peer, c),
+            device_id_type=mesh_ids,
+        )
+        copy.start()
+        sends.append(copy)
+    for d, peer in enumerate(col_peers):
+        copy = pltpu.make_async_remote_copy(
+            src_ref=rows_ref.at[:, :, col_slice(c)],
+            dst_ref=rows_ref.at[:, :, col_slice(c)],
+            send_sem=sems.at[4, d],
+            recv_sem=sems.at[5, d],
+            device_id=(leaf, r, peer),
+            device_id_type=mesh_ids,
+        )
+        copy.start()
+        sends.append(copy)
+    for d in range(1, row_count):
+        source = lax.rem(r + row_count - d, row_count)
+        pltpu.make_async_remote_copy(
+            src_ref=cols_ref.at[:, col_slice(source), :],
+            dst_ref=cols_ref.at[:, col_slice(source), :],
+            send_sem=sems.at[2, d - 1],
+            recv_sem=sems.at[3, d - 1],
+            device_id=(leaf, source, c),
+            device_id_type=mesh_ids,
+        ).wait_recv()
+    for d in range(1, col_count):
+        source = lax.rem(c + col_count - d, col_count)
+        pltpu.make_async_remote_copy(
+            src_ref=rows_ref.at[:, :, col_slice(source)],
+            dst_ref=rows_ref.at[:, :, col_slice(source)],
+            send_sem=sems.at[4, d - 1],
+            recv_sem=sems.at[5, d - 1],
+            device_id=(leaf, r, source),
+            device_id_type=mesh_ids,
+        ).wait_recv()
+    for copy in sends:
+        copy.wait_send()
+
+
+def factor_exchange(partial, row_count, col_count, tile, collective_id):
+    nodes, rows, width = partial.shape
+    vmem = pl.BlockSpec(memory_space=pltpu.VMEM)
+    peers = max(row_count, col_count) - 1
+    return pl.pallas_call(
+        functools.partial(factor_kernel, tile=tile),
+        out_shape=(
+            jax.ShapeDtypeStruct((nodes, rows, width), partial.dtype),
+            jax.ShapeDtypeStruct((nodes, row_count * tile, tile), partial.dtype),
+        ),
+        in_specs=[vmem],
+        out_specs=(vmem, vmem),
+        scratch_shapes=[
+            pltpu.VMEM((col_count - 1, nodes, rows, tile), partial.dtype),
+            pltpu.SemaphoreType.DMA((6, peers)),
+        ],
+        compiler_params=pltpu.CompilerParams(collective_id=collective_id, has_side_effects=True),
+    )(partial)
+
+
 def body(sigma_top, panels, inverse_diag, slot_lists, parent_links):
     tile = TILE
     row_count = lax.axis_size("row")
@@ -239,12 +348,11 @@
     band = width // row_count
 
     partial_factor = mm(panel, inverse)
-    factor_rows = axis_reduce(partial_factor, "col", col_count, True, 3)
+    factor_rows, factor_cols = factor_exchange(partial_factor, row_count, col_count, tile, 3)
     living = jnp.concatenate([jnp.ones((1, slot_count), jnp.bool_), picks_all >= 0], axis=0)
-    live_here = jnp.take(living, r, axis=1).astype(jnp.float32)
-    factor_rows = factor_rows * live_here[:, None, None]
-    factor_tile = lax.dynamic_slice_in_dim(factor_rows, c * tile, tile, 2)
-    factor_cols = lax.all_gather(factor_tile, "row", axis=1, tiled=True)
+    live_weight = living.astype(jnp.float32)
+    factor_rows = factor_rows * jnp.take(live_weight, r, axis=1)[:, None, None]
+    factor_cols = factor_cols * jnp.repeat(live_weight, tile, axis=1)[:, :, None]
 
     inverse_band = lax.dynamic_slice_in_dim(inverse, r * band, band, 2)
     partial_gram = mm(jnp.transpose(inverse_band, (0, 2, 1)), inverse)

time: 309 us -> 312 us (level)
  Pallas kernels: 116 us -> 149 us
  waiting for transfers between devices: 115 us -> 87.2 us
  local copies, waits for them, and re-layouts: 36.3 us -> 31.4 us
  other arithmetic: 8.43 us -> 12.3 us
    pallas_call x0 -> x1, Pallas kernels: none -> 83.6 us  [factor_exchange(): pl.pallas_call(functools.partial(factor_kernel, tile=tile), out_shape=(ja...]
    pallas_call x4 -> x3, Pallas kernels: 103 us -> 53.3 us  [axis_reduce(): pl.pallas_call(kernel, out_shape=jax.ShapeDtypeStruct((lead, out_rows, la...]
    all_gather x1 -> x0, waiting for transfers between devices: 19.4 us -> none  [body(): factor_cols = lax.all_gather(factor_tile, 'row', axis=1, tiled=True)]
    all_gather x1, waiting for transfers between devices: 21.8 us -> 16 us  [body(): gathered = lax.all_gather(sigma_top, ('leaf', 'row', 'col'), axis=0)]
    unnamed x23 -> x27, local copies, waits for them, and re-layouts: 7.84 us -> 3.83 us
    mul x1 -> x2, other arithmetic: 1.78 us -> 5.67 us  [the longest x1 3.24 us: body(): factor_rows = factor_rows * jnp.take(live_weight, r, axis=1)[:, None, None]]
  transfers between devices with their start and end apart: 5 -> 4, of which waited for: 4 -> 3; matrix products, arithmetic and copies ran while one was open for 13% -> 13% of each run, Pallas kernels for 19% -> 30%
where the time goes in v7:
time: 312 us
  Pallas kernels  149 us (48%)
  waiting for transfers between devices  87.2 us (28%)
  local copies, waits for them, and re-layouts  31.4 us (10%)
  between operations  15.9 us (5%)
  matrix products  15 us (5%)
  other arithmetic  12.3 us (4%)
    pallas_call x1, Pallas kernels, factor_exchange(): pl.pallas_call(functools.partial(factor_kernel, tile=tile), out_shape=(ja...  83.6 us
    all_gather x2, waiting for transfers between devices, reduce_and_gather(): everything = lax.all_gather(both, ('row', 'col'), axis=0)  70.4 us
    pallas_call x3, Pallas kernels, axis_reduce(): pl.pallas_call(kernel, out_shape=jax.ShapeDtypeStruct((lead, out_rows, la...  53.3 us
    all_gather x1, waiting for transfers between devices, body(): gathered = lax.all_gather(sigma_top, ('leaf', 'row', 'col'), axis=0)  16 us
    dot_general x6, matrix products, mm(): jnp.matmul(a, b, precision=HIGHEST, preferred_element_type=jnp.float32)  15 us
    pallas_call x2, Pallas kernels, level_products(): pl.pallas_call(kernel, out_shape=tuple(shapes), in_specs=[pl.BlockSpec(me...  12.6 us
    another operation x2, local copies, waits for them, and re-layouts, body(): sigma.reshape(sigma.shape[0], slot_count, tile)  10.4 us
  transfers between devices with their start and end apart: 4, of which 3 were waited for; matrix products, arithmetic and copies ran while one was open for 13% of the time, Pallas kernels for 30%

profile of v7, /device:TPU:1, one launch (start us, length us, event | category | flops | bytes accessed | tf_op | source)
XLA Modules:
  0.0 311.5 jit_solution(12067053448456979722)
XLA Ops:
  9.5 2.3 fusion
  11.9 2.8 fusion.2.x_ref
  14.7 83.6 %shard_map.68 = (f32[7,128,512]{2,1,0:T(8,128)}, f32[7,1024,128]{2,1,0:T(8,128)}) custom-call(f32[7,128,512]{2,1,0:T(8,128)} %fusion.2.x_ref), custom_call_target="tpu_custom_call" | custom-call | tf_op jit(solution)/shard_map/pallas_call | solution.py:316
  98.6 3.2 %broadcast_multiply_fusion.1 = f32[7,128,512]{2,1,0:T(8,128)} fusion(f32[7,128,512]{2,1,0:T(8,128)} %get-tuple-element.7, f32[7]{0:T(128)S(1)} %select_reduce_fusion), kind=kLoop, calls=%fused_computation.8 | loop fusion | flops 458752 | bytes 3670044 | tf_op jit(solution)/shard_map/mul | solution.py:354
  101.8 2.4 broadcast_multiply_fusion
  104.3 16.0 %all-gather.7.cloned.1.call-done = f32[4096,256]{1,0:T(8,128)} async-done(((f32[32,256]{1,0:T(8,128)}), f32[4096,256]{1,0:T(8,128)}) %all-gather.7.cloned.1.call-update) | async-done | bytes 4194320 | tf_op jit(solution)/shard_map/all_gather | solution.py:362
  120.3 5.8 %copy.38 = f32[32,4,32,256]{3,1,2,0:T(4,128)S(1)} copy(f32[32,4,32,256]{3,2,1,0:T(8,128)} %bitcast.70) | data formatting | bytes 8388608 | tf_op jit(solution)/shard_map/reshape | solution.py:363
  128.1 1.7 fusion.4
  129.8 2.2 convolution_bitcast_fusion.x_ref
  132.1 8.7 %shard_map.69 = f32[1,64,128]{2,1,0:T(8,128)} custom-call(f32[1,512,128]{2,1,0:T(8,128)} %convolution_bitcast_fusion.x_ref), custom_call_target="tpu_custom_call" | custom-call | tf_op jit(solution)/shard_map/pallas_call | solution.py:207
  142.5 2.3 slice.64.fac_ref
  145.6 5.5 %reshape_reshape.3 = f32[1024,8,128]{2,1,0:T(8,128)} reshape(f32[32,32,4,256]{3,2,1,0:T(4,128)} %bitcast.62) | data formatting | bytes 8388608 | tf_op jit(solution)/shard_map/reshape;reshape | solution.py:407
  151.1 4.9 %copy.36 = f32[1024,8,128]{2,0,1:T(8,128)} copy(f32[1024,8,128]{2,1,0:T(8,128)} %reshape_reshape.3) | data formatting | bytes 8388608 | tf_op jit(solution)/shard_map/reshape;reshape | solution.py:407
  156.0 29.1 %all-gather.9.cloned.1.call-done = f32[32,192,128]{2,1,0:T(8,128)} async-done(((f32[1,192,128]{2,1,0:T(8,128)}), f32[32,192,128]{2,1,0:T(8,128)}) %all-gather.9.cloned.1.call-update) | async-done | bytes 3145744 | tf_op jit(solution)/shard_map/all_gather | solution.py:377
  185.2 5.4 %shard_map.70 = (f32[2,128,128]{2,1,0:T(8,128)}, f32[2,64,128]{2,1,0:T(8,128)}) custom-call(s32[19]{0:T(128)} %pad_add_fusion.info_ref, f32[8,4,1,192,128]{4,3,2,1,0:T(8,128)} %bitcast.63, f32[8,1024,128]{2,1,0:T(8,128)} %bitcast.66, f32[2,1024,128]{2,1,0:T(8,128)} %slice.64.fac_ref), custom_call_target="tpu_custom_call" | custom-call | tf_op jit(solution)/shard_map/pallas_call | solution.py:125
  190.5 2.9 fusion.13.x_ref
  193.4 12.0 %shard_map.71 = f32[2,64,128]{2,1,0:T(8,128)} custom-call(f32[2,512,128]{2,1,0:T(8,128)} %fusion.13.x_ref), custom_call_target="tpu_custom_call" | custom-call | tf_op jit(solution)/shard_map/pallas_call | solution.py:207
  207.0 3.1 slice.66.fac_ref
  212.2 41.3 %all-gather.11.cloned.1.call-done = f32[64,128,128]{2,1,0:T(8,128)} async-done(((f32[2,128,128]{2,1,0:T(8,128)}), f32[64,128,128]{2,1,0:T(8,128)}) %all-gather.11.cloned.1.call-update) | async-done | bytes 4194320 | tf_op jit(solution)/shard_map/all_gather | solution.py:377
  253.4 3.2 %slice.68 = f32[8,4,2,64,128]{4,3,2,1,0:T(8,128)} slice(f32[8,4,2,128,128]{4,3,2,1,0:T(8,128)} %bitcast.67), slice={[0:8], [0:4], [0:2], [64:128], [0:128]} | slice | bytes 4194304 | tf_op jit(solution)/shard_map/slice | solution.py:398
  256.6 7.3 %shard_map.72 = f32[4,128,128]{2,1,0:T(8,128)} custom-call(s32[37]{0:T(128)} %pad_add_fusion.1.info_ref, f32[8,4,2,128,128]{4,3,2,1,0:T(8,128)} %bitcast.68, f32[8,4,1,192,128]{4,3,2,1,0:T(8,128)} %bitcast.65, f32[4,1024,128]{2,1,0:T(8,128)} %slice.66.fac_ref), custom_call_target="tpu_custom_call" | custom-call | tf_op jit(solution)/shard_map/pallas_call | solution.py:125
  263.9 3.1 fusion.14
  267.9 32.6 %shard_map.73 = f32[4,512,128]{2,1,0:T(8,128)} custom-call(f32[4,512,128]{2,1,0:T(8,128)} %copy-done.2), custom_call_target="tpu_custom_call" | custom-call | tf_op jit(solution)/shard_map/pallas_call | solution.py:207
  302.6 1.3 maximum_bitcast_fusion
  (57 shorter events, 13.0 us)
Async XLA Ops:
  8.0 1.5 copy-start
  8.0 112.3 %all-gather.7.cloned.1.call-start = ((), (), s32[]{:S(2)}) async-start(), calls=%async_computation.2 | async-start | bytes 4227072 | tf_op jit(solution)/shard_map/all_gather | solution.py:362
  8.7 132.1 %reduce-scatter.2.cloned.1.call-start = ((), (), s32[]{:S(2)}) async-start(), calls=%async_computation.1 | async-start | bytes 1146880 | tf_op jit(solution)/shard_map/reduce_scatter | solution.py:359
  9.5 2.3 copy-start.7
  11.8 173.4 %all-gather.9.cloned.1.call-start = ((), (), s32[]{:S(2)}) async-start(), calls=%async_computation.3 | async-start | bytes 3244032 | tf_op jit(solution)/shard_map/all_gather | solution.py:377
  14.7 83.6 %copy-start.10 = (s32[1,6,8]{2,0,1:T(1,128)S(1)}, s32[1,6,8]{2,0,1:T(1,128)}, u32[]{:S(2)}) copy-start(s32[1,6,8]{2,0,1:T(1,128)} %param.8) | copy-start | bytes 580
  98.6 3.2 %copy-start.4 = (f32[7,1024,128]{2,1,0:T(8,128)S(1)}, f32[7,1024,128]{2,1,0:T(8,128)}, u32[]{:S(2)}) copy-start(f32[7,1024,128]{2,1,0:T(8,128)} %get-tuple-element.6) | copy-start | bytes 11010052
  126.1 2.1 copy-start.1
  142.3 111.1 %all-gather.11.cloned.1.call-start = ((), (), s32[]{:S(2)}) async-start(), calls=%async_computation.4 | async-start | bytes 4325376 | tf_op jit(solution)/shard_map/all_gather | solution.py:377
  190.5 14.9 %copy-start.8 = (f32[7,64,128]{2,1,0:T(8,128)S(1)}, f32[7,64,128]{2,1,0:T(8,128)}, u32[]{:S(2)}) copy-start(f32[7,64,128]{2,1,0:T(8,128)} %reduce-scatter.2.cloned.1.call-done) | copy-start | bytes 688132
  190.5 15.7 %copy-start.9 = (f32[2,64,128]{2,1,0:T(8,128)S(1)}, f32[2,64,128]{2,1,0:T(8,128)}, u32[]{:S(2)}) copy-start(f32[2,64,128]{2,1,0:T(8,128)} %get-tuple-element.9) | copy-start | bytes 196612
  207.0 3.2 %copy-start.11 = (s32[1,4]{1,0:T(1,128)S(1)}, s32[1,4]{1,0:T(1,128)}, u32[]{:S(2)}) copy-start(s32[1,4]{1,0:T(1,128)} %param.9) | copy-start | bytes 52
  267.0 1.0 copy-start.2
  267.9 33.8 %copy-start.5 = (f32[4,128,128]{2,1,0:T(8,128)S(1)}, f32[4,128,128]{2,1,0:T(8,128)}, u32[]{:S(2)}) copy-start(f32[4,128,128]{2,1,0:T(8,128)} %shard_map.72) | copy-start | bytes 786436
  300.5 1.3 copy-start.6
  300.5 2.1 copy-start.3
Sparse Core Ops, SparseCore 0:
  12.0 108.2 all-gather.6
Sparse Core Ops, SparseCore 1:
  11.9 42.4 reduce-scatter.1
  142.4 42.8 all-gather.8
  207.1 46.3 all-gather.10

commit v8 on v7

--- a/solution.py
+++ b/solution.py
@@ -48,6 +48,7 @@
     count = out_ref.shape[0]
     split = tile // band
     r = info_ref[0]
+    col = info_ref[1 + count * slot_count + count]
     own = lax.rem(r, own_tiles)
 
     def p_tile(ref, prow, node, q, m):
@@ -90,12 +91,10 @@
         def _():
             if level == 1:
                 s = jnp.clip(source, 0, slot_count - 1)
-                start = pl.multiple_of(s * tile, tile)
-                acc = -dot_hi(p_tile(par_ref, par_prow, parent, s, 0), factor[0])
-                for k in range(1, own_tiles):
+                lifted = tile + band + i * tile
+                acc = par_ref[s, col, parent, lifted:lifted + tile, :]
+                for k in range(own_tiles):
                     acc -= dot_hi(p_tile(par_ref, par_prow, parent, s, k), factor[k])
-                for k in range(own_tiles, slot_count):
-                    acc += dot_hi(low_ref[picks[k], pl.ds(start, tile), :], factor[k])
             else:
                 s = jnp.clip(source, 0, own_tiles - 1)
                 acc = -dot_hi(p_tile(par_ref, par_prow, parent, s, 0), factor[0])
@@ -358,24 +357,38 @@
     partial_gram = mm(jnp.transpose(inverse_band, (0, 2, 1)), inverse)
     gram_piece = lax.psum_scatter(partial_gram, "col", scatter_dimension=2, tiled=True)
 
-    local_rows, local_cols = sigma_top.shape
-    gathered = lax.all_gather(sigma_top, ("leaf", "row", "col"), axis=0)
-    sigma = gathered.reshape(leaf_count * row_count, col_count, local_rows, local_cols)
-    sigma = jnp.transpose(sigma, (0, 2, 1, 3)).reshape(
-        leaf_count * row_count * local_rows, col_count * local_cols
-    )
+    leaf = lax.axis_index("leaf")
+    local_rows = sigma_top.shape[0]
+    chunk_rows = lax.all_gather(sigma_top, "col", axis=1, tiled=True)
+    chunks_per_tile = tile // local_rows
+    rounds = []
+    for t in range(chunks_per_tile):
+        pairs = []
+        for src_leaf in range(leaf_count):
+            for src_row in range(row_count):
+                q = src_leaf * row_count + src_row
+                dst_leaf = (q % chunks_per_tile + t) % leaf_count
+                dst_row = q // chunks_per_tile
+                for col in range(col_count):
+                    pairs.append(
+                        ((src_leaf * row_count + src_row) * col_count + col,
+                         (dst_leaf * row_count + dst_row) * col_count + col)
+                    )
+        rounds.append(lax.ppermute(chunk_rows, ("leaf", "row", "col"), pairs))
+    order = lax.rem(leaf - jnp.arange(chunks_per_tile, dtype=jnp.int32) + 4 * leaf_count, leaf_count)
+    sigma_rows = jnp.take(jnp.stack(rounds), order, axis=0).reshape(tile, -1)
 
     def diag_partial(first, products):
         rows = factor_rows[first:first + products.shape[0]]
         return mm(jnp.transpose(rows, (0, 2, 1)), products)
 
-    def reduce_and_gather(first, products, sent):
+    def reduce_and_gather(first, products, sent, extra):
         count = products.shape[0]
         piece = axis_reduce(diag_partial(first, products), "row", row_count, False, first)
         piece = piece + gram_piece[first:first + count]
-        both = jnp.concatenate([sent, piece], axis=1)
+        both = jnp.concatenate([sent, piece] + extra, axis=1)
         everything = lax.all_gather(both, ("row", "col"), axis=0)
-        return everything.reshape(row_count, col_count, count, sent.shape[1] + band, tile)
+        return everything.reshape(row_count, col_count, count, both.shape[1], tile)
 
     bands_per_tile = tile // band
 
@@ -394,27 +407,33 @@
         pieces = lax.dynamic_index_in_dim(pieces, node, 2, keepdims=False)
         return jnp.transpose(pieces, (0, 2, 1, 3)).reshape(tile, -1)
 
-    def diag_col(gathered, m):
-        pieces = lax.dynamic_index_in_dim(gathered[:, :, :, -band:], m, 1, keepdims=False)
+    def diag_col(gathered, m, offset):
+        pieces = lax.dynamic_index_in_dim(gathered[:, :, :, offset:offset + band], m, 1, keepdims=False)
         return jnp.transpose(pieces, (1, 0, 2, 3)).reshape(pieces.shape[1], -1, tile)
 
     own_row = jnp.minimum(r, own_tiles - 1)
     upper = r < own_tiles
 
-    product_0 = mm(tile_rows(sigma, r, tile), factor_cols[0])
-    gathered_0 = reduce_and_gather(0, product_0[None], product_0[None])
-
-    sigma_tiles = jnp.transpose(sigma.reshape(sigma.shape[0], slot_count, tile), (1, 0, 2))
-    info_1 = jnp.concatenate([r.astype(jnp.int32)[None], picks_all[0:2].reshape(-1), jnp.zeros((2,), jnp.int32)])
+    product_0 = mm(sigma_rows, factor_cols[0])
+    lifted = [
+        mm(sigma_rows, scatter_factor(factor_cols[node], picks_all[node - 1], slot_count, tile))[None]
+        for node in (1, 2)
+    ]
+    gathered_0 = reduce_and_gather(0, product_0[None], product_0[None], lifted)
+
+    info_1 = jnp.concatenate(
+        [r.astype(jnp.int32)[None], picks_all[0:2].reshape(-1), jnp.zeros((2,), jnp.int32), c.astype(jnp.int32)[None]]
+    )
     halves = row_count // own_tiles
     product_1, upper_half = level_products(
-        info_1, gathered_0, sigma_tiles, factor_cols[1:3], 1, tile, band, own_tiles, slot_count,
+        info_1, gathered_0, gathered_0, factor_cols[1:3], 1, tile, band, own_tiles, slot_count,
         tile, tile, halves,
     )
-    gathered_1 = reduce_and_gather(1, product_1, upper_half)
+    gathered_1 = reduce_and_gather(1, product_1, upper_half, [])
 
     info_2 = jnp.concatenate(
-        [r.astype(jnp.int32)[None], picks_all[2:nodes - 1].reshape(-1), (parents - 1).astype(jnp.int32)]
+        [r.astype(jnp.int32)[None], picks_all[2:nodes - 1].reshape(-1), (parents - 1).astype(jnp.int32),
+         c.astype(jnp.int32)[None]]
     )
     (product_2,) = level_products(
         info_2, gathered_1, gathered_0, factor_cols[3:nodes], 2, tile, band, own_tiles, slot_count,
@@ -427,7 +446,9 @@
     diag_2 = axis_reduce(diag_partial(first_2, product_2) + gram_rows, "row", row_count, True, 2)
 
     products = jnp.concatenate([product_0[None], product_1, product_2], axis=0)
-    diag_cols = jnp.concatenate([diag_col(gathered_0, c), diag_col(gathered_1, c), diag_2], axis=0)
+    diag_cols = jnp.concatenate(
+        [diag_col(gathered_0, c, tile), diag_col(gathered_1, c, tile // halves), diag_2], axis=0
+    )
     return (-products)[None], diag_cols[None]
 
 

time: 312 us -> 328 us (1.051)
  starting transfers between devices: 0.35 us -> 16.9 us
  local copies, waits for them, and re-layouts: 31.4 us -> 15 us
  blocking collectives: 0 us -> 10.6 us
  other arithmetic: 12.3 us -> 19.7 us
    ppermute x0 -> x4, starting transfers between devices: none -> 16.8 us  [body(): rounds.append(lax.ppermute(chunk_rows, ('leaf', 'row', 'col'), pairs))]
    all_gather x1 -> x0, waiting for transfers between devices: 16 us -> none  [body(): gathered = lax.all_gather(sigma_top, ('leaf', 'row', 'col'), axis=0)]
    all_gather x2, waiting for transfers between devices: 70.4 us -> 86.3 us  [reduce_and_gather(): everything = lax.all_gather(both, ('row', 'col'), axis=0)]
    all_gather x0 -> x1, blocking collectives: none -> 10.6 us  [body(): chunk_rows = lax.all_gather(sigma_top, 'col', axis=1, tiled=True)]
    another operation x3 -> x1, local copies, waits for them, and re-layouts: 10.4 us -> 0.01 us  [the longest x2 10.4 us: body(): sigma.reshape(sigma.shape[0], slot_count, tile)]
    reshape x1 -> x0, local copies, waits for them, and re-layouts: 5.78 us -> none  [body(): gathered.reshape(leaf_count * row_count, col_count, local_rows, local_cols)]
    pallas_call x1, Pallas kernels: 83.6 us -> 80 us  [factor_exchange(): pl.pallas_call(functools.partial(factor_kernel, tile=tile), out_shape=(ja...]
    select_n x0 -> x5, other arithmetic: none -> 3.37 us  [the longest x2 1.72 us: scatter_factor(): moved = jnp.where(present[:, None, None], moved, 0.0)]
  transfers between devices with their start and end apart: 4 -> 7, of which waited for: 3 -> 2; matrix products, arithmetic and copies ran while one was open for 13% -> 10% of each run, Pallas kernels for 30% -> 27%
where the time goes in v8:
time: 328 us; the launch traced here: 327 us
  Pallas kernels  148 us (45%)
  waiting for transfers between devices  86.4 us (26%)
  other arithmetic  19.7 us (6%)
  starting transfers between devices  16.9 us (5%)
  matrix products  16.3 us (5%)
  local copies, waits for them, and re-layouts  15 us (5%)
  between operations  14.2 us (4%)
  blocking collectives  10.6 us (3%)
    all_gather x2, waiting for transfers between devices, reduce_and_gather(): everything = lax.all_gather(both, ('row', 'col'), axis=0)  86.3 us
    pallas_call x1, Pallas kernels, factor_exchange(): pl.pallas_call(functools.partial(factor_kernel, tile=tile), out_shape=(ja...  80 us
    pallas_call x3, Pallas kernels, axis_reduce(): pl.pallas_call(kernel, out_shape=jax.ShapeDtypeStruct((lead, out_rows, la...  52.8 us
    ppermute x4, starting transfers between devices, body(): rounds.append(lax.ppermute(chunk_rows, ('leaf', 'row', 'col'), pairs))  16.8 us
    dot_general x8, matrix products, mm(): jnp.matmul(a, b, precision=HIGHEST, preferred_element_type=jnp.float32)  16.3 us
    pallas_call x2, Pallas kernels, level_products(): pl.pallas_call(kernel, out_shape=tuple(shapes), in_specs=[pl.BlockSpec(me...  15.7 us
    all_gather x1, blocking collectives, body(): chunk_rows = lax.all_gather(sigma_top, 'col', axis=1, tiled=True)  10.6 us
  transfers between devices with their start and end apart: 7, of which 2 were waited for; matrix products, arithmetic and copies ran while one was open for 10% of the time, Pallas kernels for 27%

profile of v8, /device:TPU:1, one launch (start us, length us, event | category | flops | bytes accessed | tf_op | source)
XLA Modules:
  0.0 327.5 jit_solution(5896232671619839010)
XLA Ops:
  7.2 10.6 %all_gather.15 = f32[32,1024]{1,0:T(8,128)S(1)} all-gather(f32[32,256]{1,0:T(8,128)} %param.7), channel_id=1, replica_groups=mesh['leaf'=4,'row'=8,'col'=4] {'col'}, dimensions={1}, use_global_device_ids=true | all-gather | bytes 163840 | tf_op jit(solution)/shard_map/all_gather | solution.py:362
  17.9 5.4 %collective-permute-start.3 = (f32[32,1024]{1,0:T(8,128)S(1)}, f32[32,1024]{1,0:T(8,128)}, u32[]{:S(2)}, u32[]{:S(2)}) collective-permute-start(f32[32,1024]{1,0:T(8,128)S(1)} %all_gather.15), channel_id=1, source_target_pairs={{0,96},{1,97},{2,98},{3,99},{4,0},{5,1},{6,2},{7,3},{8,32},{9,33},... | collective-permute-start | bytes 393224 | tf_op jit(solution)/shard_map/ppermute | solution.py:377
  23.3 6.7 %collective-permute-start.2 = (f32[32,1024]{1,0:T(8,128)S(1)}, f32[32,1024]{1,0:T(8,128)}, u32[]{:S(2)}, u32[]{:S(2)}) collective-permute-start(f32[32,1024]{1,0:T(8,128)S(1)} %all_gather.15), channel_id=1, source_target_pairs={{0,64},{1,65},{2,66},{3,67},{4,96},{5,97},{6,98},{7,99},{8,0},{9,1... | collective-permute-start | bytes 393224 | tf_op jit(solution)/shard_map/ppermute | solution.py:377
  30.1 2.7 collective-permute-start.1
  32.7 1.9 collective-permute-start
  34.7 2.3 fusion
  40.8 2.8 fusion.2.x_ref
  43.7 80.0 %shard_map.68 = (f32[7,128,512]{2,1,0:T(8,128)}, f32[7,1024,128]{2,1,0:T(8,128)}) custom-call(f32[7,128,512]{2,1,0:T(8,128)} %fusion.2.x_ref), custom_call_target="tpu_custom_call" | custom-call | tf_op jit(solution)/shard_map/pallas_call | solution.py:315
  123.7 2.6 broadcast_multiply_fusion
  126.3 1.9 copy-done.1
  138.2 2.2 convolution_bitcast_fusion.x_ref
  140.4 8.6 %shard_map.69 = f32[1,64,128]{2,1,0:T(8,128)} custom-call(f32[1,512,128]{2,1,0:T(8,128)} %convolution_bitcast_fusion.x_ref), custom_call_target="tpu_custom_call" | custom-call | tf_op jit(solution)/shard_map/pallas_call | solution.py:206
  151.9 2.3 slice.90.fac_ref
  154.9 46.0 %all-gather.5.cloned.1.call-done = f32[32,448,128]{2,1,0:T(8,128)} async-done(((f32[1,448,128]{2,1,0:T(8,128)}), f32[32,448,128]{2,1,0:T(8,128)}) %all-gather.5.cloned.1.call-update) | async-done | bytes 7340048 | tf_op jit(solution)/shard_map/all_gather | solution.py:390
  201.0 7.6 %shard_map.70 = (f32[2,128,128]{2,1,0:T(8,128)}, f32[2,64,128]{2,1,0:T(8,128)}) custom-call(s32[20]{0:T(128)} %pad_add_fusion.info_ref, f32[8,4,1,448,128]{4,3,2,1,0:T(8,128)} %bitcast.76, f32[8,4,1,448,128]{4,3,2,1,0:T(8,128)} %bitcast.77, f32[2,1024,128]{2,1,0:T(8,128)} %slice.90.fac_ref), custom_call_target="tpu_custom_call" | custom-call | tf_op jit(solution)/shard_map/pallas_call | solution.py:124
  208.5 2.9 fusion.17.x_ref
  211.4 11.8 %shard_map.71 = f32[2,64,128]{2,1,0:T(8,128)} custom-call(f32[2,512,128]{2,1,0:T(8,128)} %fusion.17.x_ref), custom_call_target="tpu_custom_call" | custom-call | tf_op jit(solution)/shard_map/pallas_call | solution.py:206
  224.8 3.1 slice.92.fac_ref
  230.6 40.3 %all-gather.7.cloned.1.call-done = f32[64,128,128]{2,1,0:T(8,128)} async-done(((f32[2,128,128]{2,1,0:T(8,128)}), f32[64,128,128]{2,1,0:T(8,128)}) %all-gather.7.cloned.1.call-update) | async-done | bytes 4194320 | tf_op jit(solution)/shard_map/all_gather | solution.py:390
  270.9 1.7 slice.94
  272.7 8.2 %shard_map.72 = f32[4,128,128]{2,1,0:T(8,128)} custom-call(s32[38]{0:T(128)} %pad_add_fusion.1.info_ref, f32[8,4,2,128,128]{4,3,2,1,0:T(8,128)} %bitcast.81, f32[8,4,1,448,128]{4,3,2,1,0:T(8,128)} %bitcast.79, f32[4,1024,128]{2,1,0:T(8,128)} %slice.92.fac_ref), custom_call_target="tpu_custom_call" | custom-call | tf_op jit(solution)/shard_map/pallas_call | solution.py:124
  280.9 3.1 fusion.18
  285.0 32.4 %shard_map.73 = f32[4,512,128]{2,1,0:T(8,128)} custom-call(f32[4,512,128]{2,1,0:T(8,128)} %copy-done.2), custom_call_target="tpu_custom_call" | custom-call | tf_op jit(solution)/shard_map/pallas_call | solution.py:206
  317.5 2.7 maximum_bitcast_fusion
  (82 shorter events, 23.6 us)
Async XLA Ops:
  7.2 27.5 %copy-start = (f32[1,7,128,512]{3,2,1,0:T(8,128)S(1)}, f32[1,7,128,512]{3,2,1,0:T(8,128)}, u32[]{:S(2)}) copy-start(f32[1,7,128,512]{3,2,1,0:T(8,128)} %param.9) | copy-start | bytes 5505028
  7.2 143.2 %reduce-scatter.2.cloned.1.call-start = ((), (), s32[]{:S(2)}) async-start(), calls=%async_computation.1 | async-start | bytes 1146880 | tf_op jit(solution)/shard_map/reduce_scatter | solution.py:358
  17.9 114.9 %collective-permute-start.3 = (f32[32,1024]{1,0:T(8,128)S(1)}, f32[32,1024]{1,0:T(8,128)}, u32[]{:S(2)}, u32[]{:S(2)}) collective-permute-start(f32[32,1024]{1,0:T(8,128)S(1)} %all_gather.15), channel_id=1, source_target_pairs={{0,96},{1,97},{2,98},{3,99},{4,0},{5,1},{6,2},{7,3},{8,32},{9,33},... | collective-permute-start | bytes 393224 | tf_op jit(solution)/shard_map/ppermute | solution.py:377
  23.3 109.5 %collective-permute-start.2 = (f32[32,1024]{1,0:T(8,128)S(1)}, f32[32,1024]{1,0:T(8,128)}, u32[]{:S(2)}, u32[]{:S(2)}) collective-permute-start(f32[32,1024]{1,0:T(8,128)S(1)} %all_gather.15), channel_id=1, source_target_pairs={{0,64},{1,65},{2,66},{3,67},{4,96},{5,97},{6,98},{7,99},{8,0},{9,1... | collective-permute-start | bytes 393224 | tf_op jit(solution)/shard_map/ppermute | solution.py:377
  30.1 102.7 %collective-permute-start.1 = (f32[32,1024]{1,0:T(8,128)S(1)}, f32[32,1024]{1,0:T(8,128)}, u32[]{:S(2)}, u32[]{:S(2)}) collective-permute-start(f32[32,1024]{1,0:T(8,128)S(1)} %all_gather.15), channel_id=1, source_target_pairs={{0,32},{1,33},{2,34},{3,35},{4,64},{5,65},{6,66},{7,67},{8,96},{9,... | collective-permute-start | bytes 393224 | tf_op jit(solution)/shard_map/ppermute | solution.py:377
  32.7 100.1 %collective-permute-start = (f32[32,1024]{1,0:T(8,128)S(1)}, f32[32,1024]{1,0:T(8,128)}, u32[]{:S(2)}, u32[]{:S(2)}) collective-permute-start(f32[32,1024]{1,0:T(8,128)S(1)} %all_gather.15), channel_id=1, source_target_pairs={{0,0},{1,1},{2,2},{3,3},{4,32},{5,33},{6,34},{7,35},{8,64},{9,65},... | collective-permute-start | bytes 393224 | tf_op jit(solution)/shard_map/ppermute | solution.py:377
  34.7 2.4 copy-start.9
  34.7 6.1 %copy-start.6 = (f32[1,7,128,128]{3,2,1,0:T(8,128)S(1)}, f32[1,7,128,128]{3,2,1,0:T(8,128)}, u32[]{:S(2)}) copy-start(f32[1,7,128,128]{3,2,1,0:T(8,128)} %param.8) | copy-start | bytes 1376260
  37.0 164.0 %all-gather.5.cloned.1.call-start = ((), (), s32[]{:S(2)}) async-start(), calls=%async_computation.2 | async-start | bytes 7569408 | tf_op jit(solution)/shard_map/all_gather | solution.py:390
  126.3 1.9 copy-start.1
  128.8 2.3 copy-start.10
  129.4 1.8 copy-start.4
  131.2 1.6 copy-start.11
  151.9 119.0 %all-gather.7.cloned.1.call-start = ((), (), s32[]{:S(2)}) async-start(), calls=%async_computation.3 | async-start | bytes 4325376 | tf_op jit(solution)/shard_map/all_gather | solution.py:390
  208.5 15.5 %copy-start.8 = (f32[2,64,128]{2,1,0:T(8,128)S(1)}, f32[2,64,128]{2,1,0:T(8,128)}, u32[]{:S(2)}) copy-start(f32[2,64,128]{2,1,0:T(8,128)} %get-tuple-element.14) | copy-start | bytes 196612
  224.8 3.2 copy-start.12
  280.9 3.1 copy-start.7
  284.0 1.0 copy-start.2
  317.5 2.7 copy-start.3
  317.5 2.7 copy-start.5
Sparse Core Ops, SparseCore 0:
  37.1 35.8 reduce-scatter.1
  152.0 48.9 all-gather.4
  224.9 45.9 all-gather.6

commit v9 on v6

--- a/solution.py
+++ b/solution.py
@@ -48,6 +48,7 @@
     count = out_ref.shape[0]
     split = tile // band
     r = info_ref[0]
+    col = info_ref[1 + count * slot_count + count]
     own = lax.rem(r, own_tiles)
 
     def p_tile(ref, prow, node, q, m):
@@ -90,12 +91,10 @@
         def _():
             if level == 1:
                 s = jnp.clip(source, 0, slot_count - 1)
-                start = pl.multiple_of(s * tile, tile)
-                acc = -dot_hi(p_tile(par_ref, par_prow, parent, s, 0), factor[0])
-                for k in range(1, own_tiles):
+                lifted = tile + band + i * tile
+                acc = par_ref[s, col, parent, lifted:lifted + tile, :]
+                for k in range(own_tiles):
                     acc -= dot_hi(p_tile(par_ref, par_prow, parent, s, k), factor[k])
-                for k in range(own_tiles, slot_count):
-                    acc += dot_hi(low_ref[picks[k], pl.ds(start, tile), :], factor[k])
             else:
                 s = jnp.clip(source, 0, own_tiles - 1)
                 acc = -dot_hi(p_tile(par_ref, par_prow, parent, s, 0), factor[0])
@@ -250,24 +249,38 @@
     partial_gram = mm(jnp.transpose(inverse_band, (0, 2, 1)), inverse)
     gram_piece = lax.psum_scatter(partial_gram, "col", scatter_dimension=2, tiled=True)
 
-    local_rows, local_cols = sigma_top.shape
-    gathered = lax.all_gather(sigma_top, ("leaf", "row", "col"), axis=0)
-    sigma = gathered.reshape(leaf_count * row_count, col_count, local_rows, local_cols)
-    sigma = jnp.transpose(sigma, (0, 2, 1, 3)).reshape(
-        leaf_count * row_count * local_rows, col_count * local_cols
-    )
+    leaf = lax.axis_index("leaf")
+    local_rows = sigma_top.shape[0]
+    chunk_rows = lax.all_gather(sigma_top, "col", axis=1, tiled=True)
+    chunks_per_tile = tile // local_rows
+    rounds = []
+    for t in range(chunks_per_tile):
+        pairs = []
+        for src_leaf in range(leaf_count):
+            for src_row in range(row_count):
+                q = src_leaf * row_count + src_row
+                dst_leaf = (q % chunks_per_tile + t) % leaf_count
+                dst_row = q // chunks_per_tile
+                for col in range(col_count):
+                    pairs.append(
+                        ((src_leaf * row_count + src_row) * col_count + col,
+                         (dst_leaf * row_count + dst_row) * col_count + col)
+                    )
+        rounds.append(lax.ppermute(chunk_rows, ("leaf", "row", "col"), pairs))
+    order = lax.rem(leaf - jnp.arange(chunks_per_tile, dtype=jnp.int32) + 4 * leaf_count, leaf_count)
+    sigma_rows = jnp.take(jnp.stack(rounds), order, axis=0).reshape(tile, -1)
 
     def diag_partial(first, products):
         rows = factor_rows[first:first + products.shape[0]]
         return mm(jnp.transpose(rows, (0, 2, 1)), products)
 
-    def reduce_and_gather(first, products, sent):
+    def reduce_and_gather(first, products, sent, extra):
         count = products.shape[0]
         piece = axis_reduce(diag_partial(first, products), "row", row_count, False, first)
         piece = piece + gram_piece[first:first + count]
-        both = jnp.concatenate([sent, piece], axis=1)
+        both = jnp.concatenate([sent, piece] + extra, axis=1)
         everything = lax.all_gather(both, ("row", "col"), axis=0)
-        return everything.reshape(row_count, col_count, count, sent.shape[1] + band, tile)
+        return everything.reshape(row_count, col_count, count, both.shape[1], tile)
 
     bands_per_tile = tile // band
 
@@ -286,27 +299,33 @@
         pieces = lax.dynamic_index_in_dim(pieces, node, 2, keepdims=False)
         return jnp.transpose(pieces, (0, 2, 1, 3)).reshape(tile, -1)
 
-    def diag_col(gathered, m):
-        pieces = lax.dynamic_index_in_dim(gathered[:, :, :, -band:], m, 1, keepdims=False)
+    def diag_col(gathered, m, offset):
+        pieces = lax.dynamic_index_in_dim(gathered[:, :, :, offset:offset + band], m, 1, keepdims=False)
         return jnp.transpose(pieces, (1, 0, 2, 3)).reshape(pieces.shape[1], -1, tile)
 
     own_row = jnp.minimum(r, own_tiles - 1)
     upper = r < own_tiles
 
-    product_0 = mm(tile_rows(sigma, r, tile), factor_cols[0])
-    gathered_0 = reduce_and_gather(0, product_0[None], product_0[None])
-
-    sigma_tiles = jnp.transpose(sigma.reshape(sigma.shape[0], slot_count, tile), (1, 0, 2))
-    info_1 = jnp.concatenate([r.astype(jnp.int32)[None], picks_all[0:2].reshape(-1), jnp.zeros((2,), jnp.int32)])
+    product_0 = mm(sigma_rows, factor_cols[0])
+    lifted = [
+        mm(sigma_rows, scatter_factor(factor_cols[node], picks_all[node - 1], slot_count, tile))[None]
+        for node in (1, 2)
+    ]
+    gathered_0 = reduce_and_gather(0, product_0[None], product_0[None], lifted)
+
+    info_1 = jnp.concatenate(
+        [r.astype(jnp.int32)[None], picks_all[0:2].reshape(-1), jnp.zeros((2,), jnp.int32), c.astype(jnp.int32)[None]]
+    )
     halves = row_count // own_tiles
     product_1, upper_half = level_products(
-        info_1, gathered_0, sigma_tiles, factor_cols[1:3], 1, tile, band, own_tiles, slot_count,
+        info_1, gathered_0, gathered_0, factor_cols[1:3], 1, tile, band, own_tiles, slot_count,
         tile, tile, halves,
     )
-    gathered_1 = reduce_and_gather(1, product_1, upper_half)
+    gathered_1 = reduce_and_gather(1, product_1, upper_half, [])
 
     info_2 = jnp.concatenate(
-        [r.astype(jnp.int32)[None], picks_all[2:nodes - 1].reshape(-1), (parents - 1).astype(jnp.int32)]
+        [r.astype(jnp.int32)[None], picks_all[2:nodes - 1].reshape(-1), (parents - 1).astype(jnp.int32),
+         c.astype(jnp.int32)[None]]
     )
     (product_2,) = level_products(
         info_2, gathered_1, gathered_0, factor_cols[3:nodes], 2, tile, band, own_tiles, slot_count,
@@ -319,7 +338,9 @@
     diag_2 = axis_reduce(diag_partial(first_2, product_2) + gram_rows, "row", row_count, True, 2)
 
     products = jnp.concatenate([product_0[None], product_1, product_2], axis=0)
-    diag_cols = jnp.concatenate([diag_col(gathered_0, c), diag_col(gathered_1, c), diag_2], axis=0)
+    diag_cols = jnp.concatenate(
+        [diag_col(gathered_0, c, tile), diag_col(gathered_1, c, tile // halves), diag_2], axis=0
+    )
     return (-products)[None], diag_cols[None]
 
 

time: 309 us -> 305 us (0.987)
  waiting for transfers between devices: 115 us -> 94.8 us
  local copies, waits for them, and re-layouts: 36.3 us -> 17.7 us
  starting transfers between devices: 0.39 us -> 18.5 us
  blocking collectives: 0 us -> 9.78 us
  other arithmetic: 8.43 us -> 12.7 us
    all_gather x1 -> x0, waiting for transfers between devices: 21.8 us -> none  [body(): gathered = lax.all_gather(sigma_top, ('leaf', 'row', 'col'), axis=0)]
    ppermute x0 -> x4, starting transfers between devices: none -> 18.3 us  [body(): rounds.append(lax.ppermute(chunk_rows, ('leaf', 'row', 'col'), pairs))]
    all_gather x1, waiting for transfers between devices: 19.4 us -> 2.63 us  [body(): factor_cols = lax.all_gather(factor_tile, 'row', axis=1, tiled=True)]
    all_gather x2, waiting for transfers between devices: 72.7 us -> 88.8 us  [reduce_and_gather(): everything = lax.all_gather(both, ('row', 'col'), axis=0)]
    another operation x3 -> x1, local copies, waits for them, and re-layouts: 10.5 us -> 0.01 us  [the longest x2 10.5 us: body(): sigma.reshape(sigma.shape[0], slot_count, tile)]
    all_gather x0 -> x1, blocking collectives: none -> 9.78 us  [body(): chunk_rows = lax.all_gather(sigma_top, 'col', axis=1, tiled=True)]
    reshape x1 -> x0, local copies, waits for them, and re-layouts: 5.82 us -> none  [body(): gathered.reshape(leaf_count * row_count, col_count, local_rows, local_cols)]
    unnamed x23 -> x22, local copies, waits for them, and re-layouts: 7.84 us -> 2.61 us
  transfers between devices with their start and end apart: 5 -> 8, of which waited for: 4 -> 5; matrix products, arithmetic and copies ran while one was open for 13% -> 8% of each run, Pallas kernels for 19% -> 3%
where the time goes in v9:
time: 305 us; the launch traced here: 304 us
  Pallas kernels  118 us (39%)
  waiting for transfers between devices  94.8 us (31%)
  starting transfers between devices  18.5 us (6%)
  local copies, waits for them, and re-layouts  17.7 us (6%)
  matrix products  17.3 us (6%)
  between operations  16 us (5%)
  other arithmetic  12.7 us (4%)
  blocking collectives  9.78 us (3%)
    pallas_call x4, Pallas kernels, axis_reduce(): pl.pallas_call(kernel, out_shape=jax.ShapeDtypeStruct((lead, out_rows, la...  102 us
    all_gather x2, waiting for transfers between devices, reduce_and_gather(): everything = lax.all_gather(both, ('row', 'col'), axis=0)  88.8 us
    ppermute x4, starting transfers between devices, body(): rounds.append(lax.ppermute(chunk_rows, ('leaf', 'row', 'col'), pairs))  18.3 us
    dot_general x8, matrix products, mm(): jnp.matmul(a, b, precision=HIGHEST, preferred_element_type=jnp.float32)  17.3 us
    pallas_call x2, Pallas kernels, level_products(): pl.pallas_call(kernel, out_shape=tuple(shapes), in_specs=[pl.BlockSpec(me...  15.7 us
    all_gather x1, blocking collectives, body(): chunk_rows = lax.all_gather(sigma_top, 'col', axis=1, tiled=True)  9.78 us
  transfers between devices with their start and end apart: 8, of which 5 were waited for; matrix products, arithmetic and copies ran while one was open for 8% of the time, Pallas kernels for 3%

profile of v9, /device:TPU:1, one launch (start us, length us, event | category | flops | bytes accessed | tf_op | source)
XLA Modules:
  0.0 304.4 jit_solution(8572690058455674434)
XLA Ops:
  9.5 3.9 %fusion.2.x_ref = f32[7,128,512]{2,1,0:T(8,128)} fusion(f32[1,7,128,512]{3,2,1,0:T(8,128)S(1)} %copy-done, f32[1,7,128,128]{3,2,1,0:T(8,128)} %param.8), kind=kOutput, calls=%fused_computation.6 | convolution fusion | flops 704643072 | bytes 4128768 | tf_op jit(solution)/shard_map/dot_general | solution.py:15
  13.4 48.4 %shard_map.68 = f32[7,128,512]{2,1,0:T(8,128)} custom-call(f32[7,128,512]{2,1,0:T(8,128)} %fusion.2.x_ref), custom_call_target="tpu_custom_call" | custom-call | tf_op jit(solution)/shard_map/pallas_call | solution.py:206
  61.8 1.8 broadcast_multiply_fusion
  65.8 9.8 %all_gather.18 = f32[32,1024]{1,0:T(8,128)S(1)} all-gather(f32[32,256]{1,0:T(8,128)S(1)} %copy-done.8), channel_id=1, replica_groups=mesh['leaf'=4,'row'=8,'col'=4] {'col'}, dimensions={1}, use_global_device_ids=true | all-gather | bytes 163840 | tf_op jit(solution)/shard_map/all_gather | solution.py:254
  75.6 7.0 %collective-permute-start.3 = (f32[32,1024]{1,0:T(8,128)S(1)}, f32[32,1024]{1,0:T(8,128)S(1)}, u32[]{:S(2)}, u32[]{:S(2)}) collective-permute-start(f32[32,1024]{1,0:T(8,128)S(1)} %all_gather.18), channel_id=1, source_target_pairs={{0,96},{1,97},{2,98},{3,99},{4,0},{5,1},{6,2},{7,3},{8,32},{9,33},... | collective-permute-start | bytes 393224 | tf_op jit(solution)/shard_map/ppermute | solution.py:269
  82.6 6.7 %collective-permute-start.2 = (f32[32,1024]{1,0:T(8,128)S(1)}, f32[32,1024]{1,0:T(8,128)S(1)}, u32[]{:S(2)}, u32[]{:S(2)}) collective-permute-start(f32[32,1024]{1,0:T(8,128)S(1)} %all_gather.18), channel_id=1, source_target_pairs={{0,64},{1,65},{2,66},{3,67},{4,96},{5,97},{6,98},{7,99},{8,0},{9,1... | collective-permute-start | bytes 393224 | tf_op jit(solution)/shard_map/ppermute | solution.py:269
  89.3 2.7 collective-permute-start.1
  92.0 1.9 collective-permute-start
  93.9 2.2 fusion
  101.8 2.6 all-gather.6.cloned.1.call-done
  106.1 2.2 convolution_bitcast_fusion.x_ref
  108.4 9.1 %shard_map.69 = f32[1,64,128]{2,1,0:T(8,128)} custom-call(f32[1,512,128]{2,1,0:T(8,128)} %convolution_bitcast_fusion.x_ref), custom_call_target="tpu_custom_call" | custom-call | tf_op jit(solution)/shard_map/pallas_call | solution.py:206
  117.5 2.1 fusion.15
  125.7 2.3 slice.90.fac_ref
  127.9 49.0 %all-gather.8.cloned.1.call-done = f32[32,448,128]{2,1,0:T(8,128)} async-done(((f32[1,448,128]{2,1,0:T(8,128)}), f32[32,448,128]{2,1,0:T(8,128)}) %all-gather.8.cloned.1.call-update) | async-done | bytes 7340048 | tf_op jit(solution)/shard_map/all_gather | solution.py:282
  176.9 7.6 %shard_map.70 = (f32[2,128,128]{2,1,0:T(8,128)}, f32[2,64,128]{2,1,0:T(8,128)}) custom-call(s32[20]{0:T(128)} %pad_add_fusion.info_ref, f32[8,4,1,448,128]{4,3,2,1,0:T(8,128)} %bitcast.69, f32[8,4,1,448,128]{4,3,2,1,0:T(8,128)} %bitcast.70, f32[2,1024,128]{2,1,0:T(8,128)} %slice.90.fac_ref), custom_call_target="tpu_custom_call" | custom-call | tf_op jit(solution)/shard_map/pallas_call | solution.py:124
  184.5 2.9 fusion.16.x_ref
  187.3 12.0 %shard_map.71 = f32[2,64,128]{2,1,0:T(8,128)} custom-call(f32[2,512,128]{2,1,0:T(8,128)} %fusion.16.x_ref), custom_call_target="tpu_custom_call" | custom-call | tf_op jit(solution)/shard_map/pallas_call | solution.py:206
  201.7 3.0 %slice.92.fac_ref = f32[4,1024,128]{2,1,0:T(8,128)} slice(f32[7,1024,128]{2,1,0:T(8,128)} %all-gather.6.cloned.1.call-done), slice={[3:7], [0:1024], [0:128]} | slice | bytes 4194304 | tf_op jit(solution)/shard_map/slice | solution.py:331
  206.8 39.8 %all-gather.10.cloned.1.call-done = f32[64,128,128]{2,1,0:T(8,128)} async-done(((f32[2,128,128]{2,1,0:T(8,128)}), f32[64,128,128]{2,1,0:T(8,128)}) %all-gather.10.cloned.1.call-update) | async-done | bytes 4194320 | tf_op jit(solution)/shard_map/all_gather | solution.py:282
  248.4 8.2 %shard_map.72 = f32[4,128,128]{2,1,0:T(8,128)} custom-call(s32[38]{0:T(128)} %pad_add_fusion.1.info_ref, f32[8,4,2,128,128]{4,3,2,1,0:T(8,128)} %bitcast.74, f32[8,4,1,448,128]{4,3,2,1,0:T(8,128)} %bitcast.72, f32[4,1024,128]{2,1,0:T(8,128)} %slice.92.fac_ref), custom_call_target="tpu_custom_call" | custom-call | tf_op jit(solution)/shard_map/pallas_call | solution.py:124
  256.6 3.1 %fusion.17 = f32[4,512,128]{2,1,0:T(8,128)S(1)} fusion(f32[7,128,512]{2,1,0:T(8,128)} %copy-done.1, f32[4,128,128]{2,1,0:T(8,128)} %shard_map.72), kind=kOutput, calls=%fused_computation.67 | convolution fusion | flops 402653184 | bytes 3145728 | tf_op jit(solution)/shard_map/dot_general | solution.py:15
  260.7 32.5 %shard_map.73 = f32[4,512,128]{2,1,0:T(8,128)} custom-call(f32[4,512,128]{2,1,0:T(8,128)} %copy-done.2), custom_call_target="tpu_custom_call" | custom-call | tf_op jit(solution)/shard_map/pallas_call | solution.py:206
  293.3 2.7 maximum_bitcast_fusion
  (78 shorter events, 25.0 us)
Async XLA Ops:
  8.0 1.5 copy-start
  8.0 96.4 %all-gather.6.cloned.1.call-start = ((), (), s32[]{:S(2)}) async-start(), calls=%async_computation.1 | async-start | bytes 4128768 | tf_op jit(solution)/shard_map/all_gather | solution.py:246
  61.8 3.9 %copy-start.8 = (f32[32,256]{1,0:T(8,128)S(1)}, f32[32,256]{1,0:T(8,128)}, u32[]{:S(2)}) copy-start(f32[32,256]{1,0:T(8,128)} %param.7) | copy-start | bytes 98308
  63.6 1.2 copy-start.1
  65.7 57.6 %reduce-scatter.2.cloned.1.call-start = ((), (), s32[]{:S(2)}) async-start(), calls=%async_computation.2 | async-start | bytes 1146880 | tf_op jit(solution)/shard_map/reduce_scatter | solution.py:250
  75.6 22.2 %collective-permute-start.3 = (f32[32,1024]{1,0:T(8,128)S(1)}, f32[32,1024]{1,0:T(8,128)S(1)}, u32[]{:S(2)}, u32[]{:S(2)}) collective-permute-start(f32[32,1024]{1,0:T(8,128)S(1)} %all_gather.18), channel_id=1, source_target_pairs={{0,96},{1,97},{2,98},{3,99},{4,0},{5,1},{6,2},{7,3},{8,32},{9,33},... | collective-permute-start | bytes 393224 | tf_op jit(solution)/shard_map/ppermute | solution.py:269
  82.6 15.2 %collective-permute-start.2 = (f32[32,1024]{1,0:T(8,128)S(1)}, f32[32,1024]{1,0:T(8,128)S(1)}, u32[]{:S(2)}, u32[]{:S(2)}) collective-permute-start(f32[32,1024]{1,0:T(8,128)S(1)} %all_gather.18), channel_id=1, source_target_pairs={{0,64},{1,65},{2,66},{3,67},{4,96},{5,97},{6,98},{7,99},{8,0},{9,1... | collective-permute-start | bytes 393224 | tf_op jit(solution)/shard_map/ppermute | solution.py:269
  89.3 10.2 %collective-permute-start.1 = (f32[32,1024]{1,0:T(8,128)S(1)}, f32[32,1024]{1,0:T(8,128)S(1)}, u32[]{:S(2)}, u32[]{:S(2)}) collective-permute-start(f32[32,1024]{1,0:T(8,128)S(1)} %all_gather.18), channel_id=1, source_target_pairs={{0,32},{1,33},{2,34},{3,35},{4,64},{5,65},{6,66},{7,67},{8,96},{9,... | collective-permute-start | bytes 393224 | tf_op jit(solution)/shard_map/ppermute | solution.py:269
  92.0 9.1 %collective-permute-start = (f32[32,1024]{1,0:T(8,128)S(1)}, f32[32,1024]{1,0:T(8,128)S(1)}, u32[]{:S(2)}, u32[]{:S(2)}) collective-permute-start(f32[32,1024]{1,0:T(8,128)S(1)} %all_gather.18), channel_id=1, source_target_pairs={{0,0},{1,1},{2,2},{3,3},{4,32},{5,33},{6,34},{7,35},{8,64},{9,65},... | collective-permute-start | bytes 393224 | tf_op jit(solution)/shard_map/ppermute | solution.py:269
  93.9 2.3 copy-start.9
  96.2 80.7 %all-gather.8.cloned.1.call-start = ((), (), s32[]{:S(2)}) async-start(), calls=%async_computation.3 | async-start | bytes 7569408 | tf_op jit(solution)/shard_map/all_gather | solution.py:282
  121.9 1.5 copy-start.6
  124.9 121.8 %all-gather.10.cloned.1.call-start = ((), (), s32[]{:S(2)}) async-start(), calls=%async_computation.4 | async-start | bytes 4325376 | tf_op jit(solution)/shard_map/all_gather | solution.py:282
  184.5 15.8 %copy-start.7 = (f32[2,64,128]{2,1,0:T(8,128)S(1)}, f32[2,64,128]{2,1,0:T(8,128)}, u32[]{:S(2)}) copy-start(f32[2,64,128]{2,1,0:T(8,128)} %get-tuple-element.10) | copy-start | bytes 196612
  184.5 16.6 %copy-start.10 = (s32[1,4]{1,0:T(1,128)S(1)}, s32[1,4]{1,0:T(1,128)}, u32[]{:S(2)}) copy-start(s32[1,4]{1,0:T(1,128)} %param.11) | copy-start | bytes 52
  256.6 3.1 %copy-start.5 = (f32[7,64,128]{2,1,0:T(8,128)S(1)}, f32[7,64,128]{2,1,0:T(8,128)}, u32[]{:S(2)}) copy-start(f32[7,64,128]{2,1,0:T(8,128)} %reduce-scatter.2.cloned.1.call-done) | copy-start | bytes 688132
  259.8 1.0 copy-start.2
  293.3 2.7 copy-start.3
  293.3 2.7 copy-start.4
Sparse Core Ops, SparseCore 0:
  65.8 38.5 all-gather.5
Sparse Core Ops, SparseCore 1:
  96.3 22.2 reduce-scatter.1
  124.9 51.9 all-gather.7
  201.0 45.6 all-gather.9

commit v10 on v9

--- a/solution.py
+++ b/solution.py
@@ -237,13 +237,13 @@
     positions = slot_count + own_tiles
     band = width // row_count
 
-    partial_factor = mm(panel, inverse)
-    factor_rows = axis_reduce(partial_factor, "col", col_count, True, 3)
+    partial_t = jnp.einsum("vkj,vrk->vjr", inverse, panel, precision=HIGHEST, preferred_element_type=jnp.float32)
+    factor_t = axis_reduce(partial_t, "col", col_count, False, 3)
     living = jnp.concatenate([jnp.ones((1, slot_count), jnp.bool_), picks_all >= 0], axis=0)
     live_here = jnp.take(living, r, axis=1).astype(jnp.float32)
-    factor_rows = factor_rows * live_here[:, None, None]
-    factor_tile = lax.dynamic_slice_in_dim(factor_rows, c * tile, tile, 2)
+    factor_tile = jnp.transpose(factor_t, (0, 2, 1)) * live_here[:, None, None]
     factor_cols = lax.all_gather(factor_tile, "row", axis=1, tiled=True)
+    factor_rows = lax.all_gather(factor_tile, "col", axis=2, tiled=True)
 
     inverse_band = lax.dynamic_slice_in_dim(inverse, r * band, band, 2)
     partial_gram = mm(jnp.transpose(inverse_band, (0, 2, 1)), inverse)

time: 305 us -> 325 us (1.066)
  waiting for transfers between devices: 94.8 us -> 138 us
  Pallas kernels: 118 us -> 97.9 us
    all_gather x0 -> x1, waiting for transfers between devices: none -> 32.2 us  [body(): factor_rows = lax.all_gather(factor_tile, 'col', axis=2, tiled=True)]
    pallas_call x4, Pallas kernels: 102 us -> 82.1 us  [axis_reduce(): pl.pallas_call(kernel, out_shape=jax.ShapeDtypeStruct((lead, out_rows, la...]
    reduce_scatter x1, waiting for transfers between devices: 0.03 us -> 7.08 us  [body(): lax.psum_scatter(partial_gram, 'col', scatter_dimension=2, tiled=True)]
    dot_general x0 -> x1, matrix products: none -> 5.26 us  [body(): jnp.einsum('vkj,vrk->vjr', inverse, panel, precision=HIGHEST, preferred_e...]
    dot_general x8 -> x7, matrix products: 17.3 us -> 13.4 us  [mm(): jnp.matmul(a, b, precision=HIGHEST, preferred_element_type=jnp.float32)]
  transfers between devices with their start and end apart: 8 -> 9, of which waited for: 5 -> 7; matrix products, arithmetic and copies ran while one was open for 8% -> 7% of each run, Pallas kernels for 3% -> 3%
where the time goes in v10:
time: 325 us; the launch traced here: 324 us
  waiting for transfers between devices  138 us (42%)
  Pallas kernels  97.9 us (30%)
  matrix products  18.7 us (6%)
  starting transfers between devices  17.3 us (5%)
  local copies, waits for them, and re-layouts  17 us (5%)
  between operations  14.1 us (4%)
  other arithmetic  11.7 us (4%)
  blocking collectives  9.65 us (3%)
    all_gather x2, waiting for transfers between devices, reduce_and_gather(): everything = lax.all_gather(both, ('row', 'col'), axis=0)  91 us
    pallas_call x4, Pallas kernels, axis_reduce(): pl.pallas_call(kernel, out_shape=jax.ShapeDtypeStruct((lead, out_rows, la...  82.1 us
    all_gather x1, waiting for transfers between devices, body(): factor_rows = lax.all_gather(factor_tile, 'col', axis=2, tiled=True)  32.2 us
    ppermute x4, starting transfers between devices, body(): rounds.append(lax.ppermute(chunk_rows, ('leaf', 'row', 'col'), pairs))  17.1 us
    pallas_call x2, Pallas kernels, level_products(): pl.pallas_call(kernel, out_shape=tuple(shapes), in_specs=[pl.BlockSpec(me...  15.7 us
    dot_general x7, matrix products, mm(): jnp.matmul(a, b, precision=HIGHEST, preferred_element_type=jnp.float32)  13.4 us
    all_gather x1, blocking collectives, body(): chunk_rows = lax.all_gather(sigma_top, 'col', axis=1, tiled=True)  9.65 us
    reduce_scatter x1, waiting for transfers between devices, body(): lax.psum_scatter(partial_gram, 'col', scatter_dimension=2, tiled=True)  7.08 us
  transfers between devices with their start and end apart: 9, of which 7 were waited for; matrix products, arithmetic and copies ran while one was open for 7% of the time, Pallas kernels for 3%

profile of v10, /device:TPU:1, one launch (start us, length us, event | category | flops | bytes accessed | tf_op | source)
XLA Modules:
  0.0 323.9 jit_solution(13435516389114843716)
XLA Ops:
  8.7 5.3 %fusion.2.x_ref = f32[7,512,128]{2,1,0:T(8,128)} fusion(f32[1,7,128,512]{3,2,1,0:T(8,128)S(1)} %copy-done, f32[1,7,128,128]{3,2,1,0:T(8,128)} %param.8), kind=kOutput, calls=%fused_computation.6 | convolution fusion | flops 704643072 | bytes 4128768 | tf_op jit(solution)/shard_map/vkj,vrk->vjr/dot_general | solution.py:240
  13.9 26.7 %shard_map.68 = f32[7,128,128]{2,1,0:T(8,128)} custom-call(f32[7,512,128]{2,1,0:T(8,128)} %fusion.2.x_ref), custom_call_target="tpu_custom_call" | custom-call | tf_op jit(solution)/shard_map/pallas_call | solution.py:206
  43.7 9.6 %all_gather.21 = f32[32,1024]{1,0:T(8,128)S(1)} all-gather(f32[32,256]{1,0:T(8,128)S(1)} %copy-done.7), channel_id=1, replica_groups=mesh['leaf'=4,'row'=8,'col'=4] {'col'}, dimensions={1}, use_global_device_ids=true | all-gather | bytes 163840 | tf_op jit(solution)/shard_map/all_gather | solution.py:254
  53.3 5.8 %collective-permute-start.3 = (f32[32,1024]{1,0:T(8,128)S(1)}, f32[32,1024]{1,0:T(8,128)S(1)}, u32[]{:S(2)}, u32[]{:S(2)}) collective-permute-start(f32[32,1024]{1,0:T(8,128)S(1)} %all_gather.21), channel_id=1, source_target_pairs={{0,96},{1,97},{2,98},{3,99},{4,0},{5,1},{6,2},{7,3},{8,32},{9,33},... | collective-permute-start | bytes 393224 | tf_op jit(solution)/shard_map/ppermute | solution.py:269
  59.1 6.7 %collective-permute-start.2 = (f32[32,1024]{1,0:T(8,128)S(1)}, f32[32,1024]{1,0:T(8,128)S(1)}, u32[]{:S(2)}, u32[]{:S(2)}) collective-permute-start(f32[32,1024]{1,0:T(8,128)S(1)} %all_gather.21), channel_id=1, source_target_pairs={{0,64},{1,65},{2,66},{3,67},{4,96},{5,97},{6,98},{7,99},{8,0},{9,1... | collective-permute-start | bytes 393224 | tf_op jit(solution)/shard_map/ppermute | solution.py:269
  65.9 2.7 collective-permute-start.1
  70.5 2.2 fusion
  76.0 2.6 collective-permute-done
  79.4 2.4 all-gather.7.cloned.1.call-done
  83.5 32.2 %all-gather.9.cloned.1.call-done = f32[7,128,512]{2,1,0:T(8,128)} async-done(((f32[7,128,128]{2,1,0:T(8,128)}), f32[7,128,512]{2,1,0:T(8,128)}) %all-gather.9.cloned.1.call-update) | async-done | bytes 1835024 | tf_op jit(solution)/shard_map/all_gather | solution.py:246
  115.6 2.2 convolution_bitcast_fusion.x_ref
  117.9 10.9 %shard_map.69 = f32[1,64,128]{2,1,0:T(8,128)} custom-call(f32[1,512,128]{2,1,0:T(8,128)} %convolution_bitcast_fusion.x_ref), custom_call_target="tpu_custom_call" | custom-call | tf_op jit(solution)/shard_map/pallas_call | solution.py:206
  134.7 7.1 %reduce-scatter.2.cloned.1.call-done = f32[7,64,128]{2,1,0:T(8,128)} async-done(((f32[7,64,512]{2,1,0:T(8,128)}), f32[7,64,128]{2,1,0:T(8,128)}) %reduce-scatter.2.cloned.1.call-update) | async-done | bytes 229392 | tf_op jit(solution)/shard_map/reduce_scatter | solution.py:250
  144.1 2.3 slice.90.fac_ref
  146.4 51.0 %all-gather.11.cloned.1.call-done = f32[32,448,128]{2,1,0:T(8,128)} async-done(((f32[1,448,128]{2,1,0:T(8,128)}), f32[32,448,128]{2,1,0:T(8,128)}) %all-gather.11.cloned.1.call-update) | async-done | bytes 7340048 | tf_op jit(solution)/shard_map/all_gather | solution.py:282
  197.4 7.6 %shard_map.70 = (f32[2,128,128]{2,1,0:T(8,128)}, f32[2,64,128]{2,1,0:T(8,128)}) custom-call(s32[20]{0:T(128)} %pad_add_fusion.info_ref, f32[8,4,1,448,128]{4,3,2,1,0:T(8,128)} %bitcast.71, f32[8,4,1,448,128]{4,3,2,1,0:T(8,128)} %bitcast.72, f32[2,1024,128]{2,1,0:T(8,128)} %slice.90.fac_ref), custom_call_target="tpu_custom_call" | custom-call | tf_op jit(solution)/shard_map/pallas_call | solution.py:124
  204.9 2.9 fusion.16.x_ref
  207.8 12.1 %shard_map.71 = f32[2,64,128]{2,1,0:T(8,128)} custom-call(f32[2,512,128]{2,1,0:T(8,128)} %fusion.16.x_ref), custom_call_target="tpu_custom_call" | custom-call | tf_op jit(solution)/shard_map/pallas_call | solution.py:206
  222.2 3.0 slice.92.fac_ref
  227.3 40.0 %all-gather.13.cloned.1.call-done = f32[64,128,128]{2,1,0:T(8,128)} async-done(((f32[2,128,128]{2,1,0:T(8,128)}), f32[64,128,128]{2,1,0:T(8,128)}) %all-gather.13.cloned.1.call-update) | async-done | bytes 4194320 | tf_op jit(solution)/shard_map/all_gather | solution.py:282
  269.1 8.2 %shard_map.72 = f32[4,128,128]{2,1,0:T(8,128)} custom-call(s32[38]{0:T(128)} %pad_add_fusion.1.info_ref, f32[8,4,2,128,128]{4,3,2,1,0:T(8,128)} %bitcast.76, f32[8,4,1,448,128]{4,3,2,1,0:T(8,128)} %bitcast.74, f32[4,1024,128]{2,1,0:T(8,128)} %slice.92.fac_ref), custom_call_target="tpu_custom_call" | custom-call | tf_op jit(solution)/shard_map/pallas_call | solution.py:124
  277.3 3.1 fusion.17
  281.4 32.4 %shard_map.73 = f32[4,512,128]{2,1,0:T(8,128)} custom-call(f32[4,512,128]{2,1,0:T(8,128)} %copy-done.1), custom_call_target="tpu_custom_call" | custom-call | tf_op jit(solution)/shard_map/pallas_call | solution.py:206
  313.9 2.7 maximum_bitcast_fusion
  (79 shorter events, 28.2 us)
Async XLA Ops:
  7.2 1.5 copy-start
  7.2 74.6 %all-gather.7.cloned.1.call-start = ((), (), s32[]{:S(2)}) async-start(), calls=%async_computation.1 | async-start | bytes 4128768 | tf_op jit(solution)/shard_map/all_gather | solution.py:245
  40.7 3.0 copy-start.7
  42.9 72.8 %all-gather.9.cloned.1.call-start = ((), (), s32[]{:S(2)}) async-start(), calls=%async_computation.2 | async-start | bytes 2293760 | tf_op jit(solution)/shard_map/all_gather | solution.py:246
  43.6 98.2 %reduce-scatter.2.cloned.1.call-start = ((), (), s32[]{:S(2)}) async-start(), calls=%async_computation.3 | async-start | bytes 1146880 | tf_op jit(solution)/shard_map/reduce_scatter | solution.py:250
  53.3 21.0 %collective-permute-start.3 = (f32[32,1024]{1,0:T(8,128)S(1)}, f32[32,1024]{1,0:T(8,128)S(1)}, u32[]{:S(2)}, u32[]{:S(2)}) collective-permute-start(f32[32,1024]{1,0:T(8,128)S(1)} %all_gather.21), channel_id=1, source_target_pairs={{0,96},{1,97},{2,98},{3,99},{4,0},{5,1},{6,2},{7,3},{8,32},{9,33},... | collective-permute-start | bytes 393224 | tf_op jit(solution)/shard_map/ppermute | solution.py:269
  59.1 15.2 %collective-permute-start.2 = (f32[32,1024]{1,0:T(8,128)S(1)}, f32[32,1024]{1,0:T(8,128)S(1)}, u32[]{:S(2)}, u32[]{:S(2)}) collective-permute-start(f32[32,1024]{1,0:T(8,128)S(1)} %all_gather.21), channel_id=1, source_target_pairs={{0,64},{1,65},{2,66},{3,67},{4,96},{5,97},{6,98},{7,99},{8,0},{9,1... | collective-permute-start | bytes 393224 | tf_op jit(solution)/shard_map/ppermute | solution.py:269
  65.9 10.2 %collective-permute-start.1 = (f32[32,1024]{1,0:T(8,128)S(1)}, f32[32,1024]{1,0:T(8,128)S(1)}, u32[]{:S(2)}, u32[]{:S(2)}) collective-permute-start(f32[32,1024]{1,0:T(8,128)S(1)} %all_gather.21), channel_id=1, source_target_pairs={{0,32},{1,33},{2,34},{3,35},{4,64},{5,65},{6,66},{7,67},{8,96},{9,... | collective-permute-start | bytes 393224 | tf_op jit(solution)/shard_map/ppermute | solution.py:269
  68.5 10.1 %collective-permute-start = (f32[32,1024]{1,0:T(8,128)S(1)}, f32[32,1024]{1,0:T(8,128)S(1)}, u32[]{:S(2)}, u32[]{:S(2)}) collective-permute-start(f32[32,1024]{1,0:T(8,128)S(1)} %all_gather.21), channel_id=1, source_target_pairs={{0,0},{1,1},{2,2},{3,3},{4,32},{5,33},{6,34},{7,35},{8,64},{9,65},... | collective-permute-start | bytes 393224 | tf_op jit(solution)/shard_map/ppermute | solution.py:269
  70.5 2.3 copy-start.8
  72.7 124.7 %all-gather.11.cloned.1.call-start = ((), (), s32[]{:S(2)}) async-start(), calls=%async_computation.4 | async-start | bytes 7569408 | tf_op jit(solution)/shard_map/all_gather | solution.py:282
  133.3 8.5 %copy-start.5 = (f32[1,64,128]{2,1,0:T(8,128)S(1)}, f32[1,64,128]{2,1,0:T(8,128)}, u32[]{:S(2)}) copy-start(f32[1,64,128]{2,1,0:T(8,128)} %shard_map.69) | copy-start | bytes 98308
  143.3 124.0 %all-gather.13.cloned.1.call-start = ((), (), s32[]{:S(2)}) async-start(), calls=%async_computation.5 | async-start | bytes 4325376 | tf_op jit(solution)/shard_map/all_gather | solution.py:282
  204.9 15.9 %copy-start.6 = (f32[2,64,128]{2,1,0:T(8,128)S(1)}, f32[2,64,128]{2,1,0:T(8,128)}, u32[]{:S(2)}) copy-start(f32[2,64,128]{2,1,0:T(8,128)} %get-tuple-element.10) | copy-start | bytes 196612
  204.9 16.7 %copy-start.9 = (s32[1,4]{1,0:T(1,128)S(1)}, s32[1,4]{1,0:T(1,128)}, u32[]{:S(2)}) copy-start(s32[1,4]{1,0:T(1,128)} %param.11) | copy-start | bytes 52
  277.3 3.1 copy-start.4
  280.4 1.0 copy-start.1
  313.9 2.7 copy-start.2
  313.9 2.7 copy-start.3
Sparse Core Ops, SparseCore 0:
  43.0 38.7 all-gather.6
  84.0 31.5 all-gather.8
  118.6 23.1 reduce-scatter.1
  144.5 52.8 all-gather.10
  221.6 45.6 all-gather.12

commit v11 on v10

--- a/solution.py
+++ b/solution.py
@@ -219,6 +219,63 @@
     )(x)
 
 
+def gather_kernel(x_ref, out_ref, send_sem, recv_sem, *, axis, count, band):
+    me = lax.axis_index(axis)
+    ids = {name: lax.axis_index(name) for name in ("leaf", "row", "col")}
+
+    def device(peer):
+        where = dict(ids)
+        where[axis] = peer
+        return (where["leaf"], where["row"], where["col"])
+
+    mesh_ids = pl.DeviceIdType.MESH
+    barrier = pltpu.get_barrier_semaphore()
+    for d in range(1, count):
+        pl.semaphore_signal(barrier, inc=1, device_id=device(lax.rem(me + d, count)), device_id_type=mesh_ids)
+    pl.semaphore_wait(barrier, count - 1)
+    own = pl.ds(pl.multiple_of(me * band, band), band)
+    sends = []
+    for d in range(1, count):
+        peer = lax.rem(me + d, count)
+        copy = pltpu.make_async_remote_copy(
+            src_ref=x_ref,
+            dst_ref=out_ref.at[:, own, :],
+            send_sem=send_sem.at[d - 1],
+            recv_sem=recv_sem.at[d - 1],
+            device_id=device(peer),
+            device_id_type=mesh_ids,
+        )
+        copy.start()
+        sends.append(copy)
+    out_ref[:, own, :] = x_ref[...]
+    for d in range(1, count):
+        source = lax.rem(me + count - d, count)
+        part = pl.ds(pl.multiple_of(source * band, band), band)
+        pltpu.make_async_remote_copy(
+            src_ref=x_ref,
+            dst_ref=out_ref.at[:, part, :],
+            send_sem=send_sem.at[d - 1],
+            recv_sem=recv_sem.at[d - 1],
+            device_id=device(source),
+            device_id_type=mesh_ids,
+        ).wait_recv()
+    for copy in sends:
+        copy.wait_send()
+
+
+def axis_gather(x, axis, count, collective_id):
+    lead, band, last = x.shape
+    vmem = pl.BlockSpec(memory_space=pltpu.VMEM)
+    return pl.pallas_call(
+        functools.partial(gather_kernel, axis=axis, count=count, band=band),
+        out_shape=jax.ShapeDtypeStruct((lead, band * count, last), x.dtype),
+        in_specs=[vmem],
+        out_specs=vmem,
+        scratch_shapes=[pltpu.SemaphoreType.DMA((count - 1,)), pltpu.SemaphoreType.DMA((count - 1,))],
+        compiler_params=pltpu.CompilerParams(collective_id=collective_id, has_side_effects=True),
+    )(x)
+
+
 def body(sigma_top, panels, inverse_diag, slot_lists, parent_links):
     tile = TILE
     row_count = lax.axis_size("row")
@@ -243,7 +300,7 @@
     live_here = jnp.take(living, r, axis=1).astype(jnp.float32)
     factor_tile = jnp.transpose(factor_t, (0, 2, 1)) * live_here[:, None, None]
     factor_cols = lax.all_gather(factor_tile, "row", axis=1, tiled=True)
-    factor_rows = lax.all_gather(factor_tile, "col", axis=2, tiled=True)
+    factor_rows = jnp.transpose(axis_gather(factor_t, "col", col_count, 4), (0, 2, 1)) * live_here[:, None, None]
 
     inverse_band = lax.dynamic_slice_in_dim(inverse, r * band, band, 2)
     partial_gram = mm(jnp.transpose(inverse_band, (0, 2, 1)), inverse)

time: 325 us -> 311 us (0.957)
  waiting for transfers between devices: 138 us -> 84.6 us
  Pallas kernels: 97.9 us -> 133 us
    pallas_call x0 -> x1, Pallas kernels: none -> 33.1 us  [axis_gather(): pl.pallas_call(functools.partial(gather_kernel, axis=axis, count=count, b...]
    all_gather x1 -> x0, waiting for transfers between devices: 32.2 us -> none  [body(): factor_rows = lax.all_gather(factor_tile, 'col', axis=2, tiled=True)]
    reduce_scatter x1, waiting for transfers between devices: 7.08 us -> 0.03 us  [body(): lax.psum_scatter(partial_gram, 'col', scatter_dimension=2, tiled=True)]
    all_gather x2, waiting for transfers between devices: 91 us -> 84.5 us  [reduce_and_gather(): everything = lax.all_gather(both, ('row', 'col'), axis=0)]
    ppermute x4, waiting for transfers between devices: 4.33 us -> 0.01 us  [body(): rounds.append(lax.ppermute(chunk_rows, ('leaf', 'row', 'col'), pairs))]
  transfers between devices with their start and end apart: 9 -> 8, of which waited for: 7 -> 2; matrix products, arithmetic and copies ran while one was open for 7% -> 8% of each run, Pallas kernels for 3% -> 15%
where the time goes in v11:
time: 311 us; the launch traced here: 310 us
  Pallas kernels  133 us (43%)
  waiting for transfers between devices  84.6 us (27%)
  matrix products  17.3 us (6%)
  starting transfers between devices  17.2 us (6%)
  local copies, waits for them, and re-layouts  16.8 us (5%)
  between operations  16 us (5%)
  other arithmetic  14.6 us (5%)
  blocking collectives  9.68 us (3%)
    all_gather x2, waiting for transfers between devices, reduce_and_gather(): everything = lax.all_gather(both, ('row', 'col'), axis=0)  84.5 us
    pallas_call x4, Pallas kernels, axis_reduce(): pl.pallas_call(kernel, out_shape=jax.ShapeDtypeStruct((lead, out_rows, la...  84.5 us
    pallas_call x1, Pallas kernels, axis_gather(): pl.pallas_call(functools.partial(gather_kernel, axis=axis, count=count, b...  33.1 us
    ppermute x4, starting transfers between devices, body(): rounds.append(lax.ppermute(chunk_rows, ('leaf', 'row', 'col'), pairs))  17.1 us
    pallas_call x2, Pallas kernels, level_products(): pl.pallas_call(kernel, out_shape=tuple(shapes), in_specs=[pl.BlockSpec(me...  15.7 us
    dot_general x7, matrix products, mm(): jnp.matmul(a, b, precision=HIGHEST, preferred_element_type=jnp.float32)  12 us
    all_gather x1, blocking collectives, body(): chunk_rows = lax.all_gather(sigma_top, 'col', axis=1, tiled=True)  9.68 us
  transfers between devices with their start and end apart: 8, of which 2 were waited for; matrix products, arithmetic and copies ran while one was open for 8% of the time, Pallas kernels for 15%

profile of v11, /device:TPU:1, one launch (start us, length us, event | category | flops | bytes accessed | tf_op | source)
XLA Modules:
  0.0 309.6 jit_solution(1148176962962491882)
XLA Ops:
  9.5 5.3 %fusion.2.x_ref = f32[7,512,128]{2,1,0:T(8,128)} fusion(f32[1,7,128,512]{3,2,1,0:T(8,128)S(1)} %copy-done, f32[1,7,128,128]{3,2,1,0:T(8,128)} %param.8), kind=kOutput, calls=%fused_computation.6 | convolution fusion | flops 704643072 | bytes 4128768 | tf_op jit(solution)/shard_map/vkj,vrk->vjr/dot_general | solution.py:297
  14.8 26.7 %shard_map.68.x_ref = f32[7,128,128]{2,1,0:T(8,128)} custom-call(f32[7,512,128]{2,1,0:T(8,128)} %fusion.2.x_ref), custom_call_target="tpu_custom_call" | custom-call | tf_op jit(solution)/shard_map/pallas_call | solution.py:206
  43.8 9.7 %all_gather.18 = f32[32,1024]{1,0:T(8,128)S(1)} all-gather(f32[32,256]{1,0:T(8,128)S(1)} %copy-done.7), channel_id=1, replica_groups=mesh['leaf'=4,'row'=8,'col'=4] {'col'}, dimensions={1}, use_global_device_ids=true | all-gather | bytes 163840 | tf_op jit(solution)/shard_map/all_gather | solution.py:311
  53.5 5.8 %collective-permute-start.3 = (f32[32,1024]{1,0:T(8,128)S(1)}, f32[32,1024]{1,0:T(8,128)S(1)}, u32[]{:S(2)}, u32[]{:S(2)}) collective-permute-start(f32[32,1024]{1,0:T(8,128)S(1)} %all_gather.18), channel_id=1, source_target_pairs={{0,96},{1,97},{2,98},{3,99},{4,0},{5,1},{6,2},{7,3},{8,32},{9,33},... | collective-permute-start | bytes 393224 | tf_op jit(solution)/shard_map/ppermute | solution.py:326
  59.2 6.7 %collective-permute-start.2 = (f32[32,1024]{1,0:T(8,128)S(1)}, f32[32,1024]{1,0:T(8,128)S(1)}, u32[]{:S(2)}, u32[]{:S(2)}) collective-permute-start(f32[32,1024]{1,0:T(8,128)S(1)} %all_gather.18), channel_id=1, source_target_pairs={{0,64},{1,65},{2,66},{3,67},{4,96},{5,97},{6,98},{7,99},{8,0},{9,1... | collective-permute-start | bytes 393224 | tf_op jit(solution)/shard_map/ppermute | solution.py:326
  66.0 2.7 collective-permute-start.1
  68.6 1.9 collective-permute-start
  70.6 2.2 fusion
  74.2 33.1 %shard_map.69 = f32[7,512,128]{2,1,0:T(8,128)} custom-call(f32[7,128,128]{2,1,0:T(8,128)} %shard_map.68.x_ref), custom_call_target="tpu_custom_call" | custom-call | tf_op jit(solution)/shard_map/pallas_call | solution.py:269
  107.4 3.0 multiply_bitcast_fusion
  112.9 2.0 convolution_bitcast_fusion.x_ref
  114.9 12.9 %shard_map.70 = f32[1,64,128]{2,1,0:T(8,128)} custom-call(f32[1,512,128]{2,1,0:T(8,128)} %convolution_bitcast_fusion.x_ref), custom_call_target="tpu_custom_call" | custom-call | tf_op jit(solution)/shard_map/pallas_call | solution.py:206
  127.8 2.1 fusion.15
  136.0 2.3 slice.90.fac_ref
  138.2 45.0 %all-gather.8.cloned.1.call-done = f32[32,448,128]{2,1,0:T(8,128)} async-done(((f32[1,448,128]{2,1,0:T(8,128)}), f32[32,448,128]{2,1,0:T(8,128)}) %all-gather.8.cloned.1.call-update) | async-done | bytes 7340048 | tf_op jit(solution)/shard_map/all_gather | solution.py:339
  183.3 7.6 %shard_map.71 = (f32[2,128,128]{2,1,0:T(8,128)}, f32[2,64,128]{2,1,0:T(8,128)}) custom-call(s32[20]{0:T(128)} %pad_add_fusion.info_ref, f32[8,4,1,448,128]{4,3,2,1,0:T(8,128)} %bitcast.73, f32[8,4,1,448,128]{4,3,2,1,0:T(8,128)} %bitcast.74, f32[2,1024,128]{2,1,0:T(8,128)} %slice.90.fac_ref), custom_call_target="tpu_custom_call" | custom-call | tf_op jit(solution)/shard_map/pallas_call | solution.py:124
  190.8 2.5 fusion.16.x_ref
  193.3 12.4 %shard_map.72 = f32[2,64,128]{2,1,0:T(8,128)} custom-call(f32[2,512,128]{2,1,0:T(8,128)} %fusion.16.x_ref), custom_call_target="tpu_custom_call" | custom-call | tf_op jit(solution)/shard_map/pallas_call | solution.py:206
  208.0 3.0 slice.92.fac_ref
  213.1 39.5 %all-gather.10.cloned.1.call-done = f32[64,128,128]{2,1,0:T(8,128)} async-done(((f32[2,128,128]{2,1,0:T(8,128)}), f32[64,128,128]{2,1,0:T(8,128)}) %all-gather.10.cloned.1.call-update) | async-done | bytes 4194320 | tf_op jit(solution)/shard_map/all_gather | solution.py:339
  254.4 8.2 %shard_map.73 = f32[4,128,128]{2,1,0:T(8,128)} custom-call(s32[38]{0:T(128)} %pad_add_fusion.1.info_ref, f32[8,4,2,128,128]{4,3,2,1,0:T(8,128)} %bitcast.78, f32[8,4,1,448,128]{4,3,2,1,0:T(8,128)} %bitcast.76, f32[4,1024,128]{2,1,0:T(8,128)} %slice.92.fac_ref), custom_call_target="tpu_custom_call" | custom-call | tf_op jit(solution)/shard_map/pallas_call | solution.py:124
  262.6 2.3 fusion.17
  265.9 32.5 %shard_map.74 = f32[4,512,128]{2,1,0:T(8,128)} custom-call(f32[4,512,128]{2,1,0:T(8,128)} %copy-done.1), custom_call_target="tpu_custom_call" | custom-call | tf_op jit(solution)/shard_map/pallas_call | solution.py:206
  298.5 2.7 maximum_bitcast_fusion
  (78 shorter events, 21.7 us)
Async XLA Ops:
  8.0 1.5 copy-start
  8.0 103.2 %all-gather.6.cloned.1.call-start = ((), (), s32[]{:S(2)}) async-start(), calls=%async_computation.1 | async-start | bytes 4128768 | tf_op jit(solution)/shard_map/all_gather | solution.py:302
  14.8 29.0 %copy-start.7 = (f32[32,256]{1,0:T(8,128)S(1)}, f32[32,256]{1,0:T(8,128)}, u32[]{:S(2)}) copy-start(f32[32,256]{1,0:T(8,128)} %param.7) | copy-start | bytes 98308
  43.7 89.9 %reduce-scatter.2.cloned.1.call-start = ((), (), s32[]{:S(2)}) async-start(), calls=%async_computation.2 | async-start | bytes 1146880 | tf_op jit(solution)/shard_map/reduce_scatter | solution.py:307
  53.5 56.9 %collective-permute-start.3 = (f32[32,1024]{1,0:T(8,128)S(1)}, f32[32,1024]{1,0:T(8,128)S(1)}, u32[]{:S(2)}, u32[]{:S(2)}) collective-permute-start(f32[32,1024]{1,0:T(8,128)S(1)} %all_gather.18), channel_id=1, source_target_pairs={{0,96},{1,97},{2,98},{3,99},{4,0},{5,1},{6,2},{7,3},{8,32},{9,33},... | collective-permute-start | bytes 393224 | tf_op jit(solution)/shard_map/ppermute | solution.py:326
  59.2 51.1 %collective-permute-start.2 = (f32[32,1024]{1,0:T(8,128)S(1)}, f32[32,1024]{1,0:T(8,128)S(1)}, u32[]{:S(2)}, u32[]{:S(2)}) collective-permute-start(f32[32,1024]{1,0:T(8,128)S(1)} %all_gather.18), channel_id=1, source_target_pairs={{0,64},{1,65},{2,66},{3,67},{4,96},{5,97},{6,98},{7,99},{8,0},{9,1... | collective-permute-start | bytes 393224 | tf_op jit(solution)/shard_map/ppermute | solution.py:326
  66.0 44.4 %collective-permute-start.1 = (f32[32,1024]{1,0:T(8,128)S(1)}, f32[32,1024]{1,0:T(8,128)S(1)}, u32[]{:S(2)}, u32[]{:S(2)}) collective-permute-start(f32[32,1024]{1,0:T(8,128)S(1)} %all_gather.18), channel_id=1, source_target_pairs={{0,32},{1,33},{2,34},{3,35},{4,64},{5,65},{6,66},{7,67},{8,96},{9,... | collective-permute-start | bytes 393224 | tf_op jit(solution)/shard_map/ppermute | solution.py:326
  68.6 41.8 %collective-permute-start = (f32[32,1024]{1,0:T(8,128)S(1)}, f32[32,1024]{1,0:T(8,128)S(1)}, u32[]{:S(2)}, u32[]{:S(2)}) collective-permute-start(f32[32,1024]{1,0:T(8,128)S(1)} %all_gather.18), channel_id=1, source_target_pairs={{0,0},{1,1},{2,2},{3,3},{4,32},{5,33},{6,34},{7,35},{8,64},{9,65},... | collective-permute-start | bytes 393224 | tf_op jit(solution)/shard_map/ppermute | solution.py:326
  70.6 2.3 copy-start.8
  72.8 110.5 %all-gather.8.cloned.1.call-start = ((), (), s32[]{:S(2)}) async-start(), calls=%async_computation.3 | async-start | bytes 7569408 | tf_op jit(solution)/shard_map/all_gather | solution.py:339
  132.2 1.5 copy-start.5
  135.2 117.4 %all-gather.10.cloned.1.call-start = ((), (), s32[]{:S(2)}) async-start(), calls=%async_computation.4 | async-start | bytes 4325376 | tf_op jit(solution)/shard_map/all_gather | solution.py:339
  190.8 15.7 %copy-start.6 = (f32[2,64,128]{2,1,0:T(8,128)S(1)}, f32[2,64,128]{2,1,0:T(8,128)}, u32[]{:S(2)}) copy-start(f32[2,64,128]{2,1,0:T(8,128)} %get-tuple-element.10) | copy-start | bytes 196612
  190.8 16.5 %copy-start.9 = (s32[1,4]{1,0:T(1,128)S(1)}, s32[1,4]{1,0:T(1,128)}, u32[]{:S(2)}) copy-start(s32[1,4]{1,0:T(1,128)} %param.11) | copy-start | bytes 52
  262.6 2.3 copy-start.4
  265.0 1.0 copy-start.1
  298.5 2.7 copy-start.2
  298.5 2.7 copy-start.3
Sparse Core Ops, SparseCore 0:
  43.8 38.2 all-gather.5
Sparse Core Ops, SparseCore 1:
  72.9 34.9 reduce-scatter.1
  135.2 48.0 all-gather.7
  207.3 45.2 all-gather.9

commit v12 on v11

--- a/solution.py
+++ b/solution.py
@@ -91,8 +91,7 @@
         def _():
             if level == 1:
                 s = jnp.clip(source, 0, slot_count - 1)
-                lifted = tile + band + i * tile
-                acc = par_ref[s, col, parent, lifted:lifted + tile, :]
+                acc = low_ref[i, pl.ds(pl.multiple_of(s * tile, tile), tile), :]
                 for k in range(own_tiles):
                     acc -= dot_hi(p_tile(par_ref, par_prow, parent, s, k), factor[k])
             else:
@@ -294,13 +293,13 @@
     positions = slot_count + own_tiles
     band = width // row_count
 
-    partial_t = jnp.einsum("vkj,vrk->vjr", inverse, panel, precision=HIGHEST, preferred_element_type=jnp.float32)
-    factor_t = axis_reduce(partial_t, "col", col_count, False, 3)
+    partial_factor = mm(panel, inverse)
+    factor_rows = axis_reduce(partial_factor, "col", col_count, True, 3)
     living = jnp.concatenate([jnp.ones((1, slot_count), jnp.bool_), picks_all >= 0], axis=0)
     live_here = jnp.take(living, r, axis=1).astype(jnp.float32)
-    factor_tile = jnp.transpose(factor_t, (0, 2, 1)) * live_here[:, None, None]
+    factor_rows = factor_rows * live_here[:, None, None]
+    factor_tile = lax.dynamic_slice_in_dim(factor_rows, c * tile, tile, 2)
     factor_cols = lax.all_gather(factor_tile, "row", axis=1, tiled=True)
-    factor_rows = jnp.transpose(axis_gather(factor_t, "col", col_count, 4), (0, 2, 1)) * live_here[:, None, None]
 
     inverse_band = lax.dynamic_slice_in_dim(inverse, r * band, band, 2)
     partial_gram = mm(jnp.transpose(inverse_band, (0, 2, 1)), inverse)
@@ -331,10 +330,13 @@
         rows = factor_rows[first:first + products.shape[0]]
         return mm(jnp.transpose(rows, (0, 2, 1)), products)
 
-    def reduce_and_gather(first, products, sent, extra):
+    def reduce_and_gather(first, products, sent, extra, tied=None):
         count = products.shape[0]
         piece = axis_reduce(diag_partial(first, products), "row", row_count, False, first)
         piece = piece + gram_piece[first:first + count]
+        if tied is not None:
+            piece, tied = lax.optimization_barrier((piece, tied))
+            tied_out.append(tied)
         both = jnp.concatenate([sent, piece] + extra, axis=1)
         everything = lax.all_gather(both, ("row", "col"), axis=0)
         return everything.reshape(row_count, col_count, count, both.shape[1], tile)
@@ -368,14 +370,16 @@
         mm(sigma_rows, scatter_factor(factor_cols[node], picks_all[node - 1], slot_count, tile))[None]
         for node in (1, 2)
     ]
-    gathered_0 = reduce_and_gather(0, product_0[None], product_0[None], lifted)
+    tied_out = []
+    gathered_0 = reduce_and_gather(0, product_0[None], product_0[None], [], jnp.concatenate(lifted, axis=0))
+    lifted_cols = axis_gather(tied_out[0], "row", row_count, 4)
 
     info_1 = jnp.concatenate(
         [r.astype(jnp.int32)[None], picks_all[0:2].reshape(-1), jnp.zeros((2,), jnp.int32), c.astype(jnp.int32)[None]]
     )
     halves = row_count // own_tiles
     product_1, upper_half = level_products(
-        info_1, gathered_0, gathered_0, factor_cols[1:3], 1, tile, band, own_tiles, slot_count,
+        info_1, gathered_0, lifted_cols, factor_cols[1:3], 1, tile, band, own_tiles, slot_count,
         tile, tile, halves,
     )
     gathered_1 = reduce_and_gather(1, product_1, upper_half, [])

time: 311 us -> 297 us (0.955)
  waiting for transfers between devices: 84.6 us -> 72 us
    all_gather x2, waiting for transfers between devices: 84.5 us -> 65.9 us  [reduce_and_gather(): everything = lax.all_gather(both, ('row', 'col'), axis=0)]
    pallas_call x4, Pallas kernels: 84.5 us -> 102 us  [axis_reduce(): pl.pallas_call(kernel, out_shape=jax.ShapeDtypeStruct((lead, out_rows, la...]
    pallas_call x1, Pallas kernels: 33.1 us -> 18 us  [axis_gather(): pl.pallas_call(functools.partial(gather_kernel, axis=axis, count=count, b...]
    dot_general x7 -> x8, matrix products: 12 us -> 17.3 us  [mm(): jnp.matmul(a, b, precision=HIGHEST, preferred_element_type=jnp.float32)]
    dot_general x1 -> x0, matrix products: 5.26 us -> none  [body(): jnp.einsum('vkj,vrk->vjr', inverse, panel, precision=HIGHEST, preferred_e...]
    pallas_call x2, Pallas kernels: 15.7 us -> 11.7 us  [level_products(): pl.pallas_call(kernel, out_shape=tuple(shapes), in_specs=[pl.BlockSpec(me...]
    ppermute x4, waiting for transfers between devices: 0.01 us -> 3.4 us  [body(): rounds.append(lax.ppermute(chunk_rows, ('leaf', 'row', 'col'), pairs))]
  transfers between devices with their start and end apart: 8 -> 8, of which waited for: 2 -> 5; matrix products, arithmetic and copies ran while one was open for 8% -> 8% of each run, Pallas kernels for 15% -> 9%
where the time goes in v12:
time: 297 us; the launch traced here: 296 us
  Pallas kernels  132 us (44%)
  waiting for transfers between devices  72 us (24%)
  starting transfers between devices  18.5 us (6%)
  local copies, waits for them, and re-layouts  17.8 us (6%)
  matrix products  17.3 us (6%)
  between operations  16 us (5%)
  other arithmetic  13 us (4%)
  blocking collectives  9.78 us (3%)
    pallas_call x4, Pallas kernels, axis_reduce(): pl.pallas_call(kernel, out_shape=jax.ShapeDtypeStruct((lead, out_rows, la...  102 us
    all_gather x2, waiting for transfers between devices, reduce_and_gather(): everything = lax.all_gather(both, ('row', 'col'), axis=0)  65.9 us
    ppermute x4, starting transfers between devices, body(): rounds.append(lax.ppermute(chunk_rows, ('leaf', 'row', 'col'), pairs))  18.3 us
    pallas_call x1, Pallas kernels, axis_gather(): pl.pallas_call(functools.partial(gather_kernel, axis=axis, count=count, b...  18 us
    dot_general x8, matrix products, mm(): jnp.matmul(a, b, precision=HIGHEST, preferred_element_type=jnp.float32)  17.3 us
    pallas_call x2, Pallas kernels, level_products(): pl.pallas_call(kernel, out_shape=tuple(shapes), in_specs=[pl.BlockSpec(me...  11.7 us
    all_gather x1, blocking collectives, body(): chunk_rows = lax.all_gather(sigma_top, 'col', axis=1, tiled=True)  9.78 us
  transfers between devices with their start and end apart: 8, of which 5 were waited for; matrix products, arithmetic and copies ran while one was open for 8% of the time, Pallas kernels for 9%

profile of v12, /device:TPU:1, one launch (start us, length us, event | category | flops | bytes accessed | tf_op | source)
XLA Modules:
  0.0 295.9 jit_solution(6097436659679461147)
XLA Ops:
  9.5 3.9 %fusion.2.x_ref = f32[7,128,512]{2,1,0:T(8,128)} fusion(f32[1,7,128,512]{3,2,1,0:T(8,128)S(1)} %copy-done, f32[1,7,128,128]{3,2,1,0:T(8,128)} %param.8), kind=kOutput, calls=%fused_computation.6 | convolution fusion | flops 704643072 | bytes 4128768 | tf_op jit(solution)/shard_map/dot_general | solution.py:15
  13.4 48.4 %shard_map.68 = f32[7,128,512]{2,1,0:T(8,128)} custom-call(f32[7,128,512]{2,1,0:T(8,128)} %fusion.2.x_ref), custom_call_target="tpu_custom_call" | custom-call | tf_op jit(solution)/shard_map/pallas_call | solution.py:205
  65.8 9.8 %all_gather.18 = f32[32,1024]{1,0:T(8,128)S(1)} all-gather(f32[32,256]{1,0:T(8,128)S(1)} %copy-done.8), channel_id=1, replica_groups=mesh['leaf'=4,'row'=8,'col'=4] {'col'}, dimensions={1}, use_global_device_ids=true | all-gather | bytes 163840 | tf_op jit(solution)/shard_map/all_gather | solution.py:310
  75.6 7.0 %collective-permute-start.3 = (f32[32,1024]{1,0:T(8,128)S(1)}, f32[32,1024]{1,0:T(8,128)S(1)}, u32[]{:S(2)}, u32[]{:S(2)}) collective-permute-start(f32[32,1024]{1,0:T(8,128)S(1)} %all_gather.18), channel_id=1, source_target_pairs={{0,96},{1,97},{2,98},{3,99},{4,0},{5,1},{6,2},{7,3},{8,32},{9,33},... | collective-permute-start | bytes 393224 | tf_op jit(solution)/shard_map/ppermute | solution.py:325
  82.6 6.7 %collective-permute-start.2 = (f32[32,1024]{1,0:T(8,128)S(1)}, f32[32,1024]{1,0:T(8,128)S(1)}, u32[]{:S(2)}, u32[]{:S(2)}) collective-permute-start(f32[32,1024]{1,0:T(8,128)S(1)} %all_gather.18), channel_id=1, source_target_pairs={{0,64},{1,65},{2,66},{3,67},{4,96},{5,97},{6,98},{7,99},{8,0},{9,1... | collective-permute-start | bytes 393224 | tf_op jit(solution)/shard_map/ppermute | solution.py:325
  89.3 2.7 collective-permute-start.1
  92.0 1.9 collective-permute-start
  93.9 2.2 fusion
  101.8 2.6 all-gather.6.cloned.1.call-done
  106.1 2.2 convolution_bitcast_fusion.x_ref
  108.4 9.1 %shard_map.69 = f32[1,64,128]{2,1,0:T(8,128)} custom-call(f32[1,512,128]{2,1,0:T(8,128)} %convolution_bitcast_fusion.x_ref), custom_call_target="tpu_custom_call" | custom-call | tf_op jit(solution)/shard_map/pallas_call | solution.py:205
  117.5 2.1 fusion.15
  126.1 18.0 %shard_map.70.low_ref = f32[2,1024,128]{2,1,0:T(8,128)} custom-call(f32[2,128,128]{2,1,0:T(8,128)} %pad_maximum_fusion.1.x_ref), custom_call_target="tpu_custom_call" | custom-call | tf_op jit(solution)/shard_map/pallas_call | solution.py:268
  144.1 2.3 slice.90.fac_ref
  146.4 25.7 %all-gather.8.cloned.1.call-done = f32[32,192,128]{2,1,0:T(8,128)} async-done(((f32[1,192,128]{2,1,0:T(8,128)}), f32[32,192,128]{2,1,0:T(8,128)}) %all-gather.8.cloned.1.call-update) | async-done | bytes 3145744 | tf_op jit(solution)/shard_map/all_gather | solution.py:341
  172.2 4.6 %shard_map.71 = (f32[2,128,128]{2,1,0:T(8,128)}, f32[2,64,128]{2,1,0:T(8,128)}) custom-call(s32[20]{0:T(128)} %pad_add_fusion.info_ref, f32[8,4,1,192,128]{4,3,2,1,0:T(8,128)} %bitcast.69, f32[2,1024,128]{2,1,0:T(8,128)} %shard_map.70.low_ref, f32[2,1024,128]{2,1,0:T(8,128)} %slice.90.fac_ref), custom_call_target="tpu_custom_call" | custom-call | tf_op jit(solution)/shard_map/pallas_call | solution.py:123
  176.8 2.9 fusion.16.x_ref
  179.7 12.0 %shard_map.72 = f32[2,64,128]{2,1,0:T(8,128)} custom-call(f32[2,512,128]{2,1,0:T(8,128)} %fusion.16.x_ref), custom_call_target="tpu_custom_call" | custom-call | tf_op jit(solution)/shard_map/pallas_call | solution.py:205
  194.0 3.1 %slice.92.fac_ref = f32[4,1024,128]{2,1,0:T(8,128)} slice(f32[7,1024,128]{2,1,0:T(8,128)} %all-gather.6.cloned.1.call-done), slice={[3:7], [0:1024], [0:128]} | slice | bytes 4194304 | tf_op jit(solution)/shard_map/slice | solution.py:392
  199.1 40.2 %all-gather.10.cloned.1.call-done = f32[64,128,128]{2,1,0:T(8,128)} async-done(((f32[2,128,128]{2,1,0:T(8,128)}), f32[64,128,128]{2,1,0:T(8,128)}) %all-gather.10.cloned.1.call-update) | async-done | bytes 4194320 | tf_op jit(solution)/shard_map/all_gather | solution.py:341
  241.1 7.0 %shard_map.73 = f32[4,128,128]{2,1,0:T(8,128)} custom-call(s32[38]{0:T(128)} %pad_add_fusion.1.info_ref, f32[8,4,2,128,128]{4,3,2,1,0:T(8,128)} %bitcast.73, f32[8,4,1,192,128]{4,3,2,1,0:T(8,128)} %bitcast.71, f32[4,1024,128]{2,1,0:T(8,128)} %slice.92.fac_ref), custom_call_target="tpu_custom_call" | custom-call | tf_op jit(solution)/shard_map/pallas_call | solution.py:123
  248.1 3.1 %fusion.17 = f32[4,512,128]{2,1,0:T(8,128)S(1)} fusion(f32[7,128,512]{2,1,0:T(8,128)} %copy-done.1, f32[4,128,128]{2,1,0:T(8,128)} %shard_map.73), kind=kOutput, calls=%fused_computation.68 | convolution fusion | flops 402653184 | bytes 3145728 | tf_op jit(solution)/shard_map/dot_general | solution.py:15
  252.2 32.5 %shard_map.74 = f32[4,512,128]{2,1,0:T(8,128)} custom-call(f32[4,512,128]{2,1,0:T(8,128)} %copy-done.2), custom_call_target="tpu_custom_call" | custom-call | tf_op jit(solution)/shard_map/pallas_call | solution.py:205
  284.8 2.7 maximum_bitcast_fusion
  (80 shorter events, 27.2 us)
Async XLA Ops:
  8.0 1.5 copy-start
  8.0 96.4 %all-gather.6.cloned.1.call-start = ((), (), s32[]{:S(2)}) async-start(), calls=%async_computation.1 | async-start | bytes 4128768 | tf_op jit(solution)/shard_map/all_gather | solution.py:302
  61.8 3.9 %copy-start.8 = (f32[32,256]{1,0:T(8,128)S(1)}, f32[32,256]{1,0:T(8,128)}, u32[]{:S(2)}) copy-start(f32[32,256]{1,0:T(8,128)} %param.7) | copy-start | bytes 98308
  63.6 1.2 copy-start.1
  65.7 58.3 %reduce-scatter.2.cloned.1.call-start = ((), (), s32[]{:S(2)}) async-start(), calls=%async_computation.2 | async-start | bytes 1146880 | tf_op jit(solution)/shard_map/reduce_scatter | solution.py:306
  75.6 22.1 %collective-permute-start.3 = (f32[32,1024]{1,0:T(8,128)S(1)}, f32[32,1024]{1,0:T(8,128)S(1)}, u32[]{:S(2)}, u32[]{:S(2)}) collective-permute-start(f32[32,1024]{1,0:T(8,128)S(1)} %all_gather.18), channel_id=1, source_target_pairs={{0,96},{1,97},{2,98},{3,99},{4,0},{5,1},{6,2},{7,3},{8,32},{9,33},... | collective-permute-start | bytes 393224 | tf_op jit(solution)/shard_map/ppermute | solution.py:325
  82.6 15.1 %collective-permute-start.2 = (f32[32,1024]{1,0:T(8,128)S(1)}, f32[32,1024]{1,0:T(8,128)S(1)}, u32[]{:S(2)}, u32[]{:S(2)}) collective-permute-start(f32[32,1024]{1,0:T(8,128)S(1)} %all_gather.18), channel_id=1, source_target_pairs={{0,64},{1,65},{2,66},{3,67},{4,96},{5,97},{6,98},{7,99},{8,0},{9,1... | collective-permute-start | bytes 393224 | tf_op jit(solution)/shard_map/ppermute | solution.py:325
  89.3 10.2 %collective-permute-start.1 = (f32[32,1024]{1,0:T(8,128)S(1)}, f32[32,1024]{1,0:T(8,128)S(1)}, u32[]{:S(2)}, u32[]{:S(2)}) collective-permute-start(f32[32,1024]{1,0:T(8,128)S(1)} %all_gather.18), channel_id=1, source_target_pairs={{0,32},{1,33},{2,34},{3,35},{4,64},{5,65},{6,66},{7,67},{8,96},{9,... | collective-permute-start | bytes 393224 | tf_op jit(solution)/shard_map/ppermute | solution.py:325
  92.0 9.1 %collective-permute-start = (f32[32,1024]{1,0:T(8,128)S(1)}, f32[32,1024]{1,0:T(8,128)S(1)}, u32[]{:S(2)}, u32[]{:S(2)}) collective-permute-start(f32[32,1024]{1,0:T(8,128)S(1)} %all_gather.18), channel_id=1, source_target_pairs={{0,0},{1,1},{2,2},{3,3},{4,32},{5,33},{6,34},{7,35},{8,64},{9,65},... | collective-permute-start | bytes 393224 | tf_op jit(solution)/shard_map/ppermute | solution.py:325
  93.9 2.3 copy-start.9
  96.2 76.0 %all-gather.8.cloned.1.call-start = ((), (), s32[]{:S(2)}) async-start(), calls=%async_computation.3 | async-start | bytes 3244032 | tf_op jit(solution)/shard_map/all_gather | solution.py:341
  121.9 2.1 copy-start.6
  125.4 113.9 %all-gather.10.cloned.1.call-start = ((), (), s32[]{:S(2)}) async-start(), calls=%async_computation.4 | async-start | bytes 4325376 | tf_op jit(solution)/shard_map/all_gather | solution.py:341
  176.8 15.7 %copy-start.7 = (f32[2,64,128]{2,1,0:T(8,128)S(1)}, f32[2,64,128]{2,1,0:T(8,128)}, u32[]{:S(2)}) copy-start(f32[2,64,128]{2,1,0:T(8,128)} %get-tuple-element.14) | copy-start | bytes 196612
  176.8 16.6 %copy-start.10 = (s32[1,4]{1,0:T(1,128)S(1)}, s32[1,4]{1,0:T(1,128)}, u32[]{:S(2)}) copy-start(s32[1,4]{1,0:T(1,128)} %param.11) | copy-start | bytes 52
  248.1 3.1 %copy-start.5 = (f32[7,64,128]{2,1,0:T(8,128)S(1)}, f32[7,64,128]{2,1,0:T(8,128)}, u32[]{:S(2)}) copy-start(f32[7,64,128]{2,1,0:T(8,128)} %reduce-scatter.2.cloned.1.call-done) | copy-start | bytes 688132
  251.3 1.0 copy-start.2
  284.8 2.7 copy-start.3
  284.8 2.7 copy-start.4
Sparse Core Ops, SparseCore 0:
  65.8 38.5 all-gather.5
Sparse Core Ops, SparseCore 1:
  96.3 22.2 reduce-scatter.1
  125.5 46.6 all-gather.7
  193.3 45.9 all-gather.9

commit v13 on v12

--- a/solution.py
+++ b/solution.py
@@ -295,14 +295,15 @@
 
     partial_factor = mm(panel, inverse)
     factor_rows = axis_reduce(partial_factor, "col", col_count, True, 3)
+    inverse_band = lax.dynamic_slice_in_dim(inverse, r * band, band, 2)
+    partial_gram = mm(jnp.transpose(inverse_band, (0, 2, 1)), inverse)
+    partial_gram, factor_rows = lax.optimization_barrier((partial_gram, factor_rows))
     living = jnp.concatenate([jnp.ones((1, slot_count), jnp.bool_), picks_all >= 0], axis=0)
     live_here = jnp.take(living, r, axis=1).astype(jnp.float32)
     factor_rows = factor_rows * live_here[:, None, None]
     factor_tile = lax.dynamic_slice_in_dim(factor_rows, c * tile, tile, 2)
     factor_cols = lax.all_gather(factor_tile, "row", axis=1, tiled=True)
 
-    inverse_band = lax.dynamic_slice_in_dim(inverse, r * band, band, 2)
-    partial_gram = mm(jnp.transpose(inverse_band, (0, 2, 1)), inverse)
     gram_piece = lax.psum_scatter(partial_gram, "col", scatter_dimension=2, tiled=True)
 
     leaf = lax.axis_index("leaf")

time: 297 us -> 298 us (level)
  transfers between devices with their start and end apart: 8 -> 8, of which waited for: 5 -> 5; matrix products, arithmetic and copies ran while one was open for 8% -> 7% of each run, Pallas kernels for 9% -> 9%
where the time goes in v13:
time: 298 us; the launch traced here: 297 us
  Pallas kernels  132 us (44%)
  waiting for transfers between devices  73.7 us (25%)
  starting transfers between devices  18.5 us (6%)
  local copies, waits for them, and re-layouts  17.7 us (6%)
  matrix products  16.3 us (5%)
  between operations  16 us (5%)
  other arithmetic  13.1 us (4%)
  blocking collectives  9.78 us (3%)
    pallas_call x4, Pallas kernels, axis_reduce(): pl.pallas_call(kernel, out_shape=jax.ShapeDtypeStruct((lead, out_rows, la...  102 us
    all_gather x2, waiting for transfers between devices, reduce_and_gather(): everything = lax.all_gather(both, ('row', 'col'), axis=0)  65.5 us
    ppermute x4, starting transfers between devices, body(): rounds.append(lax.ppermute(chunk_rows, ('leaf', 'row', 'col'), pairs))  18.3 us
    pallas_call x1, Pallas kernels, axis_gather(): pl.pallas_call(functools.partial(gather_kernel, axis=axis, count=count, b...  18 us
    dot_general x8, matrix products, mm(): jnp.matmul(a, b, precision=HIGHEST, preferred_element_type=jnp.float32)  16.3 us
    pallas_call x2, Pallas kernels, level_products(): pl.pallas_call(kernel, out_shape=tuple(shapes), in_specs=[pl.BlockSpec(me...  11.7 us
    all_gather x1, blocking collectives, body(): chunk_rows = lax.all_gather(sigma_top, 'col', axis=1, tiled=True)  9.78 us
  transfers between devices with their start and end apart: 8, of which 5 were waited for; matrix products, arithmetic and copies ran while one was open for 7% of the time, Pallas kernels for 9%

profile of v13, /device:TPU:1, one launch (start us, length us, event | category | flops | bytes accessed | tf_op | source)
XLA Modules:
  0.0 297.1 jit_solution(9240392659690136838)
XLA Ops:
  9.5 2.2 fusion.2
  11.7 2.8 fusion.x_ref
  14.6 48.4 %shard_map.68 = f32[7,128,512]{2,1,0:T(8,128)} custom-call(f32[7,128,512]{2,1,0:T(8,128)} %fusion.x_ref), custom_call_target="tpu_custom_call" | custom-call | tf_op jit(solution)/shard_map/pallas_call | solution.py:205
  67.0 9.8 %all_gather.18 = f32[32,1024]{1,0:T(8,128)S(1)} all-gather(f32[32,256]{1,0:T(8,128)S(1)} %copy-done.9), channel_id=1, replica_groups=mesh['leaf'=4,'row'=8,'col'=4] {'col'}, dimensions={1}, use_global_device_ids=true | all-gather | bytes 163840 | tf_op jit(solution)/shard_map/all_gather | solution.py:311
  76.8 7.0 %collective-permute-start.3 = (f32[32,1024]{1,0:T(8,128)S(1)}, f32[32,1024]{1,0:T(8,128)S(1)}, u32[]{:S(2)}, u32[]{:S(2)}) collective-permute-start(f32[32,1024]{1,0:T(8,128)S(1)} %all_gather.18), channel_id=1, source_target_pairs={{0,96},{1,97},{2,98},{3,99},{4,0},{5,1},{6,2},{7,3},{8,32},{9,33},... | collective-permute-start | bytes 393224 | tf_op jit(solution)/shard_map/ppermute | solution.py:326
  83.8 6.7 %collective-permute-start.2 = (f32[32,1024]{1,0:T(8,128)S(1)}, f32[32,1024]{1,0:T(8,128)S(1)}, u32[]{:S(2)}, u32[]{:S(2)}) collective-permute-start(f32[32,1024]{1,0:T(8,128)S(1)} %all_gather.18), channel_id=1, source_target_pairs={{0,64},{1,65},{2,66},{3,67},{4,96},{5,97},{6,98},{7,99},{8,0},{9,1... | collective-permute-start | bytes 393224 | tf_op jit(solution)/shard_map/ppermute | solution.py:326
  90.5 2.7 collective-permute-start.1
  96.8 3.9 %collective-permute-done.1 = f32[32,1024]{1,0:T(8,128)S(1)} collective-permute-done((f32[32,1024]{1,0:T(8,128)S(1)}, f32[32,1024]{1,0:T(8,128)S(1)}, u32[]{:S(2)}, u32[]{:S(2)}) %collective-permute-start.1) | collective-permute-done | bytes 131104 | tf_op jit(solution)/shard_map/ppermute | solution.py:326
  103.0 2.6 all-gather.6.cloned.1.call-done
  107.3 2.2 convolution_bitcast_fusion.x_ref
  109.6 9.1 %shard_map.69 = f32[1,64,128]{2,1,0:T(8,128)} custom-call(f32[1,512,128]{2,1,0:T(8,128)} %convolution_bitcast_fusion.x_ref), custom_call_target="tpu_custom_call" | custom-call | tf_op jit(solution)/shard_map/pallas_call | solution.py:205
  118.6 2.1 fusion.15
  127.3 18.0 %shard_map.70.low_ref = f32[2,1024,128]{2,1,0:T(8,128)} custom-call(f32[2,128,128]{2,1,0:T(8,128)} %pad_maximum_fusion.1.x_ref), custom_call_target="tpu_custom_call" | custom-call | tf_op jit(solution)/shard_map/pallas_call | solution.py:268
  145.3 2.3 slice.90.fac_ref
  147.7 25.7 %all-gather.8.cloned.1.call-done = f32[32,192,128]{2,1,0:T(8,128)} async-done(((f32[1,192,128]{2,1,0:T(8,128)}), f32[32,192,128]{2,1,0:T(8,128)}) %all-gather.8.cloned.1.call-update) | async-done | bytes 3145744 | tf_op jit(solution)/shard_map/all_gather | solution.py:342
  173.3 4.6 %shard_map.71 = (f32[2,128,128]{2,1,0:T(8,128)}, f32[2,64,128]{2,1,0:T(8,128)}) custom-call(s32[20]{0:T(128)} %pad_add_fusion.info_ref, f32[8,4,1,192,128]{4,3,2,1,0:T(8,128)} %bitcast.69, f32[2,1024,128]{2,1,0:T(8,128)} %shard_map.70.low_ref, f32[2,1024,128]{2,1,0:T(8,128)} %slice.90.fac_ref), custom_call_target="tpu_custom_call" | custom-call | tf_op jit(solution)/shard_map/pallas_call | solution.py:123
  178.0 2.9 fusion.16.x_ref
  180.9 12.3 %shard_map.72 = f32[2,64,128]{2,1,0:T(8,128)} custom-call(f32[2,512,128]{2,1,0:T(8,128)} %fusion.16.x_ref), custom_call_target="tpu_custom_call" | custom-call | tf_op jit(solution)/shard_map/pallas_call | solution.py:205
  195.5 3.1 %slice.92.fac_ref = f32[4,1024,128]{2,1,0:T(8,128)} slice(f32[7,1024,128]{2,1,0:T(8,128)} %all-gather.6.cloned.1.call-done), slice={[3:7], [0:1024], [0:128]} | slice | bytes 4194304 | tf_op jit(solution)/shard_map/slice | solution.py:393
  200.6 39.8 %all-gather.10.cloned.1.call-done = f32[64,128,128]{2,1,0:T(8,128)} async-done(((f32[2,128,128]{2,1,0:T(8,128)}), f32[64,128,128]{2,1,0:T(8,128)}) %all-gather.10.cloned.1.call-update) | async-done | bytes 4194320 | tf_op jit(solution)/shard_map/all_gather | solution.py:342
  242.2 7.0 %shard_map.73 = f32[4,128,128]{2,1,0:T(8,128)} custom-call(s32[38]{0:T(128)} %pad_add_fusion.1.info_ref, f32[8,4,2,128,128]{4,3,2,1,0:T(8,128)} %bitcast.73, f32[8,4,1,192,128]{4,3,2,1,0:T(8,128)} %bitcast.71, f32[4,1024,128]{2,1,0:T(8,128)} %slice.92.fac_ref), custom_call_target="tpu_custom_call" | custom-call | tf_op jit(solution)/shard_map/pallas_call | solution.py:123
  249.3 3.1 %fusion.17 = f32[4,512,128]{2,1,0:T(8,128)S(1)} fusion(f32[7,128,512]{2,1,0:T(8,128)} %copy-done.1, f32[4,128,128]{2,1,0:T(8,128)} %shard_map.73), kind=kOutput, calls=%fused_computation.68 | convolution fusion | flops 402653184 | bytes 3145728 | tf_op jit(solution)/shard_map/dot_general | solution.py:15
  253.4 32.5 %shard_map.74 = f32[4,512,128]{2,1,0:T(8,128)} custom-call(f32[4,512,128]{2,1,0:T(8,128)} %copy-done.2), custom_call_target="tpu_custom_call" | custom-call | tf_op jit(solution)/shard_map/pallas_call | solution.py:205
  286.0 2.7 maximum_bitcast_fusion
  (82 shorter events, 27.4 us)
Async XLA Ops:
  8.0 1.5 copy-start
  8.0 3.7 %copy-start.5 = (f32[1,7,128,128]{3,2,1,0:T(8,128)S(1)}, f32[1,7,128,128]{3,2,1,0:T(8,128)}, u32[]{:S(2)}) copy-start(f32[1,7,128,128]{3,2,1,0:T(8,128)} %param.8) | copy-start | bytes 1376260
  8.0 97.6 %all-gather.6.cloned.1.call-start = ((), (), s32[]{:S(2)}) async-start(), calls=%async_computation.1 | async-start | bytes 4128768 | tf_op jit(solution)/shard_map/all_gather | solution.py:305
  63.0 3.9 %copy-start.9 = (f32[32,256]{1,0:T(8,128)S(1)}, f32[32,256]{1,0:T(8,128)}, u32[]{:S(2)}) copy-start(f32[32,256]{1,0:T(8,128)} %param.7) | copy-start | bytes 98308
  64.8 1.2 copy-start.1
  66.1 29.1 %copy-start.10 = (s32[1,6,8]{2,0,1:T(1,128)S(1)}, s32[1,6,8]{2,0,1:T(1,128)}, u32[]{:S(2)}) copy-start(s32[1,6,8]{2,0,1:T(1,128)} %param.10) | copy-start | bytes 580
  66.9 58.3 %reduce-scatter.2.cloned.1.call-start = ((), (), s32[]{:S(2)}) async-start(), calls=%async_computation.2 | async-start | bytes 1146880 | tf_op jit(solution)/shard_map/reduce_scatter | solution.py:307
  76.8 20.0 %collective-permute-start.3 = (f32[32,1024]{1,0:T(8,128)S(1)}, f32[32,1024]{1,0:T(8,128)S(1)}, u32[]{:S(2)}, u32[]{:S(2)}) collective-permute-start(f32[32,1024]{1,0:T(8,128)S(1)} %all_gather.18), channel_id=1, source_target_pairs={{0,96},{1,97},{2,98},{3,99},{4,0},{5,1},{6,2},{7,3},{8,32},{9,33},... | collective-permute-start | bytes 393224 | tf_op jit(solution)/shard_map/ppermute | solution.py:326
  83.8 13.0 %collective-permute-start.2 = (f32[32,1024]{1,0:T(8,128)S(1)}, f32[32,1024]{1,0:T(8,128)S(1)}, u32[]{:S(2)}, u32[]{:S(2)}) collective-permute-start(f32[32,1024]{1,0:T(8,128)S(1)} %all_gather.18), channel_id=1, source_target_pairs={{0,64},{1,65},{2,66},{3,67},{4,96},{5,97},{6,98},{7,99},{8,0},{9,1... | collective-permute-start | bytes 393224 | tf_op jit(solution)/shard_map/ppermute | solution.py:326
  90.5 10.2 %collective-permute-start.1 = (f32[32,1024]{1,0:T(8,128)S(1)}, f32[32,1024]{1,0:T(8,128)S(1)}, u32[]{:S(2)}, u32[]{:S(2)}) collective-permute-start(f32[32,1024]{1,0:T(8,128)S(1)} %all_gather.18), channel_id=1, source_target_pairs={{0,32},{1,33},{2,34},{3,35},{4,64},{5,65},{6,66},{7,67},{8,96},{9,... | collective-permute-start | bytes 393224 | tf_op jit(solution)/shard_map/ppermute | solution.py:326
  93.2 9.1 %collective-permute-start = (f32[32,1024]{1,0:T(8,128)S(1)}, f32[32,1024]{1,0:T(8,128)S(1)}, u32[]{:S(2)}, u32[]{:S(2)}) collective-permute-start(f32[32,1024]{1,0:T(8,128)S(1)} %all_gather.18), channel_id=1, source_target_pairs={{0,0},{1,1},{2,2},{3,3},{4,32},{5,33},{6,34},{7,35},{8,64},{9,65},... | collective-permute-start | bytes 393224 | tf_op jit(solution)/shard_map/ppermute | solution.py:326
  95.1 78.2 %all-gather.8.cloned.1.call-start = ((), (), s32[]{:S(2)}) async-start(), calls=%async_computation.3 | async-start | bytes 3244032 | tf_op jit(solution)/shard_map/all_gather | solution.py:342
  123.1 2.1 copy-start.7
  126.6 113.8 %all-gather.10.cloned.1.call-start = ((), (), s32[]{:S(2)}) async-start(), calls=%async_computation.4 | async-start | bytes 4325376 | tf_op jit(solution)/shard_map/all_gather | solution.py:342
  178.0 16.1 %copy-start.8 = (f32[2,64,128]{2,1,0:T(8,128)S(1)}, f32[2,64,128]{2,1,0:T(8,128)}, u32[]{:S(2)}) copy-start(f32[2,64,128]{2,1,0:T(8,128)} %get-tuple-element.18) | copy-start | bytes 196612
  178.0 16.9 %copy-start.11 = (s32[1,4]{1,0:T(1,128)S(1)}, s32[1,4]{1,0:T(1,128)}, u32[]{:S(2)}) copy-start(s32[1,4]{1,0:T(1,128)} %param.11) | copy-start | bytes 52
  249.3 3.1 %copy-start.6 = (f32[7,64,128]{2,1,0:T(8,128)S(1)}, f32[7,64,128]{2,1,0:T(8,128)}, u32[]{:S(2)}) copy-start(f32[7,64,128]{2,1,0:T(8,128)} %reduce-scatter.2.cloned.1.call-done) | copy-start | bytes 688132
  252.4 1.0 copy-start.2
  286.0 2.7 copy-start.3
  286.0 2.7 copy-start.4
Sparse Core Ops, SparseCore 0:
  67.0 38.5 all-gather.5
Sparse Core Ops, SparseCore 1:
  95.2 22.2 reduce-scatter.1
  126.7 46.6 all-gather.7
  194.9 45.5 all-gather.9

commit v14 on v12

--- a/solution.py
+++ b/solution.py
@@ -299,7 +299,13 @@
     live_here = jnp.take(living, r, axis=1).astype(jnp.float32)
     factor_rows = factor_rows * live_here[:, None, None]
     factor_tile = lax.dynamic_slice_in_dim(factor_rows, c * tile, tile, 2)
-    factor_cols = lax.all_gather(factor_tile, "row", axis=1, tiled=True)
+    factor_cols = jnp.concatenate(
+        [
+            lax.all_gather(factor_tile[0:1], "row", axis=1, tiled=True),
+            lax.all_gather(factor_tile[1:], "row", axis=1, tiled=True),
+        ],
+        axis=0,
+    )
 
     inverse_band = lax.dynamic_slice_in_dim(inverse, r * band, band, 2)
     partial_gram = mm(jnp.transpose(inverse_band, (0, 2, 1)), inverse)

time: 297 us -> 311 us (1.047)
  blocking collectives: 9.78 us -> 24.3 us
  Pallas kernels: 132 us -> 140 us
  waiting for transfers between devices: 72 us -> 64.6 us
    all_gather x0 -> x1, blocking collectives: none -> 14.5 us  [body(): lax.all_gather(factor_tile[0:1], 'row', axis=1, tiled=True)]
    pallas_call x4, Pallas kernels: 102 us -> 110 us  [axis_reduce(): pl.pallas_call(kernel, out_shape=jax.ShapeDtypeStruct((lead, out_rows, la...]
    ppermute x4, waiting for transfers between devices: 3.4 us -> 0.01 us  [body(): rounds.append(lax.ppermute(chunk_rows, ('leaf', 'row', 'col'), pairs))]
  transfers between devices with their start and end apart: 8 -> 8, of which waited for: 5 -> 2; matrix products, arithmetic and copies ran while one was open for 8% -> 7% of each run, Pallas kernels for 9% -> 27%
where the time goes in v14:
time: 311 us; the launch traced here: 310 us
  Pallas kernels  140 us (45%)
  waiting for transfers between devices  64.6 us (21%)
  blocking collectives  24.3 us (8%)
  local copies, waits for them, and re-layouts  19.6 us (6%)
  starting transfers between devices  18.5 us (6%)
  between operations  15.6 us (5%)
  matrix products  15.2 us (5%)
  other arithmetic  13 us (4%)
    pallas_call x4, Pallas kernels, axis_reduce(): pl.pallas_call(kernel, out_shape=jax.ShapeDtypeStruct((lead, out_rows, la...  110 us
    all_gather x2, waiting for transfers between devices, reduce_and_gather(): everything = lax.all_gather(both, ('row', 'col'), axis=0)  64.5 us
    ppermute x4, starting transfers between devices, body(): rounds.append(lax.ppermute(chunk_rows, ('leaf', 'row', 'col'), pairs))  18.3 us
    pallas_call x1, Pallas kernels, axis_gather(): pl.pallas_call(functools.partial(gather_kernel, axis=axis, count=count, b...  18 us
    dot_general x8, matrix products, mm(): jnp.matmul(a, b, precision=HIGHEST, preferred_element_type=jnp.float32)  15.2 us
    all_gather x1, blocking collectives, body(): lax.all_gather(factor_tile[0:1], 'row', axis=1, tiled=True)  14.5 us
    pallas_call x2, Pallas kernels, level_products(): pl.pallas_call(kernel, out_shape=tuple(shapes), in_specs=[pl.BlockSpec(me...  11.7 us
    all_gather x1, blocking collectives, body(): chunk_rows = lax.all_gather(sigma_top, 'col', axis=1, tiled=True)  9.82 us
  transfers between devices with their start and end apart: 8, of which 2 were waited for; matrix products, arithmetic and copies ran while one was open for 7% of the time, Pallas kernels for 27%

profile of v14, /device:TPU:1, one launch (start us, length us, event | category | flops | bytes accessed | tf_op | source)
XLA Modules:
  0.0 310.4 jit_solution(16374087105512726813)
XLA Ops:
  9.5 2.2 fusion
  11.8 2.8 fusion.2.x_ref
  14.7 55.7 %shard_map.68 = f32[7,128,512]{2,1,0:T(8,128)} custom-call(f32[7,128,512]{2,1,0:T(8,128)} %fusion.2.x_ref), custom_call_target="tpu_custom_call" | custom-call | tf_op jit(solution)/shard_map/pallas_call | solution.py:205
  74.7 9.8 %all_gather.21 = f32[32,1024]{1,0:T(8,128)S(1)} all-gather(f32[32,256]{1,0:T(8,128)S(1)} %copy-done.9), channel_id=1, replica_groups=mesh['leaf'=4,'row'=8,'col'=4] {'col'}, dimensions={1}, use_global_device_ids=true | all-gather | bytes 163840 | tf_op jit(solution)/shard_map/all_gather | solution.py:316
  84.5 7.0 %collective-permute-start.3 = (f32[32,1024]{1,0:T(8,128)S(1)}, f32[32,1024]{1,0:T(8,128)S(1)}, u32[]{:S(2)}, u32[]{:S(2)}) collective-permute-start(f32[32,1024]{1,0:T(8,128)S(1)} %all_gather.21), channel_id=1, source_target_pairs={{0,96},{1,97},{2,98},{3,99},{4,0},{5,1},{6,2},{7,3},{8,32},{9,33},... | collective-permute-start | bytes 393224 | tf_op jit(solution)/shard_map/ppermute | solution.py:331
  91.5 6.7 %collective-permute-start.2 = (f32[32,1024]{1,0:T(8,128)S(1)}, f32[32,1024]{1,0:T(8,128)S(1)}, u32[]{:S(2)}, u32[]{:S(2)}) collective-permute-start(f32[32,1024]{1,0:T(8,128)S(1)} %all_gather.21), channel_id=1, source_target_pairs={{0,64},{1,65},{2,66},{3,67},{4,96},{5,97},{6,98},{7,99},{8,0},{9,1... | collective-permute-start | bytes 393224 | tf_op jit(solution)/shard_map/ppermute | solution.py:331
  98.3 2.7 collective-permute-start.1
  100.9 1.9 collective-permute-start
  105.1 14.5 %all_gather.22 = f32[1,1024,128]{2,1,0:T(8,128)S(1)} all-gather(f32[1,128,128]{2,1,0:T(8,128)S(1)} %constant_dynamic-slice_fusion), channel_id=1, replica_groups=mesh['leaf'=4,'row'=8,'col'=4] {'row'}, dimensions={1}, use_global_device_ids=true | all-gather | bytes 589824 | tf_op jit(solution)/shard_map/all_gather | solution.py:304
  121.1 2.2 convolution_bitcast_fusion.x_ref
  123.4 9.2 %shard_map.69 = f32[1,64,128]{2,1,0:T(8,128)} custom-call(f32[1,512,128]{2,1,0:T(8,128)} %convolution_bitcast_fusion.x_ref), custom_call_target="tpu_custom_call" | custom-call | tf_op jit(solution)/shard_map/pallas_call | solution.py:205
  134.0 2.1 fusion.16
  142.0 18.0 %shard_map.70.low_ref = f32[2,1024,128]{2,1,0:T(8,128)} custom-call(f32[2,128,128]{2,1,0:T(8,128)} %pad_maximum_fusion.1.x_ref), custom_call_target="tpu_custom_call" | custom-call | tf_op jit(solution)/shard_map/pallas_call | solution.py:268
  160.0 2.3 slice.93.fac_ref
  162.3 24.8 %all-gather.8.cloned.1.call-done = f32[32,192,128]{2,1,0:T(8,128)} async-done(((f32[1,192,128]{2,1,0:T(8,128)}), f32[32,192,128]{2,1,0:T(8,128)}) %all-gather.8.cloned.1.call-update) | async-done | bytes 3145744 | tf_op jit(solution)/shard_map/all_gather | solution.py:347
  187.2 4.6 %shard_map.71 = (f32[2,128,128]{2,1,0:T(8,128)}, f32[2,64,128]{2,1,0:T(8,128)}) custom-call(s32[20]{0:T(128)} %pad_add_fusion.info_ref, f32[8,4,1,192,128]{4,3,2,1,0:T(8,128)} %bitcast.69, f32[2,1024,128]{2,1,0:T(8,128)} %shard_map.70.low_ref, f32[2,1024,128]{2,1,0:T(8,128)} %slice.93.fac_ref), custom_call_target="tpu_custom_call" | custom-call | tf_op jit(solution)/shard_map/pallas_call | solution.py:123
  191.8 2.9 fusion.17.x_ref
  194.7 12.7 %shard_map.72 = f32[2,64,128]{2,1,0:T(8,128)} custom-call(f32[2,512,128]{2,1,0:T(8,128)} %fusion.17.x_ref), custom_call_target="tpu_custom_call" | custom-call | tf_op jit(solution)/shard_map/pallas_call | solution.py:205
  209.7 3.0 slice.95.fac_ref
  214.8 39.6 %all-gather.10.cloned.1.call-done = f32[64,128,128]{2,1,0:T(8,128)} async-done(((f32[2,128,128]{2,1,0:T(8,128)}), f32[64,128,128]{2,1,0:T(8,128)}) %all-gather.10.cloned.1.call-update) | async-done | bytes 4194320 | tf_op jit(solution)/shard_map/all_gather | solution.py:347
  256.2 7.0 %shard_map.73 = f32[4,128,128]{2,1,0:T(8,128)} custom-call(s32[38]{0:T(128)} %pad_add_fusion.1.info_ref, f32[8,4,2,128,128]{4,3,2,1,0:T(8,128)} %bitcast.73, f32[8,4,1,192,128]{4,3,2,1,0:T(8,128)} %bitcast.71, f32[4,1024,128]{2,1,0:T(8,128)} %slice.95.fac_ref), custom_call_target="tpu_custom_call" | custom-call | tf_op jit(solution)/shard_map/pallas_call | solution.py:123
  263.2 3.1 %fusion.18 = f32[4,512,128]{2,1,0:T(8,128)S(1)} fusion(f32[7,128,512]{2,1,0:T(8,128)} %copy-done.1, f32[4,128,128]{2,1,0:T(8,128)} %shard_map.73), kind=kOutput, calls=%fused_computation.69 | convolution fusion | flops 402653184 | bytes 3145728 | tf_op jit(solution)/shard_map/dot_general | solution.py:15
  267.3 32.4 %shard_map.74 = f32[4,512,128]{2,1,0:T(8,128)} custom-call(f32[4,512,128]{2,1,0:T(8,128)} %copy-done.2), custom_call_target="tpu_custom_call" | custom-call | tf_op jit(solution)/shard_map/pallas_call | solution.py:205
  299.8 2.7 maximum_bitcast_fusion
  (84 shorter events, 24.7 us)
Async XLA Ops:
  8.0 1.5 copy-start
  8.0 124.6 %reduce-scatter.2.cloned.1.call-start = ((), (), s32[]{:S(2)}) async-start(), calls=%async_computation.1 | async-start | bytes 1146880 | tf_op jit(solution)/shard_map/reduce_scatter | solution.py:312
  9.5 2.3 copy-start.5
  11.8 122.3 %all-gather.6.cloned.1.call-start = ((), (), s32[]{:S(2)}) async-start(), calls=%async_computation.2 | async-start | bytes 3538944 | tf_op jit(solution)/shard_map/all_gather | solution.py:305
  14.7 55.7 %copy-start.10 = (s32[1,6,8]{2,0,1:T(1,128)S(1)}, s32[1,6,8]{2,0,1:T(1,128)}, u32[]{:S(2)}) copy-start(s32[1,6,8]{2,0,1:T(1,128)} %param.10) | copy-start | bytes 580
  70.8 3.9 %copy-start.9 = (f32[32,256]{1,0:T(8,128)S(1)}, f32[32,256]{1,0:T(8,128)}, u32[]{:S(2)}) copy-start(f32[32,256]{1,0:T(8,128)} %param.7) | copy-start | bytes 98308
  72.6 1.2 copy-start.1
  74.6 112.6 %all-gather.8.cloned.1.call-start = ((), (), s32[]{:S(2)}) async-start(), calls=%async_computation.3 | async-start | bytes 3244032 | tf_op jit(solution)/shard_map/all_gather | solution.py:347
  84.5 35.2 %collective-permute-start.3 = (f32[32,1024]{1,0:T(8,128)S(1)}, f32[32,1024]{1,0:T(8,128)S(1)}, u32[]{:S(2)}, u32[]{:S(2)}) collective-permute-start(f32[32,1024]{1,0:T(8,128)S(1)} %all_gather.21), channel_id=1, source_target_pairs={{0,96},{1,97},{2,98},{3,99},{4,0},{5,1},{6,2},{7,3},{8,32},{9,33},... | collective-permute-start | bytes 393224 | tf_op jit(solution)/shard_map/ppermute | solution.py:331
  91.5 28.2 %collective-permute-start.2 = (f32[32,1024]{1,0:T(8,128)S(1)}, f32[32,1024]{1,0:T(8,128)S(1)}, u32[]{:S(2)}, u32[]{:S(2)}) collective-permute-start(f32[32,1024]{1,0:T(8,128)S(1)} %all_gather.21), channel_id=1, source_target_pairs={{0,64},{1,65},{2,66},{3,67},{4,96},{5,97},{6,98},{7,99},{8,0},{9,1... | collective-permute-start | bytes 393224 | tf_op jit(solution)/shard_map/ppermute | solution.py:331
  98.3 21.5 %collective-permute-start.1 = (f32[32,1024]{1,0:T(8,128)S(1)}, f32[32,1024]{1,0:T(8,128)S(1)}, u32[]{:S(2)}, u32[]{:S(2)}) collective-permute-start(f32[32,1024]{1,0:T(8,128)S(1)} %all_gather.21), channel_id=1, source_target_pairs={{0,32},{1,33},{2,34},{3,35},{4,64},{5,65},{6,66},{7,67},{8,96},{9,... | collective-permute-start | bytes 393224 | tf_op jit(solution)/shard_map/ppermute | solution.py:331
  100.9 18.8 %collective-permute-start = (f32[32,1024]{1,0:T(8,128)S(1)}, f32[32,1024]{1,0:T(8,128)S(1)}, u32[]{:S(2)}, u32[]{:S(2)}) collective-permute-start(f32[32,1024]{1,0:T(8,128)S(1)} %all_gather.21), channel_id=1, source_target_pairs={{0,0},{1,1},{2,2},{3,3},{4,32},{5,33},{6,34},{7,35},{8,64},{9,65},... | collective-permute-start | bytes 393224 | tf_op jit(solution)/shard_map/ppermute | solution.py:331
  139.1 1.5 copy-start.7
  141.2 113.2 %all-gather.10.cloned.1.call-start = ((), (), s32[]{:S(2)}) async-start(), calls=%async_computation.4 | async-start | bytes 4325376 | tf_op jit(solution)/shard_map/all_gather | solution.py:347
  191.8 16.5 %copy-start.8 = (f32[2,64,128]{2,1,0:T(8,128)S(1)}, f32[2,64,128]{2,1,0:T(8,128)}, u32[]{:S(2)}) copy-start(f32[2,64,128]{2,1,0:T(8,128)} %get-tuple-element.14) | copy-start | bytes 196612
  191.8 17.3 %copy-start.11 = (s32[1,4]{1,0:T(1,128)S(1)}, s32[1,4]{1,0:T(1,128)}, u32[]{:S(2)}) copy-start(s32[1,4]{1,0:T(1,128)} %param.11) | copy-start | bytes 52
  263.2 3.1 %copy-start.6 = (f32[7,64,128]{2,1,0:T(8,128)S(1)}, f32[7,64,128]{2,1,0:T(8,128)}, u32[]{:S(2)}) copy-start(f32[7,64,128]{2,1,0:T(8,128)} %reduce-scatter.2.cloned.1.call-done) | copy-start | bytes 688132
  266.4 1.0 copy-start.2
  299.8 2.7 copy-start.3
  299.8 2.7 copy-start.4
Sparse Core Ops, SparseCore 0:
  11.9 39.2 reduce-scatter.1
  141.3 45.7 all-gather.7
  209.1 45.2 all-gather.9
Sparse Core Ops, SparseCore 1:
  74.7 36.9 all-gather.5

commit v15 on v12

--- a/solution.py
+++ b/solution.py
@@ -275,6 +275,110 @@
     )(x)
 
 
+def pair_reduce_kernel(x_ref, out_ref, recv_a, recv_b, sems, *, band, chips):
+    r = lax.axis_index("row")
+    leaf = lax.axis_index("leaf")
+    c = lax.axis_index("col")
+    core = lax.rem(r, 2)
+    chip = r // 2
+    partner = r + 1 - 2 * core
+    half = band * chips
+    mesh_ids = pl.DeviceIdType.MESH
+    peers = [2 * lax.rem(chip + d, chips) + core for d in range(1, chips)]
+
+    barrier = pltpu.get_barrier_semaphore()
+    for peer in [partner] + peers:
+        pl.semaphore_signal(barrier, inc=1, device_id=(leaf, peer, c), device_id_type=mesh_ids)
+    pl.semaphore_wait(barrier, chips)
+
+    def rows(start, size):
+        return pl.ds(pl.multiple_of(start, band), size)
+
+    mine = rows(core * half, half)
+    theirs = rows((1 - core) * half, half)
+    copy = pltpu.make_async_remote_copy(
+        src_ref=x_ref.at[:, theirs, :], dst_ref=recv_a, send_sem=sems.at[0, 0], recv_sem=sems.at[1, 0],
+        device_id=(leaf, partner, c), device_id_type=mesh_ids,
+    )
+    copy.start()
+    copy.wait_recv()
+    copy.wait_send()
+    recv_a[...] = recv_a[...] + x_ref[:, mine, :]
+
+    sends = []
+    for d in range(1, chips):
+        target = lax.rem(chip + d, chips)
+        copy = pltpu.make_async_remote_copy(
+            src_ref=recv_a.at[:, rows(target * band, band), :], dst_ref=recv_b.at[d - 1],
+            send_sem=sems.at[0, d], recv_sem=sems.at[1, d],
+            device_id=(leaf, 2 * target + core, c), device_id_type=mesh_ids,
+        )
+        copy.start()
+        sends.append(copy)
+    for copy in sends:
+        copy.wait_recv()
+    for copy in sends:
+        copy.wait_send()
+    total = recv_a[:, rows(chip * band, band), :]
+    for d in range(1, chips):
+        total = total + recv_b[d - 1]
+    own = rows(core * half + chip * band, band)
+    out_ref[:, own, :] = total
+
+    sends = []
+    for d in range(1, chips):
+        target = lax.rem(chip + d, chips)
+        copy = pltpu.make_async_remote_copy(
+            src_ref=out_ref.at[:, own, :], dst_ref=out_ref.at[:, own, :],
+            send_sem=sems.at[2, d - 1], recv_sem=sems.at[3, d - 1],
+            device_id=(leaf, 2 * target + core, c), device_id_type=mesh_ids,
+        )
+        copy.start()
+        sends.append(copy)
+    for d in range(1, chips):
+        source = lax.rem(chip + chips - d, chips)
+        part = rows(core * half + source * band, band)
+        pltpu.make_async_remote_copy(
+            src_ref=out_ref.at[:, part, :], dst_ref=out_ref.at[:, part, :],
+            send_sem=sems.at[2, d - 1], recv_sem=sems.at[3, d - 1],
+            device_id=(leaf, 2 * source + core, c), device_id_type=mesh_ids,
+        ).wait_recv()
+    for copy in sends:
+        copy.wait_send()
+
+    copy = pltpu.make_async_remote_copy(
+        src_ref=out_ref.at[:, mine, :], dst_ref=out_ref.at[:, mine, :],
+        send_sem=sems.at[2, chips - 1], recv_sem=sems.at[3, chips - 1],
+        device_id=(leaf, partner, c), device_id_type=mesh_ids,
+    )
+    copy.start()
+    pltpu.make_async_remote_copy(
+        src_ref=out_ref.at[:, theirs, :], dst_ref=out_ref.at[:, theirs, :],
+        send_sem=sems.at[2, chips - 1], recv_sem=sems.at[3, chips - 1],
+        device_id=(leaf, partner, c), device_id_type=mesh_ids,
+    ).wait_recv()
+    copy.wait_send()
+
+
+def pair_reduce(x, row_count, collective_id):
+    lead, total_rows, last = x.shape
+    chips = row_count // 2
+    band = total_rows // row_count
+    vmem = pl.BlockSpec(memory_space=pltpu.VMEM)
+    return pl.pallas_call(
+        functools.partial(pair_reduce_kernel, band=band, chips=chips),
+        out_shape=jax.ShapeDtypeStruct(x.shape, x.dtype),
+        in_specs=[vmem],
+        out_specs=vmem,
+        scratch_shapes=[
+            pltpu.VMEM((lead, band * chips, last), x.dtype),
+            pltpu.VMEM((chips - 1, lead, band, last), x.dtype),
+            pltpu.SemaphoreType.DMA((4, chips)),
+        ],
+        compiler_params=pltpu.CompilerParams(collective_id=collective_id, has_side_effects=True),
+    )(x)
+
+
 def body(sigma_top, panels, inverse_diag, slot_lists, parent_links):
     tile = TILE
     row_count = lax.axis_size("row")
@@ -396,7 +500,7 @@
     count_2 = product_2.shape[0]
     gram_rows = jnp.zeros((count_2, width, tile), jnp.float32)
     gram_rows = lax.dynamic_update_slice_in_dim(gram_rows, gram_piece[first_2:first_2 + count_2], r * band, 1)
-    diag_2 = axis_reduce(diag_partial(first_2, product_2) + gram_rows, "row", row_count, True, 2)
+    diag_2 = pair_reduce(diag_partial(first_2, product_2) + gram_rows, row_count, 2)
 
     products = jnp.concatenate([product_0[None], product_1, product_2], axis=0)
     diag_cols = jnp.concatenate(

time: 297 us -> 291 us (0.980)
  Pallas kernels: 132 us -> 126 us
    pallas_call x4 -> x3, Pallas kernels: 102 us -> 69.4 us  [axis_reduce(): pl.pallas_call(kernel, out_shape=jax.ShapeDtypeStruct((lead, out_rows, la...]
    pallas_call x0 -> x1, Pallas kernels: none -> 26.5 us  [pair_reduce(): pl.pallas_call(functools.partial(pair_reduce_kernel, band=band, chips=chi...]
where the time goes in v15:
time: 291 us; the launch traced here: 290 us
  Pallas kernels  126 us (43%)
  waiting for transfers between devices  72 us (25%)
  starting transfers between devices  18.5 us (6%)
  local copies, waits for them, and re-layouts  17.8 us (6%)
  matrix products  17.3 us (6%)
  between operations  16 us (5%)
  other arithmetic  13 us (4%)
  blocking collectives  9.78 us (3%)
    pallas_call x3, Pallas kernels, axis_reduce(): pl.pallas_call(kernel, out_shape=jax.ShapeDtypeStruct((lead, out_rows, la...  69.4 us
    all_gather x2, waiting for transfers between devices, reduce_and_gather(): everything = lax.all_gather(both, ('row', 'col'), axis=0)  65.9 us
    pallas_call x1, Pallas kernels, pair_reduce(): pl.pallas_call(functools.partial(pair_reduce_kernel, band=band, chips=chi...  26.5 us
    ppermute x4, starting transfers between devices, body(): rounds.append(lax.ppermute(chunk_rows, ('leaf', 'row', 'col'), pairs))  18.3 us
    pallas_call x1, Pallas kernels, axis_gather(): pl.pallas_call(functools.partial(gather_kernel, axis=axis, count=count, b...  18 us
    dot_general x8, matrix products, mm(): jnp.matmul(a, b, precision=HIGHEST, preferred_element_type=jnp.float32)  17.3 us
    pallas_call x2, Pallas kernels, level_products(): pl.pallas_call(kernel, out_shape=tuple(shapes), in_specs=[pl.BlockSpec(me...  11.7 us
    all_gather x1, blocking collectives, body(): chunk_rows = lax.all_gather(sigma_top, 'col', axis=1, tiled=True)  9.78 us
  transfers between devices with their start and end apart: 8, of which 5 were waited for; matrix products, arithmetic and copies ran while one was open for 8% of the time, Pallas kernels for 9%

profile of v15, /device:TPU:1, one launch (start us, length us, event | category | flops | bytes accessed | tf_op | source)
XLA Modules:
  0.0 289.9 jit_solution(2230663661737751730)
XLA Ops:
  9.5 3.9 %fusion.2.x_ref = f32[7,128,512]{2,1,0:T(8,128)} fusion(f32[1,7,128,512]{3,2,1,0:T(8,128)S(1)} %copy-done, f32[1,7,128,128]{3,2,1,0:T(8,128)} %param.8), kind=kOutput, calls=%fused_computation.6 | convolution fusion | flops 704643072 | bytes 4128768 | tf_op jit(solution)/shard_map/dot_general | solution.py:15
  13.4 48.4 %shard_map.68 = f32[7,128,512]{2,1,0:T(8,128)} custom-call(f32[7,128,512]{2,1,0:T(8,128)} %fusion.2.x_ref), custom_call_target="tpu_custom_call" | custom-call | tf_op jit(solution)/shard_map/pallas_call | solution.py:205
  65.8 9.8 %all_gather.18 = f32[32,1024]{1,0:T(8,128)S(1)} all-gather(f32[32,256]{1,0:T(8,128)S(1)} %copy-done.8), channel_id=1, replica_groups=mesh['leaf'=4,'row'=8,'col'=4] {'col'}, dimensions={1}, use_global_device_ids=true | all-gather | bytes 163840 | tf_op jit(solution)/shard_map/all_gather | solution.py:414
  75.6 7.0 %collective-permute-start.3 = (f32[32,1024]{1,0:T(8,128)S(1)}, f32[32,1024]{1,0:T(8,128)S(1)}, u32[]{:S(2)}, u32[]{:S(2)}) collective-permute-start(f32[32,1024]{1,0:T(8,128)S(1)} %all_gather.18), channel_id=1, source_target_pairs={{0,96},{1,97},{2,98},{3,99},{4,0},{5,1},{6,2},{7,3},{8,32},{9,33},... | collective-permute-start | bytes 393224 | tf_op jit(solution)/shard_map/ppermute | solution.py:429
  82.6 6.7 %collective-permute-start.2 = (f32[32,1024]{1,0:T(8,128)S(1)}, f32[32,1024]{1,0:T(8,128)S(1)}, u32[]{:S(2)}, u32[]{:S(2)}) collective-permute-start(f32[32,1024]{1,0:T(8,128)S(1)} %all_gather.18), channel_id=1, source_target_pairs={{0,64},{1,65},{2,66},{3,67},{4,96},{5,97},{6,98},{7,99},{8,0},{9,1... | collective-permute-start | bytes 393224 | tf_op jit(solution)/shard_map/ppermute | solution.py:429
  89.3 2.7 collective-permute-start.1
  92.0 1.9 collective-permute-start
  93.9 2.2 fusion
  101.8 2.6 all-gather.6.cloned.1.call-done
  106.1 2.2 convolution_bitcast_fusion.x_ref
  108.4 9.1 %shard_map.69 = f32[1,64,128]{2,1,0:T(8,128)} custom-call(f32[1,512,128]{2,1,0:T(8,128)} %convolution_bitcast_fusion.x_ref), custom_call_target="tpu_custom_call" | custom-call | tf_op jit(solution)/shard_map/pallas_call | solution.py:205
  117.5 2.1 fusion.15
  126.1 18.0 %shard_map.70.low_ref = f32[2,1024,128]{2,1,0:T(8,128)} custom-call(f32[2,128,128]{2,1,0:T(8,128)} %pad_maximum_fusion.1.x_ref), custom_call_target="tpu_custom_call" | custom-call | tf_op jit(solution)/shard_map/pallas_call | solution.py:268
  144.1 2.3 slice.90.fac_ref
  146.4 25.7 %all-gather.8.cloned.1.call-done = f32[32,192,128]{2,1,0:T(8,128)} async-done(((f32[1,192,128]{2,1,0:T(8,128)}), f32[32,192,128]{2,1,0:T(8,128)}) %all-gather.8.cloned.1.call-update) | async-done | bytes 3145744 | tf_op jit(solution)/shard_map/all_gather | solution.py:445
  172.2 4.6 %shard_map.71 = (f32[2,128,128]{2,1,0:T(8,128)}, f32[2,64,128]{2,1,0:T(8,128)}) custom-call(s32[20]{0:T(128)} %pad_add_fusion.info_ref, f32[8,4,1,192,128]{4,3,2,1,0:T(8,128)} %bitcast.69, f32[2,1024,128]{2,1,0:T(8,128)} %shard_map.70.low_ref, f32[2,1024,128]{2,1,0:T(8,128)} %slice.90.fac_ref), custom_call_target="tpu_custom_call" | custom-call | tf_op jit(solution)/shard_map/pallas_call | solution.py:123
  176.8 2.9 fusion.16.x_ref
  179.7 12.0 %shard_map.72 = f32[2,64,128]{2,1,0:T(8,128)} custom-call(f32[2,512,128]{2,1,0:T(8,128)} %fusion.16.x_ref), custom_call_target="tpu_custom_call" | custom-call | tf_op jit(solution)/shard_map/pallas_call | solution.py:205
  194.0 3.1 %slice.92.fac_ref = f32[4,1024,128]{2,1,0:T(8,128)} slice(f32[7,1024,128]{2,1,0:T(8,128)} %all-gather.6.cloned.1.call-done), slice={[3:7], [0:1024], [0:128]} | slice | bytes 4194304 | tf_op jit(solution)/shard_map/slice | solution.py:496
  199.1 40.2 %all-gather.10.cloned.1.call-done = f32[64,128,128]{2,1,0:T(8,128)} async-done(((f32[2,128,128]{2,1,0:T(8,128)}), f32[64,128,128]{2,1,0:T(8,128)}) %all-gather.10.cloned.1.call-update) | async-done | bytes 4194320 | tf_op jit(solution)/shard_map/all_gather | solution.py:445
  241.1 7.0 %shard_map.73 = f32[4,128,128]{2,1,0:T(8,128)} custom-call(s32[38]{0:T(128)} %pad_add_fusion.1.info_ref, f32[8,4,2,128,128]{4,3,2,1,0:T(8,128)} %bitcast.73, f32[8,4,1,192,128]{4,3,2,1,0:T(8,128)} %bitcast.71, f32[4,1024,128]{2,1,0:T(8,128)} %slice.92.fac_ref), custom_call_target="tpu_custom_call" | custom-call | tf_op jit(solution)/shard_map/pallas_call | solution.py:123
  248.1 3.1 %fusion.17 = f32[4,512,128]{2,1,0:T(8,128)S(1)} fusion(f32[7,128,512]{2,1,0:T(8,128)} %copy-done.1, f32[4,128,128]{2,1,0:T(8,128)} %shard_map.73), kind=kOutput, calls=%fused_computation.68 | convolution fusion | flops 402653184 | bytes 3145728 | tf_op jit(solution)/shard_map/dot_general | solution.py:15
  252.2 26.5 %shard_map.74 = f32[4,512,128]{2,1,0:T(8,128)} custom-call(f32[4,512,128]{2,1,0:T(8,128)} %copy-done.2), custom_call_target="tpu_custom_call" | custom-call | tf_op jit(solution)/shard_map/pallas_call | solution.py:368
  278.8 2.7 maximum_bitcast_fusion
  (80 shorter events, 27.2 us)
Async XLA Ops:
  8.0 1.5 copy-start
  8.0 96.4 %all-gather.6.cloned.1.call-start = ((), (), s32[]{:S(2)}) async-start(), calls=%async_computation.1 | async-start | bytes 4128768 | tf_op jit(solution)/shard_map/all_gather | solution.py:406
  61.8 3.9 %copy-start.8 = (f32[32,256]{1,0:T(8,128)S(1)}, f32[32,256]{1,0:T(8,128)}, u32[]{:S(2)}) copy-start(f32[32,256]{1,0:T(8,128)} %param.7) | copy-start | bytes 98308
  63.6 1.2 copy-start.1
  65.7 58.3 %reduce-scatter.2.cloned.1.call-start = ((), (), s32[]{:S(2)}) async-start(), calls=%async_computation.2 | async-start | bytes 1146880 | tf_op jit(solution)/shard_map/reduce_scatter | solution.py:410
  75.6 22.1 %collective-permute-start.3 = (f32[32,1024]{1,0:T(8,128)S(1)}, f32[32,1024]{1,0:T(8,128)S(1)}, u32[]{:S(2)}, u32[]{:S(2)}) collective-permute-start(f32[32,1024]{1,0:T(8,128)S(1)} %all_gather.18), channel_id=1, source_target_pairs={{0,96},{1,97},{2,98},{3,99},{4,0},{5,1},{6,2},{7,3},{8,32},{9,33},... | collective-permute-start | bytes 393224 | tf_op jit(solution)/shard_map/ppermute | solution.py:429
  82.6 15.1 %collective-permute-start.2 = (f32[32,1024]{1,0:T(8,128)S(1)}, f32[32,1024]{1,0:T(8,128)S(1)}, u32[]{:S(2)}, u32[]{:S(2)}) collective-permute-start(f32[32,1024]{1,0:T(8,128)S(1)} %all_gather.18), channel_id=1, source_target_pairs={{0,64},{1,65},{2,66},{3,67},{4,96},{5,97},{6,98},{7,99},{8,0},{9,1... | collective-permute-start | bytes 393224 | tf_op jit(solution)/shard_map/ppermute | solution.py:429
  89.3 10.2 %collective-permute-start.1 = (f32[32,1024]{1,0:T(8,128)S(1)}, f32[32,1024]{1,0:T(8,128)S(1)}, u32[]{:S(2)}, u32[]{:S(2)}) collective-permute-start(f32[32,1024]{1,0:T(8,128)S(1)} %all_gather.18), channel_id=1, source_target_pairs={{0,32},{1,33},{2,34},{3,35},{4,64},{5,65},{6,66},{7,67},{8,96},{9,... | collective-permute-start | bytes 393224 | tf_op jit(solution)/shard_map/ppermute | solution.py:429
  92.0 9.1 %collective-permute-start = (f32[32,1024]{1,0:T(8,128)S(1)}, f32[32,1024]{1,0:T(8,128)S(1)}, u32[]{:S(2)}, u32[]{:S(2)}) collective-permute-start(f32[32,1024]{1,0:T(8,128)S(1)} %all_gather.18), channel_id=1, source_target_pairs={{0,0},{1,1},{2,2},{3,3},{4,32},{5,33},{6,34},{7,35},{8,64},{9,65},... | collective-permute-start | bytes 393224 | tf_op jit(solution)/shard_map/ppermute | solution.py:429
  93.9 2.3 copy-start.9
  96.2 76.0 %all-gather.8.cloned.1.call-start = ((), (), s32[]{:S(2)}) async-start(), calls=%async_computation.3 | async-start | bytes 3244032 | tf_op jit(solution)/shard_map/all_gather | solution.py:445
  121.9 2.1 copy-start.6
  125.4 113.9 %all-gather.10.cloned.1.call-start = ((), (), s32[]{:S(2)}) async-start(), calls=%async_computation.4 | async-start | bytes 4325376 | tf_op jit(solution)/shard_map/all_gather | solution.py:445
  176.8 15.7 %copy-start.7 = (f32[2,64,128]{2,1,0:T(8,128)S(1)}, f32[2,64,128]{2,1,0:T(8,128)}, u32[]{:S(2)}) copy-start(f32[2,64,128]{2,1,0:T(8,128)} %get-tuple-element.14) | copy-start | bytes 196612
  176.8 16.6 %copy-start.10 = (s32[1,4]{1,0:T(1,128)S(1)}, s32[1,4]{1,0:T(1,128)}, u32[]{:S(2)}) copy-start(s32[1,4]{1,0:T(1,128)} %param.11) | copy-start | bytes 52
  248.1 3.1 %copy-start.5 = (f32[7,64,128]{2,1,0:T(8,128)S(1)}, f32[7,64,128]{2,1,0:T(8,128)}, u32[]{:S(2)}) copy-start(f32[7,64,128]{2,1,0:T(8,128)} %reduce-scatter.2.cloned.1.call-done) | copy-start | bytes 688132
  251.3 1.0 copy-start.2
  278.8 2.7 copy-start.3
  278.8 2.7 copy-start.4
Sparse Core Ops, SparseCore 0:
  65.8 38.5 all-gather.5
Sparse Core Ops, SparseCore 1:
  96.3 22.2 reduce-scatter.1
  125.5 46.6 all-gather.7
  193.3 45.9 all-gather.9

commit v16 on v15

--- a/solution.py
+++ b/solution.py
@@ -379,6 +379,69 @@
     )(x)
 
 
+def pair_scatter_kernel(x_ref, out_ref, recv_a, recv_b, sems, *, chips):
+    r = lax.axis_index("row")
+    leaf = lax.axis_index("leaf")
+    c = lax.axis_index("col")
+    core = lax.rem(r, 2)
+    chip = r // 2
+    partner = r + 1 - 2 * core
+    mesh_ids = pl.DeviceIdType.MESH
+    peers = [2 * lax.rem(chip + d, chips) + core for d in range(1, chips)]
+
+    barrier = pltpu.get_barrier_semaphore()
+    for peer in [partner] + peers:
+        pl.semaphore_signal(barrier, inc=1, device_id=(leaf, peer, c), device_id_type=mesh_ids)
+    pl.semaphore_wait(barrier, chips)
+
+    copy = pltpu.make_async_remote_copy(
+        src_ref=x_ref.at[:, :, 1 - core], dst_ref=recv_a, send_sem=sems.at[0, 0], recv_sem=sems.at[1, 0],
+        device_id=(leaf, partner, c), device_id_type=mesh_ids,
+    )
+    copy.start()
+    copy.wait_recv()
+    copy.wait_send()
+    recv_a[...] = recv_a[...] + x_ref[:, :, core]
+
+    sends = []
+    for d in range(1, chips):
+        target = lax.rem(chip + d, chips)
+        copy = pltpu.make_async_remote_copy(
+            src_ref=recv_a.at[:, target], dst_ref=recv_b.at[d - 1],
+            send_sem=sems.at[0, d], recv_sem=sems.at[1, d],
+            device_id=(leaf, 2 * target + core, c), device_id_type=mesh_ids,
+        )
+        copy.start()
+        sends.append(copy)
+    for copy in sends:
+        copy.wait_recv()
+    for copy in sends:
+        copy.wait_send()
+    total = recv_a[:, chip]
+    for d in range(1, chips):
+        total = total + recv_b[d - 1]
+    out_ref[...] = total
+
+
+def pair_scatter(x, row_count, collective_id):
+    lead, total_rows, last = x.shape
+    chips = row_count // 2
+    band = total_rows // row_count
+    vmem = pl.BlockSpec(memory_space=pltpu.VMEM)
+    return pl.pallas_call(
+        functools.partial(pair_scatter_kernel, chips=chips),
+        out_shape=jax.ShapeDtypeStruct((lead, band, last), x.dtype),
+        in_specs=[vmem],
+        out_specs=vmem,
+        scratch_shapes=[
+            pltpu.VMEM((lead, chips, band, last), x.dtype),
+            pltpu.VMEM((chips - 1, lead, band, last), x.dtype),
+            pltpu.SemaphoreType.DMA((2, chips)),
+        ],
+        compiler_params=pltpu.CompilerParams(collective_id=collective_id, has_side_effects=True),
+    )(x.reshape(lead, chips, 2, band, last))
+
+
 def body(sigma_top, panels, inverse_diag, slot_lists, parent_links):
     tile = TILE
     row_count = lax.axis_size("row")
@@ -436,7 +499,7 @@
 
     def reduce_and_gather(first, products, sent, extra, tied=None):
         count = products.shape[0]
-        piece = axis_reduce(diag_partial(first, products), "row", row_count, False, first)
+        piece = pair_scatter(diag_partial(first, products), row_count, first)
         piece = piece + gram_piece[first:first + count]
         if tied is not None:
             piece, tied = lax.optimization_barrier((piece, tied))

time: 291 us -> 289 us (level)
    pallas_call x3 -> x1, Pallas kernels: 69.4 us -> 48.4 us  [axis_reduce(): pl.pallas_call(kernel, out_shape=jax.ShapeDtypeStruct((lead, out_rows, la...]
    pallas_call x0 -> x2, Pallas kernels: none -> 19 us  [pair_scatter(): pl.pallas_call(functools.partial(pair_scatter_kernel, chips=chips), out_s...]
where the time goes in v16:
time: 289 us; the launch traced here: 288 us
  Pallas kernels  124 us (43%)
  waiting for transfers between devices  71.5 us (25%)
  local copies, waits for them, and re-layouts  18.9 us (7%)
  starting transfers between devices  18.5 us (6%)
  matrix products  16.1 us (6%)
  between operations  16 us (6%)
  other arithmetic  13 us (4%)
  blocking collectives  9.78 us (3%)
    all_gather x2, waiting for transfers between devices, reduce_and_gather(): everything = lax.all_gather(both, ('row', 'col'), axis=0)  66.5 us
    pallas_call x1, Pallas kernels, axis_reduce(): pl.pallas_call(kernel, out_shape=jax.ShapeDtypeStruct((lead, out_rows, la...  48.4 us
    pallas_call x1, Pallas kernels, pair_reduce(): pl.pallas_call(functools.partial(pair_reduce_kernel, band=band, chips=chi...  26.5 us
    pallas_call x2, Pallas kernels, pair_scatter(): pl.pallas_call(functools.partial(pair_scatter_kernel, chips=chips), out_s...  19 us
    pallas_call x1, Pallas kernels, axis_gather(): pl.pallas_call(functools.partial(gather_kernel, axis=axis, count=count, b...  18.3 us
    ppermute x4, starting transfers between devices, body(): rounds.append(lax.ppermute(chunk_rows, ('leaf', 'row', 'col'), pairs))  18.3 us
    dot_general x8, matrix products, mm(): jnp.matmul(a, b, precision=HIGHEST, preferred_element_type=jnp.float32)  16.1 us
    pallas_call x2, Pallas kernels, level_products(): pl.pallas_call(kernel, out_shape=tuple(shapes), in_specs=[pl.BlockSpec(me...  11.7 us
  transfers between devices with their start and end apart: 8, of which 5 were waited for; matrix products, arithmetic and copies ran while one was open for 8% of the time, Pallas kernels for 9%

profile of v16, /device:TPU:1, one launch (start us, length us, event | category | flops | bytes accessed | tf_op | source)
XLA Modules:
  0.0 287.6 jit_solution(12429463093401190700)
XLA Ops:
  9.5 3.9 %fusion.2.x_ref = f32[7,128,512]{2,1,0:T(8,128)} fusion(f32[1,7,128,512]{3,2,1,0:T(8,128)S(1)} %copy-done, f32[1,7,128,128]{3,2,1,0:T(8,128)} %param.8), kind=kOutput, calls=%fused_computation.6 | convolution fusion | flops 704643072 | bytes 4128768 | tf_op jit(solution)/shard_map/dot_general | solution.py:15
  13.4 48.4 %shard_map.68 = f32[7,128,512]{2,1,0:T(8,128)} custom-call(f32[7,128,512]{2,1,0:T(8,128)} %fusion.2.x_ref), custom_call_target="tpu_custom_call" | custom-call | tf_op jit(solution)/shard_map/pallas_call | solution.py:205
  61.8 1.8 broadcast_multiply_fusion
  65.8 9.8 %all_gather.18 = f32[32,1024]{1,0:T(8,128)S(1)} all-gather(f32[32,256]{1,0:T(8,128)S(1)} %copy-done.8), channel_id=1, replica_groups=mesh['leaf'=4,'row'=8,'col'=4] {'col'}, dimensions={1}, use_global_device_ids=true | all-gather | bytes 163840 | tf_op jit(solution)/shard_map/all_gather | solution.py:477
  75.6 7.0 %collective-permute-start.3 = (f32[32,1024]{1,0:T(8,128)S(1)}, f32[32,1024]{1,0:T(8,128)S(1)}, u32[]{:S(2)}, u32[]{:S(2)}) collective-permute-start(f32[32,1024]{1,0:T(8,128)S(1)} %all_gather.18), channel_id=1, source_target_pairs={{0,96},{1,97},{2,98},{3,99},{4,0},{5,1},{6,2},{7,3},{8,32},{9,33},... | collective-permute-start | bytes 393224 | tf_op jit(solution)/shard_map/ppermute | solution.py:492
  82.6 6.7 %collective-permute-start.2 = (f32[32,1024]{1,0:T(8,128)S(1)}, f32[32,1024]{1,0:T(8,128)S(1)}, u32[]{:S(2)}, u32[]{:S(2)}) collective-permute-start(f32[32,1024]{1,0:T(8,128)S(1)} %all_gather.18), channel_id=1, source_target_pairs={{0,64},{1,65},{2,66},{3,67},{4,96},{5,97},{6,98},{7,99},{8,0},{9,1... | collective-permute-start | bytes 393224 | tf_op jit(solution)/shard_map/ppermute | solution.py:492
  89.3 2.7 collective-permute-start.1
  92.0 1.9 collective-permute-start
  93.9 2.2 fusion
  101.8 2.6 all-gather.6.cloned.1.call-done
  107.2 8.6 %shard_map.69 = f32[1,64,128]{2,1,0:T(8,128)} custom-call(f32[1,4,2,64,128]{4,3,2,1,0:T(8,128)} %convolution_bitcast_fusion.x_ref), custom_call_target="tpu_custom_call" | custom-call | tf_op jit(solution)/shard_map/pallas_call | solution.py:431
  115.8 2.1 fusion.16
  124.5 18.3 %shard_map.70.low_ref = f32[2,1024,128]{2,1,0:T(8,128)} custom-call(f32[2,128,128]{2,1,0:T(8,128)} %pad_maximum_fusion.1.x_ref), custom_call_target="tpu_custom_call" | custom-call | tf_op jit(solution)/shard_map/pallas_call | solution.py:268
  142.9 2.3 slice.90.fac_ref
  145.2 25.7 %all-gather.8.cloned.1.call-done = f32[32,192,128]{2,1,0:T(8,128)} async-done(((f32[1,192,128]{2,1,0:T(8,128)}), f32[32,192,128]{2,1,0:T(8,128)}) %all-gather.8.cloned.1.call-update) | async-done | bytes 3145744 | tf_op jit(solution)/shard_map/all_gather | solution.py:508
  170.9 4.6 %shard_map.71 = (f32[2,128,128]{2,1,0:T(8,128)}, f32[2,64,128]{2,1,0:T(8,128)}) custom-call(s32[20]{0:T(128)} %pad_add_fusion.info_ref, f32[8,4,1,192,128]{4,3,2,1,0:T(8,128)} %bitcast.73, f32[2,1024,128]{2,1,0:T(8,128)} %shard_map.70.low_ref, f32[2,1024,128]{2,1,0:T(8,128)} %slice.90.fac_ref), custom_call_target="tpu_custom_call" | custom-call | tf_op jit(solution)/shard_map/pallas_call | solution.py:123
  175.6 2.9 fusion.17
  178.4 10.4 %shard_map.72 = f32[2,64,128]{2,1,0:T(8,128)} custom-call(f32[2,4,2,64,128]{4,3,2,1,0:T(8,128)} %bitcast.85), custom_call_target="tpu_custom_call" | custom-call | tf_op jit(solution)/shard_map/pallas_call | solution.py:431
  191.1 3.1 %slice.92.fac_ref = f32[4,1024,128]{2,1,0:T(8,128)} slice(f32[7,1024,128]{2,1,0:T(8,128)} %all-gather.6.cloned.1.call-done), slice={[3:7], [0:1024], [0:128]} | slice | bytes 4194304 | tf_op jit(solution)/shard_map/slice | solution.py:559
  196.2 40.8 %all-gather.10.cloned.1.call-done = f32[64,128,128]{2,1,0:T(8,128)} async-done(((f32[2,128,128]{2,1,0:T(8,128)}), f32[64,128,128]{2,1,0:T(8,128)}) %all-gather.10.cloned.1.call-update) | async-done | bytes 4194320 | tf_op jit(solution)/shard_map/all_gather | solution.py:508
  238.8 7.0 %shard_map.73 = f32[4,128,128]{2,1,0:T(8,128)} custom-call(s32[38]{0:T(128)} %pad_add_fusion.1.info_ref, f32[8,4,2,128,128]{4,3,2,1,0:T(8,128)} %bitcast.77, f32[8,4,1,192,128]{4,3,2,1,0:T(8,128)} %bitcast.75, f32[4,1024,128]{2,1,0:T(8,128)} %slice.92.fac_ref), custom_call_target="tpu_custom_call" | custom-call | tf_op jit(solution)/shard_map/pallas_call | solution.py:123
  245.8 3.1 %fusion.18 = f32[4,512,128]{2,1,0:T(8,128)S(1)} fusion(f32[7,128,512]{2,1,0:T(8,128)} %copy-done.1, f32[4,128,128]{2,1,0:T(8,128)} %shard_map.73), kind=kOutput, calls=%fused_computation.69 | convolution fusion | flops 402653184 | bytes 3145728 | tf_op jit(solution)/shard_map/dot_general | solution.py:15
  250.0 26.5 %shard_map.74 = f32[4,512,128]{2,1,0:T(8,128)} custom-call(f32[4,512,128]{2,1,0:T(8,128)} %copy-done.2), custom_call_target="tpu_custom_call" | custom-call | tf_op jit(solution)/shard_map/pallas_call | solution.py:368
  276.5 2.7 maximum_bitcast_fusion
  (82 shorter events, 26.5 us)
Async XLA Ops:
  8.0 1.5 copy-start
  8.0 96.4 %all-gather.6.cloned.1.call-start = ((), (), s32[]{:S(2)}) async-start(), calls=%async_computation.1 | async-start | bytes 4128768 | tf_op jit(solution)/shard_map/all_gather | solution.py:469
  61.8 3.9 %copy-start.8 = (f32[32,256]{1,0:T(8,128)S(1)}, f32[32,256]{1,0:T(8,128)}, u32[]{:S(2)}) copy-start(f32[32,256]{1,0:T(8,128)} %param.7) | copy-start | bytes 98308
  63.6 1.2 copy-start.1
  65.7 56.7 %reduce-scatter.2.cloned.1.call-start = ((), (), s32[]{:S(2)}) async-start(), calls=%async_computation.2 | async-start | bytes 1146880 | tf_op jit(solution)/shard_map/reduce_scatter | solution.py:473
  75.6 23.2 %collective-permute-start.3 = (f32[32,1024]{1,0:T(8,128)S(1)}, f32[32,1024]{1,0:T(8,128)S(1)}, u32[]{:S(2)}, u32[]{:S(2)}) collective-permute-start(f32[32,1024]{1,0:T(8,128)S(1)} %all_gather.18), channel_id=1, source_target_pairs={{0,96},{1,97},{2,98},{3,99},{4,0},{5,1},{6,2},{7,3},{8,32},{9,33},... | collective-permute-start | bytes 393224 | tf_op jit(solution)/shard_map/ppermute | solution.py:492
  82.6 16.2 %collective-permute-start.2 = (f32[32,1024]{1,0:T(8,128)S(1)}, f32[32,1024]{1,0:T(8,128)S(1)}, u32[]{:S(2)}, u32[]{:S(2)}) collective-permute-start(f32[32,1024]{1,0:T(8,128)S(1)} %all_gather.18), channel_id=1, source_target_pairs={{0,64},{1,65},{2,66},{3,67},{4,96},{5,97},{6,98},{7,99},{8,0},{9,1... | collective-permute-start | bytes 393224 | tf_op jit(solution)/shard_map/ppermute | solution.py:492
  89.3 10.2 %collective-permute-start.1 = (f32[32,1024]{1,0:T(8,128)S(1)}, f32[32,1024]{1,0:T(8,128)S(1)}, u32[]{:S(2)}, u32[]{:S(2)}) collective-permute-start(f32[32,1024]{1,0:T(8,128)S(1)} %all_gather.18), channel_id=1, source_target_pairs={{0,32},{1,33},{2,34},{3,35},{4,64},{5,65},{6,66},{7,67},{8,96},{9,... | collective-permute-start | bytes 393224 | tf_op jit(solution)/shard_map/ppermute | solution.py:492
  92.0 9.1 %collective-permute-start = (f32[32,1024]{1,0:T(8,128)S(1)}, f32[32,1024]{1,0:T(8,128)S(1)}, u32[]{:S(2)}, u32[]{:S(2)}) collective-permute-start(f32[32,1024]{1,0:T(8,128)S(1)} %all_gather.18), channel_id=1, source_target_pairs={{0,0},{1,1},{2,2},{3,3},{4,32},{5,33},{6,34},{7,35},{8,64},{9,65},... | collective-permute-start | bytes 393224 | tf_op jit(solution)/shard_map/ppermute | solution.py:492
  93.9 2.3 copy-start.9
  96.2 74.7 %all-gather.8.cloned.1.call-start = ((), (), s32[]{:S(2)}) async-start(), calls=%async_computation.3 | async-start | bytes 3244032 | tf_op jit(solution)/shard_map/all_gather | solution.py:508
  120.3 2.1 copy-start.6
  123.8 113.2 %all-gather.10.cloned.1.call-start = ((), (), s32[]{:S(2)}) async-start(), calls=%async_computation.4 | async-start | bytes 4325376 | tf_op jit(solution)/shard_map/all_gather | solution.py:508
  175.5 14.1 %copy-start.7 = (f32[2,64,128]{2,1,0:T(8,128)S(1)}, f32[2,64,128]{2,1,0:T(8,128)}, u32[]{:S(2)}) copy-start(f32[2,64,128]{2,1,0:T(8,128)} %get-tuple-element.14) | copy-start | bytes 196612
  175.5 14.9 %copy-start.10 = (s32[1,4]{1,0:T(1,128)S(1)}, s32[1,4]{1,0:T(1,128)}, u32[]{:S(2)}) copy-start(s32[1,4]{1,0:T(1,128)} %param.11) | copy-start | bytes 52
  245.8 3.1 %copy-start.5 = (f32[7,64,128]{2,1,0:T(8,128)S(1)}, f32[7,64,128]{2,1,0:T(8,128)}, u32[]{:S(2)}) copy-start(f32[7,64,128]{2,1,0:T(8,128)} %reduce-scatter.2.cloned.1.call-done) | copy-start | bytes 688132
  249.0 1.0 copy-start.2
  276.5 2.7 copy-start.3
  276.5 2.7 copy-start.4
Sparse Core Ops, SparseCore 0:
  65.8 38.5 all-gather.5
Sparse Core Ops, SparseCore 1:
  96.3 22.2 reduce-scatter.1
  123.9 47.0 all-gather.7
  190.5 46.5 all-gather.9

commit v17 on v16

--- a/solution.py
+++ b/solution.py
@@ -442,6 +442,81 @@
     )(x.reshape(lead, chips, 2, band, last))
 
 
+def pair_gather_kernel(x_ref, out_ref, sems, *, chips, rows):
+    r = lax.axis_index("row")
+    leaf = lax.axis_index("leaf")
+    c = lax.axis_index("col")
+    core = lax.rem(r, 2)
+    chip = r // 2
+    partner = r + 1 - 2 * core
+    mesh_ids = pl.DeviceIdType.MESH
+
+    def at(index):
+        return out_ref.at[:, pl.ds(pl.multiple_of(index * rows, rows), rows), :]
+
+    barrier = pltpu.get_barrier_semaphore()
+    pl.semaphore_signal(barrier, inc=1, device_id=(leaf, partner, c), device_id_type=mesh_ids)
+    for d in range(1, chips):
+        peer = 2 * lax.rem(chip + d, chips) + core
+        pl.semaphore_signal(barrier, inc=1, device_id=(leaf, peer, c), device_id_type=mesh_ids)
+    pl.semaphore_wait(barrier, chips)
+
+    sends = []
+    copy = pltpu.make_async_remote_copy(
+        src_ref=x_ref, dst_ref=at(r), send_sem=sems.at[0, 0], recv_sem=sems.at[1, 0],
+        device_id=(leaf, partner, c), device_id_type=mesh_ids,
+    )
+    copy.start()
+    sends.append(copy)
+    for d in range(1, chips):
+        peer = 2 * lax.rem(chip + d, chips) + core
+        copy = pltpu.make_async_remote_copy(
+            src_ref=x_ref, dst_ref=at(r), send_sem=sems.at[0, d], recv_sem=sems.at[1, d],
+            device_id=(leaf, peer, c), device_id_type=mesh_ids,
+        )
+        copy.start()
+        sends.append(copy)
+    out_ref[:, pl.ds(pl.multiple_of(r * rows, rows), rows), :] = x_ref[...]
+    for d in range(1, chips):
+        source = 2 * lax.rem(chip + chips - d, chips) + core
+        pltpu.make_async_remote_copy(
+            src_ref=x_ref, dst_ref=at(source), send_sem=sems.at[0, d], recv_sem=sems.at[1, d],
+            device_id=(leaf, source, c), device_id_type=mesh_ids,
+        ).wait_recv()
+        copy = pltpu.make_async_remote_copy(
+            src_ref=at(source), dst_ref=at(source), send_sem=sems.at[0, chips + d - 1],
+            recv_sem=sems.at[1, chips + d - 1], device_id=(leaf, partner, c), device_id_type=mesh_ids,
+        )
+        copy.start()
+        sends.append(copy)
+    pltpu.make_async_remote_copy(
+        src_ref=x_ref, dst_ref=at(partner), send_sem=sems.at[0, 0], recv_sem=sems.at[1, 0],
+        device_id=(leaf, partner, c), device_id_type=mesh_ids,
+    ).wait_recv()
+    for d in range(1, chips):
+        source = 2 * lax.rem(chip + chips - d, chips) + 1 - core
+        pltpu.make_async_remote_copy(
+            src_ref=at(source), dst_ref=at(source), send_sem=sems.at[0, chips + d - 1],
+            recv_sem=sems.at[1, chips + d - 1], device_id=(leaf, partner, c), device_id_type=mesh_ids,
+        ).wait_recv()
+    for copy in sends:
+        copy.wait_send()
+
+
+def pair_gather(x, row_count, collective_id):
+    lead, rows, last = x.shape
+    chips = row_count // 2
+    vmem = pl.BlockSpec(memory_space=pltpu.VMEM)
+    return pl.pallas_call(
+        functools.partial(pair_gather_kernel, chips=chips, rows=rows),
+        out_shape=jax.ShapeDtypeStruct((lead, rows * row_count, last), x.dtype),
+        in_specs=[vmem],
+        out_specs=vmem,
+        scratch_shapes=[pltpu.SemaphoreType.DMA((2, 2 * chips - 1))],
+        compiler_params=pltpu.CompilerParams(collective_id=collective_id, has_side_effects=True),
+    )(x)
+
+
 def body(sigma_top, panels, inverse_diag, slot_lists, parent_links):
     tile = TILE
     row_count = lax.axis_size("row")
@@ -466,7 +541,7 @@
     live_here = jnp.take(living, r, axis=1).astype(jnp.float32)
     factor_rows = factor_rows * live_here[:, None, None]
     factor_tile = lax.dynamic_slice_in_dim(factor_rows, c * tile, tile, 2)
-    factor_cols = lax.all_gather(factor_tile, "row", axis=1, tiled=True)
+    factor_cols = pair_gather(factor_tile, row_count, 5)
 
     inverse_band = lax.dynamic_slice_in_dim(inverse, r * band, band, 2)
     partial_gram = mm(jnp.transpose(inverse_band, (0, 2, 1)), inverse)

time: 289 us -> 321 us (1.11)
  Pallas kernels: 124 us -> 164 us
  waiting for transfers between devices: 71.5 us -> 62.4 us
  other arithmetic: 13 us -> 17.3 us
    pallas_call x0 -> x1, Pallas kernels: none -> 31.7 us  [pair_gather(): pl.pallas_call(functools.partial(pair_gather_kernel, chips=chips, rows=ro...]
    pallas_call x1, Pallas kernels: 48.4 us -> 56.6 us  [axis_reduce(): pl.pallas_call(kernel, out_shape=jax.ShapeDtypeStruct((lead, out_rows, la...]
    all_gather x2, waiting for transfers between devices: 66.5 us -> 62.3 us  [reduce_and_gather(): everything = lax.all_gather(both, ('row', 'col'), axis=0)]
  transfers between devices with their start and end apart: 8 -> 7, of which waited for: 5 -> 2; matrix products, arithmetic and copies ran while one was open for 8% -> 11% of each run, Pallas kernels for 9% -> 36%
where the time goes in v17:
time: 321 us
  Pallas kernels  164 us (51%)
  waiting for transfers between devices  62.4 us (19%)
  local copies, waits for them, and re-layouts  19.8 us (6%)
  other arithmetic  17.3 us (5%)
  starting transfers between devices  16.9 us (5%)
  matrix products  15.1 us (5%)
  between operations  14.1 us (4%)
  blocking collectives  10.6 us (3%)
    all_gather x2, waiting for transfers between devices, reduce_and_gather(): everything = lax.all_gather(both, ('row', 'col'), axis=0)  62.3 us
    pallas_call x1, Pallas kernels, axis_reduce(): pl.pallas_call(kernel, out_shape=jax.ShapeDtypeStruct((lead, out_rows, la...  56.6 us
    pallas_call x1, Pallas kernels, pair_gather(): pl.pallas_call(functools.partial(pair_gather_kernel, chips=chips, rows=ro...  31.7 us
    pallas_call x1, Pallas kernels, pair_reduce(): pl.pallas_call(functools.partial(pair_reduce_kernel, band=band, chips=chi...  26.4 us
    pallas_call x1, Pallas kernels, axis_gather(): pl.pallas_call(functools.partial(gather_kernel, axis=axis, count=count, b...  19.3 us
    pallas_call x2, Pallas kernels, pair_scatter(): pl.pallas_call(functools.partial(pair_scatter_kernel, chips=chips), out_s...  18.6 us
    ppermute x4, starting transfers between devices, body(): rounds.append(lax.ppermute(chunk_rows, ('leaf', 'row', 'col'), pairs))  16.8 us
    dot_general x8, matrix products, mm(): jnp.matmul(a, b, precision=HIGHEST, preferred_element_type=jnp.float32)  15.1 us
  transfers between devices with their start and end apart: 7, of which 2 were waited for; matrix products, arithmetic and copies ran while one was open for 11% of the time, Pallas kernels for 36%

profile of v17, /device:TPU:1, one launch (start us, length us, event | category | flops | bytes accessed | tf_op | source)
XLA Modules:
  0.0 320.5 jit_solution(16384623498100322714)
XLA Ops:
  7.2 10.6 %all_gather.15 = f32[32,1024]{1,0:T(8,128)S(1)} all-gather(f32[32,256]{1,0:T(8,128)} %param.7), channel_id=1, replica_groups=mesh['leaf'=4,'row'=8,'col'=4] {'col'}, dimensions={1}, use_global_device_ids=true | all-gather | bytes 163840 | tf_op jit(solution)/shard_map/all_gather | solution.py:552
  17.9 5.4 %collective-permute-start.3 = (f32[32,1024]{1,0:T(8,128)S(1)}, f32[32,1024]{1,0:T(8,128)}, u32[]{:S(2)}, u32[]{:S(2)}) collective-permute-start(f32[32,1024]{1,0:T(8,128)S(1)} %all_gather.15), channel_id=1, source_target_pairs={{0,96},{1,97},{2,98},{3,99},{4,0},{5,1},{6,2},{7,3},{8,32},{9,33},... | collective-permute-start | bytes 393224 | tf_op jit(solution)/shard_map/ppermute | solution.py:567
  23.3 6.7 %collective-permute-start.2 = (f32[32,1024]{1,0:T(8,128)S(1)}, f32[32,1024]{1,0:T(8,128)}, u32[]{:S(2)}, u32[]{:S(2)}) collective-permute-start(f32[32,1024]{1,0:T(8,128)S(1)} %all_gather.15), channel_id=1, source_target_pairs={{0,64},{1,65},{2,66},{3,67},{4,96},{5,97},{6,98},{7,99},{8,0},{9,1... | collective-permute-start | bytes 393224 | tf_op jit(solution)/shard_map/ppermute | solution.py:567
  30.1 2.7 collective-permute-start.1
  32.7 1.9 collective-permute-start
  34.7 2.2 fusion
  40.3 2.8 fusion.2.x_ref
  43.1 56.6 %shard_map.68 = f32[7,128,512]{2,1,0:T(8,128)} custom-call(f32[7,128,512]{2,1,0:T(8,128)} %fusion.2.x_ref), custom_call_target="tpu_custom_call" | custom-call | tf_op jit(solution)/shard_map/pallas_call | solution.py:205
  99.8 1.8 broadcast_multiply_fusion
  103.6 31.7 %shard_map.69 = f32[7,1024,128]{2,1,0:T(8,128)} custom-call(f32[7,128,128]{2,1,0:T(8,128)} %constant_dynamic-slice_fusion.1.x_ref), custom_call_target="tpu_custom_call" | custom-call | tf_op jit(solution)/shard_map/pallas_call | solution.py:510
  140.5 1.8 copy.21
  149.4 8.2 %shard_map.70 = f32[1,64,128]{2,1,0:T(8,128)} custom-call(f32[1,4,2,64,128]{4,3,2,1,0:T(8,128)} %convolution_bitcast_fusion.x_ref), custom_call_target="tpu_custom_call" | custom-call | tf_op jit(solution)/shard_map/pallas_call | solution.py:431
  161.1 2.3 slice.63.fac_ref
  164.1 19.3 %shard_map.71.low_ref = f32[2,1024,128]{2,1,0:T(8,128)} custom-call(f32[2,128,128]{2,1,0:T(8,128)} %pad_maximum_fusion.1.x_ref), custom_call_target="tpu_custom_call" | custom-call | tf_op jit(solution)/shard_map/pallas_call | solution.py:268
  183.5 21.5 %all-gather.5.cloned.1.call-done = f32[32,192,128]{2,1,0:T(8,128)} async-done(((f32[1,192,128]{2,1,0:T(8,128)}), f32[32,192,128]{2,1,0:T(8,128)}) %all-gather.5.cloned.1.call-update) | async-done | bytes 3145744 | tf_op jit(solution)/shard_map/all_gather | solution.py:583
  205.0 4.6 %shard_map.72 = (f32[2,128,128]{2,1,0:T(8,128)}, f32[2,64,128]{2,1,0:T(8,128)}) custom-call(s32[20]{0:T(128)} %pad_add_fusion.info_ref, f32[8,4,1,192,128]{4,3,2,1,0:T(8,128)} %bitcast.73, f32[2,1024,128]{2,1,0:T(8,128)} %shard_map.71.low_ref, f32[2,1024,128]{2,1,0:T(8,128)} %slice.63.fac_ref), custom_call_target="tpu_custom_call" | custom-call | tf_op jit(solution)/shard_map/pallas_call | solution.py:123
  209.6 2.9 fusion.19
  212.5 10.4 %shard_map.73 = f32[2,64,128]{2,1,0:T(8,128)} custom-call(f32[2,4,2,64,128]{4,3,2,1,0:T(8,128)} %bitcast.85), custom_call_target="tpu_custom_call" | custom-call | tf_op jit(solution)/shard_map/pallas_call | solution.py:431
  224.5 3.1 slice.67.fac_ref
  230.3 40.8 %all-gather.7.cloned.1.call-done = f32[64,128,128]{2,1,0:T(8,128)} async-done(((f32[2,128,128]{2,1,0:T(8,128)}), f32[64,128,128]{2,1,0:T(8,128)}) %all-gather.7.cloned.1.call-update) | async-done | bytes 4194320 | tf_op jit(solution)/shard_map/all_gather | solution.py:583
  272.9 7.0 %shard_map.74 = f32[4,128,128]{2,1,0:T(8,128)} custom-call(s32[38]{0:T(128)} %pad_add_fusion.1.info_ref, f32[8,4,2,128,128]{4,3,2,1,0:T(8,128)} %bitcast.77, f32[8,4,1,192,128]{4,3,2,1,0:T(8,128)} %bitcast.75, f32[4,1024,128]{2,1,0:T(8,128)} %slice.67.fac_ref), custom_call_target="tpu_custom_call" | custom-call | tf_op jit(solution)/shard_map/pallas_call | solution.py:123
  280.0 3.1 fusion.20
  284.1 26.4 %shard_map.75 = f32[4,512,128]{2,1,0:T(8,128)} custom-call(f32[4,512,128]{2,1,0:T(8,128)} %copy-done.2), custom_call_target="tpu_custom_call" | custom-call | tf_op jit(solution)/shard_map/pallas_call | solution.py:368
  310.5 2.7 maximum_bitcast_fusion
  (84 shorter events, 29.7 us)
Async XLA Ops:
  7.2 27.5 %copy-start = (f32[1,7,128,512]{3,2,1,0:T(8,128)S(1)}, f32[1,7,128,512]{3,2,1,0:T(8,128)}, u32[]{:S(2)}) copy-start(f32[1,7,128,512]{3,2,1,0:T(8,128)} %param.9) | copy-start | bytes 5505028
  7.2 152.4 %reduce-scatter.2.cloned.1.call-start = ((), (), s32[]{:S(2)}) async-start(), calls=%async_computation.1 | async-start | bytes 1146880 | tf_op jit(solution)/shard_map/reduce_scatter | solution.py:548
  17.9 125.1 %collective-permute-start.3 = (f32[32,1024]{1,0:T(8,128)S(1)}, f32[32,1024]{1,0:T(8,128)}, u32[]{:S(2)}, u32[]{:S(2)}) collective-permute-start(f32[32,1024]{1,0:T(8,128)S(1)} %all_gather.15), channel_id=1, source_target_pairs={{0,96},{1,97},{2,98},{3,99},{4,0},{5,1},{6,2},{7,3},{8,32},{9,33},... | collective-permute-start | bytes 393224 | tf_op jit(solution)/shard_map/ppermute | solution.py:567
  23.3 119.6 %collective-permute-start.2 = (f32[32,1024]{1,0:T(8,128)S(1)}, f32[32,1024]{1,0:T(8,128)}, u32[]{:S(2)}, u32[]{:S(2)}) collective-permute-start(f32[32,1024]{1,0:T(8,128)S(1)} %all_gather.15), channel_id=1, source_target_pairs={{0,64},{1,65},{2,66},{3,67},{4,96},{5,97},{6,98},{7,99},{8,0},{9,1... | collective-permute-start | bytes 393224 | tf_op jit(solution)/shard_map/ppermute | solution.py:567
  30.1 112.9 %collective-permute-start.1 = (f32[32,1024]{1,0:T(8,128)S(1)}, f32[32,1024]{1,0:T(8,128)}, u32[]{:S(2)}, u32[]{:S(2)}) collective-permute-start(f32[32,1024]{1,0:T(8,128)S(1)} %all_gather.15), channel_id=1, source_target_pairs={{0,32},{1,33},{2,34},{3,35},{4,64},{5,65},{6,66},{7,67},{8,96},{9,... | collective-permute-start | bytes 393224 | tf_op jit(solution)/shard_map/ppermute | solution.py:567
  32.7 110.2 %collective-permute-start = (f32[32,1024]{1,0:T(8,128)S(1)}, f32[32,1024]{1,0:T(8,128)}, u32[]{:S(2)}, u32[]{:S(2)}) collective-permute-start(f32[32,1024]{1,0:T(8,128)S(1)} %all_gather.15), channel_id=1, source_target_pairs={{0,0},{1,1},{2,2},{3,3},{4,32},{5,33},{6,34},{7,35},{8,64},{9,65},... | collective-permute-start | bytes 393224 | tf_op jit(solution)/shard_map/ppermute | solution.py:567
  34.7 2.3 copy-start.10
  34.7 5.6 %copy-start.6 = (f32[1,7,128,128]{3,2,1,0:T(8,128)S(1)}, f32[1,7,128,128]{3,2,1,0:T(8,128)}, u32[]{:S(2)}) copy-start(f32[1,7,128,128]{3,2,1,0:T(8,128)} %param.8) | copy-start | bytes 1376260
  36.9 168.0 %all-gather.5.cloned.1.call-start = ((), (), s32[]{:S(2)}) async-start(), calls=%async_computation.2 | async-start | bytes 3244032 | tf_op jit(solution)/shard_map/all_gather | solution.py:583
  101.6 1.2 copy-start.1
  137.2 3.1 copy-start.11
  145.5 2.9 copy-start.4
  157.7 2.0 copy-start.8
  161.1 110.1 %all-gather.7.cloned.1.call-start = ((), (), s32[]{:S(2)}) async-start(), calls=%async_computation.3 | async-start | bytes 4325376 | tf_op jit(solution)/shard_map/all_gather | solution.py:583
  209.6 14.1 %copy-start.9 = (f32[2,64,128]{2,1,0:T(8,128)S(1)}, f32[2,64,128]{2,1,0:T(8,128)}, u32[]{:S(2)}) copy-start(f32[2,64,128]{2,1,0:T(8,128)} %get-tuple-element.14) | copy-start | bytes 196612
  224.4 3.2 copy-start.12
  280.0 3.1 copy-start.7
  283.1 1.0 copy-start.2
  310.5 2.7 copy-start.3
  310.5 2.7 copy-start.5
Sparse Core Ops, SparseCore 0:
  37.1 40.5 reduce-scatter.1
  161.2 43.7 all-gather.4
  224.6 46.5 all-gather.6

commit v18 on v16

--- a/solution.py
+++ b/solution.py
@@ -43,8 +43,14 @@
     )
 
 
-def level_kernel(info_ref, par_ref, low_ref, fac_ref, out_ref, *rest, level, tile, band, own_tiles, slot_count,
-                 par_prow, low_prow, halves):
+def level_kernel(info_ref, par_ref, low_ref, fac_ref, *rest, level, tile, band, own_tiles, slot_count,
+                 par_prow, low_prow, halves, with_diag):
+    extra = ()
+    if with_diag:
+        extra = (rest[0], rest[1], rest[3])
+        rest = (rest[2],) + rest[4:]
+    out_ref = rest[0]
+    rest = rest[1:]
     count = out_ref.shape[0]
     split = tile // band
     r = info_ref[0]
@@ -108,24 +114,33 @@
         def _():
             out_ref[i] = jnp.zeros((tile, tile), jnp.float32)
 
+        if extra:
+            rows_ref, gram_ref, diag_ref = extra
+            diag_ref[i] = dot_t_hi(rows_ref[i], out_ref[i])
+            start = pl.multiple_of(r * band, band)
+            diag_ref[i, pl.ds(start, band), :] = diag_ref[i, pl.ds(start, band), :] + gram_ref[i]
+
 
 def level_products(info, parent_data, low_data, factors, level, tile, band, own_tiles, slot_count,
-                   par_prow, low_prow, halves):
+                   par_prow, low_prow, halves, diag_inputs=()):
     kernel = functools.partial(
         level_kernel, level=level, tile=tile, band=band, own_tiles=own_tiles, slot_count=slot_count,
-        par_prow=par_prow, low_prow=low_prow, halves=halves,
+        par_prow=par_prow, low_prow=low_prow, halves=halves, with_diag=bool(diag_inputs),
     )
     vmem = pl.BlockSpec(memory_space=pltpu.VMEM)
     count = factors.shape[0]
     shapes = [jax.ShapeDtypeStruct((count, tile, tile), jnp.float32)]
     if halves:
         shapes.append(jax.ShapeDtypeStruct((count, tile // halves, tile), jnp.float32))
+    if diag_inputs:
+        width = diag_inputs[0].shape[2]
+        shapes.append(jax.ShapeDtypeStruct((count, width, tile), jnp.float32))
     return pl.pallas_call(
         kernel,
         out_shape=tuple(shapes),
-        in_specs=[pl.BlockSpec(memory_space=pltpu.SMEM), vmem, vmem, vmem],
+        in_specs=[pl.BlockSpec(memory_space=pltpu.SMEM)] + [vmem] * (3 + len(diag_inputs)),
         out_specs=tuple([vmem] * len(shapes)),
-    )(info, parent_data, low_data, factors)
+    )(info, parent_data, low_data, factors, *diag_inputs)
 
 
 def reduce_kernel(x_ref, out_ref, recv_ref, send_sem, recv_sem, back_send, back_recv, *, axis, count, band, gather):
@@ -555,15 +570,11 @@
         [r.astype(jnp.int32)[None], picks_all[2:nodes - 1].reshape(-1), (parents - 1).astype(jnp.int32),
          c.astype(jnp.int32)[None]]
     )
-    (product_2,) = level_products(
+    product_2, partial_2 = level_products(
         info_2, gathered_1, gathered_0, factor_cols[3:nodes], 2, tile, band, own_tiles, slot_count,
-        tile // halves, tile, 0,
-    )
-    first_2 = 3
-    count_2 = product_2.shape[0]
-    gram_rows = jnp.zeros((count_2, width, tile), jnp.float32)
-    gram_rows = lax.dynamic_update_slice_in_dim(gram_rows, gram_piece[first_2:first_2 + count_2], r * band, 1)
-    diag_2 = pair_reduce(diag_partial(first_2, product_2) + gram_rows, row_count, 2)
+        tile // halves, tile, 0, (factor_rows[3:nodes], gram_piece[3:nodes]),
+    )
+    diag_2 = pair_reduce(partial_2, row_count, 2)
 
     products = jnp.concatenate([product_0[None], product_1, product_2], axis=0)
     diag_cols = jnp.concatenate(

time: 289 us -> 286 us (0.990)
  matrix products: 16.1 us -> 13 us
    dot_general x8 -> x7, matrix products: 16.1 us -> 13 us  [mm(): jnp.matmul(a, b, precision=HIGHEST, preferred_element_type=jnp.float32)]
    slice x0 -> x2, local copies, waits for them, and re-layouts: none -> 2.95 us  [the longest x1 2.29 us: body(): factor_rows[3:nodes]]
  transfers between devices with their start and end apart: 8 -> 8, of which waited for: 5 -> 5; matrix products, arithmetic and copies ran while one was open for 8% -> 9% of each run, Pallas kernels for 9% -> 9%
where the time goes in v18:
time: 286 us; the launch traced here: 285 us
  Pallas kernels  126 us (44%)
  waiting for transfers between devices  68.9 us (24%)
  local copies, waits for them, and re-layouts  20.2 us (7%)
  starting transfers between devices  18.5 us (6%)
  between operations  16 us (6%)
  other arithmetic  13 us (5%)
  matrix products  13 us (5%)
  blocking collectives  9.78 us (3%)
    all_gather x2, waiting for transfers between devices, reduce_and_gather(): everything = lax.all_gather(both, ('row', 'col'), axis=0)  64 us
    pallas_call x1, Pallas kernels, axis_reduce(): pl.pallas_call(kernel, out_shape=jax.ShapeDtypeStruct((lead, out_rows, la...  48.4 us
    pallas_call x1, Pallas kernels, pair_reduce(): pl.pallas_call(functools.partial(pair_reduce_kernel, band=band, chips=chi...  26.5 us
    pallas_call x2, Pallas kernels, pair_scatter(): pl.pallas_call(functools.partial(pair_scatter_kernel, chips=chips), out_s...  19 us
    pallas_call x1, Pallas kernels, axis_gather(): pl.pallas_call(functools.partial(gather_kernel, axis=axis, count=count, b...  18.4 us
    ppermute x4, starting transfers between devices, body(): rounds.append(lax.ppermute(chunk_rows, ('leaf', 'row', 'col'), pairs))  18.3 us
    pallas_call x2, Pallas kernels, level_products(): pl.pallas_call(kernel, out_shape=tuple(shapes), in_specs=[pl.BlockSpec(me...  13.3 us
    dot_general x7, matrix products, mm(): jnp.matmul(a, b, precision=HIGHEST, preferred_element_type=jnp.float32)  13 us
  transfers between devices with their start and end apart: 8, of which 5 were waited for; matrix products, arithmetic and copies ran while one was open for 9% of the time, Pallas kernels for 9%

profile of v18, /device:TPU:1, one launch (start us, length us, event | category | flops | bytes accessed | tf_op | source)
XLA Modules:
  0.0 285.0 jit_solution(14685758607920152705)
XLA Ops:
  9.5 3.9 %fusion.2.x_ref = f32[7,128,512]{2,1,0:T(8,128)} fusion(f32[1,7,128,512]{3,2,1,0:T(8,128)S(1)} %copy-done, f32[1,7,128,128]{3,2,1,0:T(8,128)} %param.8), kind=kOutput, calls=%fused_computation.6 | convolution fusion | flops 704643072 | bytes 4128768 | tf_op jit(solution)/shard_map/dot_general | solution.py:15
  13.4 48.4 %shard_map.68 = f32[7,128,512]{2,1,0:T(8,128)} custom-call(f32[7,128,512]{2,1,0:T(8,128)} %fusion.2.x_ref), custom_call_target="tpu_custom_call" | custom-call | tf_op jit(solution)/shard_map/pallas_call | solution.py:220
  61.8 1.8 broadcast_multiply_fusion
  65.8 9.8 %all_gather.18 = f32[32,1024]{1,0:T(8,128)S(1)} all-gather(f32[32,256]{1,0:T(8,128)S(1)} %copy-done.7), channel_id=1, replica_groups=mesh['leaf'=4,'row'=8,'col'=4] {'col'}, dimensions={1}, use_global_device_ids=true | all-gather | bytes 163840 | tf_op jit(solution)/shard_map/all_gather | solution.py:492
  75.6 7.0 %collective-permute-start.3 = (f32[32,1024]{1,0:T(8,128)S(1)}, f32[32,1024]{1,0:T(8,128)S(1)}, u32[]{:S(2)}, u32[]{:S(2)}) collective-permute-start(f32[32,1024]{1,0:T(8,128)S(1)} %all_gather.18), channel_id=1, source_target_pairs={{0,96},{1,97},{2,98},{3,99},{4,0},{5,1},{6,2},{7,3},{8,32},{9,33},... | collective-permute-start | bytes 393224 | tf_op jit(solution)/shard_map/ppermute | solution.py:507
  82.6 6.7 %collective-permute-start.2 = (f32[32,1024]{1,0:T(8,128)S(1)}, f32[32,1024]{1,0:T(8,128)S(1)}, u32[]{:S(2)}, u32[]{:S(2)}) collective-permute-start(f32[32,1024]{1,0:T(8,128)S(1)} %all_gather.18), channel_id=1, source_target_pairs={{0,64},{1,65},{2,66},{3,67},{4,96},{5,97},{6,98},{7,99},{8,0},{9,1... | collective-permute-start | bytes 393224 | tf_op jit(solution)/shard_map/ppermute | solution.py:507
  89.3 2.7 collective-permute-start.1
  92.0 1.9 collective-permute-start
  93.9 2.2 fusion
  101.8 2.6 all-gather.6.cloned.1.call-done
  107.2 8.6 %shard_map.69 = f32[1,64,128]{2,1,0:T(8,128)} custom-call(f32[1,4,2,64,128]{4,3,2,1,0:T(8,128)} %convolution_bitcast_fusion.x_ref), custom_call_target="tpu_custom_call" | custom-call | tf_op jit(solution)/shard_map/pallas_call | solution.py:446
  115.8 2.1 fusion.15
  124.6 18.4 %shard_map.70.low_ref = f32[2,1024,128]{2,1,0:T(8,128)} custom-call(f32[2,128,128]{2,1,0:T(8,128)} %pad_maximum_fusion.1.x_ref), custom_call_target="tpu_custom_call" | custom-call | tf_op jit(solution)/shard_map/pallas_call | solution.py:283
  143.0 2.3 slice.90.fac_ref
  145.4 25.5 %all-gather.8.cloned.1.call-done = f32[32,192,128]{2,1,0:T(8,128)} async-done(((f32[1,192,128]{2,1,0:T(8,128)}), f32[32,192,128]{2,1,0:T(8,128)}) %all-gather.8.cloned.1.call-update) | async-done | bytes 3145744 | tf_op jit(solution)/shard_map/all_gather | solution.py:523
  170.9 4.6 %shard_map.71 = (f32[2,128,128]{2,1,0:T(8,128)}, f32[2,64,128]{2,1,0:T(8,128)}) custom-call(s32[20]{0:T(128)} %pad_add_fusion.info_ref, f32[8,4,1,192,128]{4,3,2,1,0:T(8,128)} %bitcast.71, f32[2,1024,128]{2,1,0:T(8,128)} %shard_map.70.low_ref, f32[2,1024,128]{2,1,0:T(8,128)} %slice.90.fac_ref), custom_call_target="tpu_custom_call" | custom-call | tf_op jit(solution)/shard_map/pallas_call | solution.py:138
  175.6 2.9 %fusion.16 = f32[2,512,128]{2,1,0:T(8,128)} fusion(f32[7,128,512]{2,1,0:T(8,128)} %copy-done.1, f32[2,128,128]{2,1,0:T(8,128)} %get-tuple-element.15), kind=kOutput, calls=%fused_computation.66 | convolution fusion | flops 201326592 | bytes 2490368 | tf_op jit(solution)/shard_map/dot_general | solution.py:15
  178.4 10.4 %shard_map.72 = f32[2,64,128]{2,1,0:T(8,128)} custom-call(f32[2,4,2,64,128]{4,3,2,1,0:T(8,128)} %bitcast.82), custom_call_target="tpu_custom_call" | custom-call | tf_op jit(solution)/shard_map/pallas_call | solution.py:446
  190.4 2.3 slice.93.rest_0_
  194.1 3.1 %slice.92.fac_ref = f32[4,1024,128]{2,1,0:T(8,128)} slice(f32[7,1024,128]{2,1,0:T(8,128)} %all-gather.6.cloned.1.call-done), slice={[3:7], [0:1024], [0:128]} | slice | bytes 4194304 | tf_op jit(solution)/shard_map/slice | solution.py:574
  198.5 38.5 %all-gather.10.cloned.1.call-done = f32[64,128,128]{2,1,0:T(8,128)} async-done(((f32[2,128,128]{2,1,0:T(8,128)}), f32[64,128,128]{2,1,0:T(8,128)}) %all-gather.10.cloned.1.call-update) | async-done | bytes 4194320 | tf_op jit(solution)/shard_map/all_gather | solution.py:523
  238.9 8.6 %shard_map.73 = (f32[4,128,128]{2,1,0:T(8,128)}, f32[4,512,128]{2,1,0:T(8,128)}) custom-call(s32[38]{0:T(128)} %pad_add_fusion.1.info_ref, f32[8,4,2,128,128]{4,3,2,1,0:T(8,128)} %bitcast.75, f32[8,4,1,192,128]{4,3,2,1,0:T(8,128)} %bitcast.73, f32[4,1024,128]{2,1,0:T(8,128)} %slice.92.fac_ref, f32[4,128,512]{2,1,0:T(8,128)} %slice.93.rest_0_, ...), custom_call_target="tpu_custom_call" | custom-call | tf_op jit(solution)/shard_map/pallas_call | solution.py:138
  247.5 26.5 %shard_map.74 = f32[4,512,128]{2,1,0:T(8,128)} custom-call(f32[4,512,128]{2,1,0:T(8,128)} %get-tuple-element.18.x_ref), custom_call_target="tpu_custom_call" | custom-call | tf_op jit(solution)/shard_map/pallas_call | solution.py:383
  274.9 2.6 maximum_bitcast_fusion
  (80 shorter events, 25.6 us)
Async XLA Ops:
  8.0 1.5 copy-start
  8.0 96.4 %all-gather.6.cloned.1.call-start = ((), (), s32[]{:S(2)}) async-start(), calls=%async_computation.1 | async-start | bytes 4128768 | tf_op jit(solution)/shard_map/all_gather | solution.py:484
  61.8 3.9 %copy-start.7 = (f32[32,256]{1,0:T(8,128)S(1)}, f32[32,256]{1,0:T(8,128)}, u32[]{:S(2)}) copy-start(f32[32,256]{1,0:T(8,128)} %param.7) | copy-start | bytes 98308
  63.6 1.2 copy-start.1
  65.7 56.7 %reduce-scatter.2.cloned.1.call-start = ((), (), s32[]{:S(2)}) async-start(), calls=%async_computation.2 | async-start | bytes 1146880 | tf_op jit(solution)/shard_map/reduce_scatter | solution.py:488
  75.6 23.3 %collective-permute-start.3 = (f32[32,1024]{1,0:T(8,128)S(1)}, f32[32,1024]{1,0:T(8,128)S(1)}, u32[]{:S(2)}, u32[]{:S(2)}) collective-permute-start(f32[32,1024]{1,0:T(8,128)S(1)} %all_gather.18), channel_id=1, source_target_pairs={{0,96},{1,97},{2,98},{3,99},{4,0},{5,1},{6,2},{7,3},{8,32},{9,33},... | collective-permute-start | bytes 393224 | tf_op jit(solution)/shard_map/ppermute | solution.py:507
  82.6 16.2 %collective-permute-start.2 = (f32[32,1024]{1,0:T(8,128)S(1)}, f32[32,1024]{1,0:T(8,128)S(1)}, u32[]{:S(2)}, u32[]{:S(2)}) collective-permute-start(f32[32,1024]{1,0:T(8,128)S(1)} %all_gather.18), channel_id=1, source_target_pairs={{0,64},{1,65},{2,66},{3,67},{4,96},{5,97},{6,98},{7,99},{8,0},{9,1... | collective-permute-start | bytes 393224 | tf_op jit(solution)/shard_map/ppermute | solution.py:507
  89.3 10.2 %collective-permute-start.1 = (f32[32,1024]{1,0:T(8,128)S(1)}, f32[32,1024]{1,0:T(8,128)S(1)}, u32[]{:S(2)}, u32[]{:S(2)}) collective-permute-start(f32[32,1024]{1,0:T(8,128)S(1)} %all_gather.18), channel_id=1, source_target_pairs={{0,32},{1,33},{2,34},{3,35},{4,64},{5,65},{6,66},{7,67},{8,96},{9,... | collective-permute-start | bytes 393224 | tf_op jit(solution)/shard_map/ppermute | solution.py:507
  92.0 9.1 %collective-permute-start = (f32[32,1024]{1,0:T(8,128)S(1)}, f32[32,1024]{1,0:T(8,128)S(1)}, u32[]{:S(2)}, u32[]{:S(2)}) collective-permute-start(f32[32,1024]{1,0:T(8,128)S(1)} %all_gather.18), channel_id=1, source_target_pairs={{0,0},{1,1},{2,2},{3,3},{4,32},{5,33},{6,34},{7,35},{8,64},{9,65},... | collective-permute-start | bytes 393224 | tf_op jit(solution)/shard_map/ppermute | solution.py:507
  93.9 2.3 copy-start.8
  96.2 74.7 %all-gather.8.cloned.1.call-start = ((), (), s32[]{:S(2)}) async-start(), calls=%async_computation.3 | async-start | bytes 3244032 | tf_op jit(solution)/shard_map/all_gather | solution.py:523
  120.3 2.1 copy-start.5
  123.8 113.2 %all-gather.10.cloned.1.call-start = ((), (), s32[]{:S(2)}) async-start(), calls=%async_computation.4 | async-start | bytes 4325376 | tf_op jit(solution)/shard_map/all_gather | solution.py:523
  175.6 13.3 %copy-start.4 = (f32[7,64,128]{2,1,0:T(8,128)S(1)}, f32[7,64,128]{2,1,0:T(8,128)}, u32[]{:S(2)}) copy-start(f32[7,64,128]{2,1,0:T(8,128)} %reduce-scatter.2.cloned.1.call-done) | copy-start | bytes 688132
  175.6 14.1 %copy-start.6 = (f32[2,64,128]{2,1,0:T(8,128)S(1)}, f32[2,64,128]{2,1,0:T(8,128)}, u32[]{:S(2)}) copy-start(f32[2,64,128]{2,1,0:T(8,128)} %get-tuple-element.16) | copy-start | bytes 196612
  178.4 14.3 %copy-start.9 = (s32[1,4]{1,0:T(1,128)S(1)}, s32[1,4]{1,0:T(1,128)}, u32[]{:S(2)}) copy-start(s32[1,4]{1,0:T(1,128)} %param.11) | copy-start | bytes 52
  247.5 26.6 %copy-start.2 = (f32[2,128,128]{2,1,0:T(8,128)S(1)}, f32[2,128,128]{2,1,0:T(8,128)}, u32[]{:S(2)}) copy-start(f32[2,128,128]{2,1,0:T(8,128)} %get-tuple-element.15) | copy-start | bytes 393220
  247.5 26.6 %copy-start.3 = (f32[4,128,128]{2,1,0:T(8,128)S(1)}, f32[4,128,128]{2,1,0:T(8,128)}, u32[]{:S(2)}) copy-start(f32[4,128,128]{2,1,0:T(8,128)} %get-tuple-element.17) | copy-start | bytes 786436
Sparse Core Ops, SparseCore 0:
  65.8 38.5 all-gather.5
Sparse Core Ops, SparseCore 1:
  96.3 22.2 reduce-scatter.1
  123.9 47.0 all-gather.7
  190.5 46.5 all-gather.9

commit v19 on v18

--- a/solution.py
+++ b/solution.py
@@ -47,8 +47,8 @@
                  par_prow, low_prow, halves, with_diag):
     extra = ()
     if with_diag:
-        extra = (rest[0], rest[1], rest[3])
-        rest = (rest[2],) + rest[4:]
+        extra = (rest[0], rest[1], rest[-1])
+        rest = rest[2:-1]
     out_ref = rest[0]
     rest = rest[1:]
     count = out_ref.shape[0]
@@ -512,10 +512,13 @@
         rows = factor_rows[first:first + products.shape[0]]
         return mm(jnp.transpose(rows, (0, 2, 1)), products)
 
-    def reduce_and_gather(first, products, sent, extra, tied=None):
+    def reduce_and_gather(first, products, sent, extra, tied=None, partial=None):
         count = products.shape[0]
-        piece = pair_scatter(diag_partial(first, products), row_count, first)
-        piece = piece + gram_piece[first:first + count]
+        if partial is None:
+            piece = pair_scatter(diag_partial(first, products), row_count, first)
+            piece = piece + gram_piece[first:first + count]
+        else:
+            piece = pair_scatter(partial, row_count, first)
         if tied is not None:
             piece, tied = lax.optimization_barrier((piece, tied))
             tied_out.append(tied)
@@ -560,11 +563,11 @@
         [r.astype(jnp.int32)[None], picks_all[0:2].reshape(-1), jnp.zeros((2,), jnp.int32), c.astype(jnp.int32)[None]]
     )
     halves = row_count // own_tiles
-    product_1, upper_half = level_products(
+    product_1, upper_half, partial_1 = level_products(
         info_1, gathered_0, lifted_cols, factor_cols[1:3], 1, tile, band, own_tiles, slot_count,
-        tile, tile, halves,
-    )
-    gathered_1 = reduce_and_gather(1, product_1, upper_half, [])
+        tile, tile, halves, (factor_rows[1:3], gram_piece[1:3]),
+    )
+    gathered_1 = reduce_and_gather(1, product_1, upper_half, [], partial=partial_1)
 
     info_2 = jnp.concatenate(
         [r.astype(jnp.int32)[None], picks_all[2:nodes - 1].reshape(-1), (parents - 1).astype(jnp.int32),

time: 286 us -> 287 us (level)
  local copies, waits for them, and re-layouts: 20.2 us -> 23.5 us
  matrix products: 13 us -> 10.1 us
    slice x0 -> x2, local copies, waits for them, and re-layouts: none -> 3.34 us  [the longest x1 1.88 us: body(): factor_rows[1:3]]
    dot_general x7 -> x6, matrix products: 13 us -> 10.1 us  [mm(): jnp.matmul(a, b, precision=HIGHEST, preferred_element_type=jnp.float32)]
  transfers between devices with their start and end apart: 8 -> 8, of which waited for: 5 -> 5; matrix products, arithmetic and copies ran while one was open for 9% -> 10% of each run, Pallas kernels for 9% -> 10%
where the time goes in v19:
time: 287 us; the launch traced here: 286 us
  Pallas kernels  127 us (44%)
  waiting for transfers between devices  67.9 us (24%)
  local copies, waits for them, and re-layouts  23.5 us (8%)
  starting transfers between devices  18.5 us (6%)
  between operations  16 us (6%)
  other arithmetic  13 us (5%)
  matrix products  10.1 us (4%)
  blocking collectives  9.78 us (3%)
    all_gather x2, waiting for transfers between devices, reduce_and_gather(): everything = lax.all_gather(both, ('row', 'col'), axis=0)  63 us
    pallas_call x1, Pallas kernels, axis_reduce(): pl.pallas_call(kernel, out_shape=jax.ShapeDtypeStruct((lead, out_rows, la...  48.4 us
    pallas_call x1, Pallas kernels, pair_reduce(): pl.pallas_call(functools.partial(pair_reduce_kernel, band=band, chips=chi...  26.5 us
    pallas_call x2, Pallas kernels, pair_scatter(): pl.pallas_call(functools.partial(pair_scatter_kernel, chips=chips), out_s...  19 us
    pallas_call x1, Pallas kernels, axis_gather(): pl.pallas_call(functools.partial(gather_kernel, axis=axis, count=count, b...  18.9 us
    ppermute x4, starting transfers between devices, body(): rounds.append(lax.ppermute(chunk_rows, ('leaf', 'row', 'col'), pairs))  18.3 us
    pallas_call x2, Pallas kernels, level_products(): pl.pallas_call(kernel, out_shape=tuple(shapes), in_specs=[pl.BlockSpec(me...  14.2 us
    dot_general x6, matrix products, mm(): jnp.matmul(a, b, precision=HIGHEST, preferred_element_type=jnp.float32)  10.1 us
  transfers between devices with their start and end apart: 8, of which 5 were waited for; matrix products, arithmetic and copies ran while one was open for 10% of the time, Pallas kernels for 10%

profile of v19, /device:TPU:1, one launch (start us, length us, event | category | flops | bytes accessed | tf_op | source)
XLA Modules:
  0.0 285.8 jit_solution(4964225479222594895)
XLA Ops:
  9.5 3.9 %fusion.2.x_ref = f32[7,128,512]{2,1,0:T(8,128)} fusion(f32[1,7,128,512]{3,2,1,0:T(8,128)S(1)} %copy-done, f32[1,7,128,128]{3,2,1,0:T(8,128)} %param.8), kind=kOutput, calls=%fused_computation.6 | convolution fusion | flops 704643072 | bytes 4128768 | tf_op jit(solution)/shard_map/dot_general | solution.py:15
  13.4 48.4 %shard_map.68 = f32[7,128,512]{2,1,0:T(8,128)} custom-call(f32[7,128,512]{2,1,0:T(8,128)} %fusion.2.x_ref), custom_call_target="tpu_custom_call" | custom-call | tf_op jit(solution)/shard_map/pallas_call | solution.py:220
  61.8 1.8 broadcast_multiply_fusion
  65.8 9.8 %all_gather.18 = f32[32,1024]{1,0:T(8,128)S(1)} all-gather(f32[32,256]{1,0:T(8,128)S(1)} %copy-done.6), channel_id=1, replica_groups=mesh['leaf'=4,'row'=8,'col'=4] {'col'}, dimensions={1}, use_global_device_ids=true | all-gather | bytes 163840 | tf_op jit(solution)/shard_map/all_gather | solution.py:492
  75.6 7.0 %collective-permute-start.3 = (f32[32,1024]{1,0:T(8,128)S(1)}, f32[32,1024]{1,0:T(8,128)S(1)}, u32[]{:S(2)}, u32[]{:S(2)}) collective-permute-start(f32[32,1024]{1,0:T(8,128)S(1)} %all_gather.18), channel_id=1, source_target_pairs={{0,96},{1,97},{2,98},{3,99},{4,0},{5,1},{6,2},{7,3},{8,32},{9,33},... | collective-permute-start | bytes 393224 | tf_op jit(solution)/shard_map/ppermute | solution.py:507
  82.6 6.7 %collective-permute-start.2 = (f32[32,1024]{1,0:T(8,128)S(1)}, f32[32,1024]{1,0:T(8,128)S(1)}, u32[]{:S(2)}, u32[]{:S(2)}) collective-permute-start(f32[32,1024]{1,0:T(8,128)S(1)} %all_gather.18), channel_id=1, source_target_pairs={{0,64},{1,65},{2,66},{3,67},{4,96},{5,97},{6,98},{7,99},{8,0},{9,1... | collective-permute-start | bytes 393224 | tf_op jit(solution)/shard_map/ppermute | solution.py:507
  89.3 2.7 collective-permute-start.1
  92.0 1.9 collective-permute-start
  93.9 2.2 fusion
  101.8 2.6 all-gather.6.cloned.1.call-done
  107.2 8.6 %shard_map.69 = f32[1,64,128]{2,1,0:T(8,128)} custom-call(f32[1,4,2,64,128]{4,3,2,1,0:T(8,128)} %convolution_bitcast_fusion.x_ref), custom_call_target="tpu_custom_call" | custom-call | tf_op jit(solution)/shard_map/pallas_call | solution.py:446
  115.8 2.1 fusion.15
  123.9 1.9 slice.91.rest_0_
  127.9 18.9 %shard_map.70.low_ref = f32[2,1024,128]{2,1,0:T(8,128)} custom-call(f32[2,128,128]{2,1,0:T(8,128)} %pad_maximum_fusion.1.x_ref), custom_call_target="tpu_custom_call" | custom-call | tf_op jit(solution)/shard_map/pallas_call | solution.py:283
  146.8 2.3 slice.90.fac_ref
  149.2 24.5 %all-gather.8.cloned.1.call-done = f32[32,192,128]{2,1,0:T(8,128)} async-done(((f32[1,192,128]{2,1,0:T(8,128)}), f32[32,192,128]{2,1,0:T(8,128)}) %all-gather.8.cloned.1.call-update) | async-done | bytes 3145744 | tf_op jit(solution)/shard_map/all_gather | solution.py:526
  173.7 5.6 %shard_map.71 = (f32[2,128,128]{2,1,0:T(8,128)}, f32[2,64,128]{2,1,0:T(8,128)}, f32[2,512,128]{2,1,0:T(8,128)}) custom-call(s32[20]{0:T(128)} %pad_add_fusion.info_ref, f32[8,4,1,192,128]{4,3,2,1,0:T(8,128)} %bitcast.69, f32[2,1024,128]{2,1,0:T(8,128)} %shard_map.70.low_ref, f32[2,1024,128]{2,1,0:T(8,128)} %slice.90.fac_ref, f32[2,128,512]{2,1,0:T(8,128)} %slice.91.rest_0_, ...), custom_call_target="tpu_custom_call" | custom-call | tf_op jit(solution)/shard_map/pallas_call | solution.py:138
  179.2 10.4 %shard_map.72 = f32[2,64,128]{2,1,0:T(8,128)} custom-call(f32[2,4,2,64,128]{4,3,2,1,0:T(8,128)} %bitcast.86), custom_call_target="tpu_custom_call" | custom-call | tf_op jit(solution)/shard_map/pallas_call | solution.py:446
  191.2 2.3 slice.94.rest_0_
  194.9 3.1 %slice.93.fac_ref = f32[4,1024,128]{2,1,0:T(8,128)} slice(f32[7,1024,128]{2,1,0:T(8,128)} %all-gather.6.cloned.1.call-done), slice={[3:7], [0:1024], [0:128]} | slice | bytes 4194304 | tf_op jit(solution)/shard_map/slice | solution.py:577
  199.4 38.5 %all-gather.10.cloned.1.call-done = f32[64,128,128]{2,1,0:T(8,128)} async-done(((f32[2,128,128]{2,1,0:T(8,128)}), f32[64,128,128]{2,1,0:T(8,128)}) %all-gather.10.cloned.1.call-update) | async-done | bytes 4194320 | tf_op jit(solution)/shard_map/all_gather | solution.py:526
  239.7 8.6 %shard_map.73 = (f32[4,128,128]{2,1,0:T(8,128)}, f32[4,512,128]{2,1,0:T(8,128)}) custom-call(s32[38]{0:T(128)} %pad_add_fusion.1.info_ref, f32[8,4,2,128,128]{4,3,2,1,0:T(8,128)} %bitcast.73, f32[8,4,1,192,128]{4,3,2,1,0:T(8,128)} %bitcast.71, f32[4,1024,128]{2,1,0:T(8,128)} %slice.93.fac_ref, f32[4,128,512]{2,1,0:T(8,128)} %slice.94.rest_0_, ...), custom_call_target="tpu_custom_call" | custom-call | tf_op jit(solution)/shard_map/pallas_call | solution.py:138
  248.3 26.5 %shard_map.74 = f32[4,512,128]{2,1,0:T(8,128)} custom-call(f32[4,512,128]{2,1,0:T(8,128)} %get-tuple-element.20.x_ref), custom_call_target="tpu_custom_call" | custom-call | tf_op jit(solution)/shard_map/pallas_call | solution.py:383
  275.7 2.6 maximum_bitcast_fusion
  (78 shorter events, 27.0 us)
Async XLA Ops:
  8.0 1.5 copy-start
  8.0 96.4 %all-gather.6.cloned.1.call-start = ((), (), s32[]{:S(2)}) async-start(), calls=%async_computation.1 | async-start | bytes 4128768 | tf_op jit(solution)/shard_map/all_gather | solution.py:484
  61.8 3.9 %copy-start.6 = (f32[32,256]{1,0:T(8,128)S(1)}, f32[32,256]{1,0:T(8,128)}, u32[]{:S(2)}) copy-start(f32[32,256]{1,0:T(8,128)} %param.7) | copy-start | bytes 98308
  63.6 1.2 copy-start.1
  65.7 56.7 %reduce-scatter.2.cloned.1.call-start = ((), (), s32[]{:S(2)}) async-start(), calls=%async_computation.2 | async-start | bytes 1146880 | tf_op jit(solution)/shard_map/reduce_scatter | solution.py:488
  75.6 23.3 %collective-permute-start.3 = (f32[32,1024]{1,0:T(8,128)S(1)}, f32[32,1024]{1,0:T(8,128)S(1)}, u32[]{:S(2)}, u32[]{:S(2)}) collective-permute-start(f32[32,1024]{1,0:T(8,128)S(1)} %all_gather.18), channel_id=1, source_target_pairs={{0,96},{1,97},{2,98},{3,99},{4,0},{5,1},{6,2},{7,3},{8,32},{9,33},... | collective-permute-start | bytes 393224 | tf_op jit(solution)/shard_map/ppermute | solution.py:507
  82.6 16.3 %collective-permute-start.2 = (f32[32,1024]{1,0:T(8,128)S(1)}, f32[32,1024]{1,0:T(8,128)S(1)}, u32[]{:S(2)}, u32[]{:S(2)}) collective-permute-start(f32[32,1024]{1,0:T(8,128)S(1)} %all_gather.18), channel_id=1, source_target_pairs={{0,64},{1,65},{2,66},{3,67},{4,96},{5,97},{6,98},{7,99},{8,0},{9,1... | collective-permute-start | bytes 393224 | tf_op jit(solution)/shard_map/ppermute | solution.py:507
  89.3 10.2 %collective-permute-start.1 = (f32[32,1024]{1,0:T(8,128)S(1)}, f32[32,1024]{1,0:T(8,128)S(1)}, u32[]{:S(2)}, u32[]{:S(2)}) collective-permute-start(f32[32,1024]{1,0:T(8,128)S(1)} %all_gather.18), channel_id=1, source_target_pairs={{0,32},{1,33},{2,34},{3,35},{4,64},{5,65},{6,66},{7,67},{8,96},{9,... | collective-permute-start | bytes 393224 | tf_op jit(solution)/shard_map/ppermute | solution.py:507
  92.0 9.1 %collective-permute-start = (f32[32,1024]{1,0:T(8,128)S(1)}, f32[32,1024]{1,0:T(8,128)S(1)}, u32[]{:S(2)}, u32[]{:S(2)}) collective-permute-start(f32[32,1024]{1,0:T(8,128)S(1)} %all_gather.18), channel_id=1, source_target_pairs={{0,0},{1,1},{2,2},{3,3},{4,32},{5,33},{6,34},{7,35},{8,64},{9,65},... | collective-permute-start | bytes 393224 | tf_op jit(solution)/shard_map/ppermute | solution.py:507
  93.9 2.3 copy-start.7
  96.2 77.5 %all-gather.8.cloned.1.call-start = ((), (), s32[]{:S(2)}) async-start(), calls=%async_computation.3 | async-start | bytes 3244032 | tf_op jit(solution)/shard_map/all_gather | solution.py:526
  120.3 2.1 copy-start.5
  123.8 114.0 %all-gather.10.cloned.1.call-start = ((), (), s32[]{:S(2)}) async-start(), calls=%async_computation.4 | async-start | bytes 4325376 | tf_op jit(solution)/shard_map/all_gather | solution.py:526
  179.2 14.4 %copy-start.8 = (s32[1,4]{1,0:T(1,128)S(1)}, s32[1,4]{1,0:T(1,128)}, u32[]{:S(2)}) copy-start(s32[1,4]{1,0:T(1,128)} %param.11) | copy-start | bytes 52
  179.2 15.0 %copy-start.3 = (f32[7,64,128]{2,1,0:T(8,128)S(1)}, f32[7,64,128]{2,1,0:T(8,128)}, u32[]{:S(2)}) copy-start(f32[7,64,128]{2,1,0:T(8,128)} %reduce-scatter.2.cloned.1.call-done) | copy-start | bytes 688132
  248.3 26.6 %copy-start.2 = (f32[4,128,128]{2,1,0:T(8,128)S(1)}, f32[4,128,128]{2,1,0:T(8,128)}, u32[]{:S(2)}) copy-start(f32[4,128,128]{2,1,0:T(8,128)} %get-tuple-element.19) | copy-start | bytes 786436
  248.3 26.6 %copy-start.4 = (f32[2,128,128]{2,1,0:T(8,128)S(1)}, f32[2,128,128]{2,1,0:T(8,128)}, u32[]{:S(2)}) copy-start(f32[2,128,128]{2,1,0:T(8,128)} %get-tuple-element.16) | copy-start | bytes 393220
Sparse Core Ops, SparseCore 0:
  65.8 38.5 all-gather.5
Sparse Core Ops, SparseCore 1:
  96.3 22.2 reduce-scatter.1
  123.9 49.7 all-gather.7
  191.3 46.5 all-gather.9

commit v20 on v17

--- a/solution.py
+++ b/solution.py
@@ -43,8 +43,14 @@
     )
 
 
-def level_kernel(info_ref, par_ref, low_ref, fac_ref, out_ref, *rest, level, tile, band, own_tiles, slot_count,
-                 par_prow, low_prow, halves):
+def level_kernel(info_ref, par_ref, low_ref, fac_ref, *rest, level, tile, band, own_tiles, slot_count,
+                 par_prow, low_prow, halves, with_diag):
+    extra = ()
+    if with_diag:
+        extra = (rest[0], rest[1], rest[3])
+        rest = (rest[2],) + rest[4:]
+    out_ref = rest[0]
+    rest = rest[1:]
     count = out_ref.shape[0]
     split = tile // band
     r = info_ref[0]
@@ -108,24 +114,33 @@
         def _():
             out_ref[i] = jnp.zeros((tile, tile), jnp.float32)
 
+        if extra:
+            rows_ref, gram_ref, diag_ref = extra
+            diag_ref[i] = dot_t_hi(rows_ref[i], out_ref[i])
+            start = pl.multiple_of(r * band, band)
+            diag_ref[i, pl.ds(start, band), :] = diag_ref[i, pl.ds(start, band), :] + gram_ref[i]
+
 
 def level_products(info, parent_data, low_data, factors, level, tile, band, own_tiles, slot_count,
-                   par_prow, low_prow, halves):
+                   par_prow, low_prow, halves, diag_inputs=()):
     kernel = functools.partial(
         level_kernel, level=level, tile=tile, band=band, own_tiles=own_tiles, slot_count=slot_count,
-        par_prow=par_prow, low_prow=low_prow, halves=halves,
+        par_prow=par_prow, low_prow=low_prow, halves=halves, with_diag=bool(diag_inputs),
     )
     vmem = pl.BlockSpec(memory_space=pltpu.VMEM)
     count = factors.shape[0]
     shapes = [jax.ShapeDtypeStruct((count, tile, tile), jnp.float32)]
     if halves:
         shapes.append(jax.ShapeDtypeStruct((count, tile // halves, tile), jnp.float32))
+    if diag_inputs:
+        width = diag_inputs[0].shape[2]
+        shapes.append(jax.ShapeDtypeStruct((count, width, tile), jnp.float32))
     return pl.pallas_call(
         kernel,
         out_shape=tuple(shapes),
-        in_specs=[pl.BlockSpec(memory_space=pltpu.SMEM), vmem, vmem, vmem],
+        in_specs=[pl.BlockSpec(memory_space=pltpu.SMEM)] + [vmem] * (3 + len(diag_inputs)),
         out_specs=tuple([vmem] * len(shapes)),
-    )(info, parent_data, low_data, factors)
+    )(info, parent_data, low_data, factors, *diag_inputs)
 
 
 def reduce_kernel(x_ref, out_ref, recv_ref, send_sem, recv_sem, back_send, back_recv, *, axis, count, band, gather):
@@ -541,7 +556,7 @@
     live_here = jnp.take(living, r, axis=1).astype(jnp.float32)
     factor_rows = factor_rows * live_here[:, None, None]
     factor_tile = lax.dynamic_slice_in_dim(factor_rows, c * tile, tile, 2)
-    factor_cols = pair_gather(factor_tile, row_count, 5)
+    factor_cols = lax.all_gather(factor_tile, "row", axis=1, tiled=True)
 
     inverse_band = lax.dynamic_slice_in_dim(inverse, r * band, band, 2)
     partial_gram = mm(jnp.transpose(inverse_band, (0, 2, 1)), inverse)
@@ -614,7 +629,7 @@
     ]
     tied_out = []
     gathered_0 = reduce_and_gather(0, product_0[None], product_0[None], [], jnp.concatenate(lifted, axis=0))
-    lifted_cols = axis_gather(tied_out[0], "row", row_count, 4)
+    lifted_cols = pair_gather(tied_out[0], row_count, 4)
 
     info_1 = jnp.concatenate(
         [r.astype(jnp.int32)[None], picks_all[0:2].reshape(-1), jnp.zeros((2,), jnp.int32), c.astype(jnp.int32)[None]]
@@ -630,15 +645,11 @@
         [r.astype(jnp.int32)[None], picks_all[2:nodes - 1].reshape(-1), (parents - 1).astype(jnp.int32),
          c.astype(jnp.int32)[None]]
     )
-    (product_2,) = level_products(
+    product_2, partial_2 = level_products(
         info_2, gathered_1, gathered_0, factor_cols[3:nodes], 2, tile, band, own_tiles, slot_count,
-        tile // halves, tile, 0,
-    )
-    first_2 = 3
-    count_2 = product_2.shape[0]
-    gram_rows = jnp.zeros((count_2, width, tile), jnp.float32)
-    gram_rows = lax.dynamic_update_slice_in_dim(gram_rows, gram_piece[first_2:first_2 + count_2], r * band, 1)
-    diag_2 = pair_reduce(diag_partial(first_2, product_2) + gram_rows, row_count, 2)
+        tile // halves, tile, 0, (factor_rows[3:nodes], gram_piece[3:nodes]),
+    )
+    diag_2 = pair_reduce(partial_2, row_count, 2)
 
     products = jnp.concatenate([product_0[None], product_1, product_2], axis=0)
     diag_cols = jnp.concatenate(

time: 321 us -> 285 us (0.89)
  Pallas kernels: 164 us -> 121 us
  waiting for transfers between devices: 62.4 us -> 73.1 us
  other arithmetic: 17.3 us -> 13 us
    pallas_call x1 -> x0, Pallas kernels: 19.3 us -> none  [axis_gather(): pl.pallas_call(functools.partial(gather_kernel, axis=axis, count=count, b...]
    pallas_call x1, Pallas kernels: 31.7 us -> 13.5 us  [pair_gather(): pl.pallas_call(functools.partial(pair_gather_kernel, chips=chips, rows=ro...]
    pallas_call x1, Pallas kernels: 56.6 us -> 48.4 us  [axis_reduce(): pl.pallas_call(kernel, out_shape=jax.ShapeDtypeStruct((lead, out_rows, la...]
    all_gather x2, waiting for transfers between devices: 62.3 us -> 68.1 us  [reduce_and_gather(): everything = lax.all_gather(both, ('row', 'col'), axis=0)]
    dot_general x8 -> x7, matrix products: 15.1 us -> 13 us  [mm(): jnp.matmul(a, b, precision=HIGHEST, preferred_element_type=jnp.float32)]
  transfers between devices with their start and end apart: 7 -> 8, of which waited for: 2 -> 5; matrix products, arithmetic and copies ran while one was open for 11% -> 9% of each run, Pallas kernels for 36% -> 8%
where the time goes in v20:
time: 285 us
  Pallas kernels  121 us (42%)
  waiting for transfers between devices  73.1 us (26%)
  local copies, waits for them, and re-layouts  20.2 us (7%)
  starting transfers between devices  18.5 us (6%)
  between operations  16 us (6%)
  other arithmetic  13 us (5%)
  matrix products  13 us (5%)
  blocking collectives  9.78 us (3%)
    all_gather x2, waiting for transfers between devices, reduce_and_gather(): everything = lax.all_gather(both, ('row', 'col'), axis=0)  68.1 us
    pallas_call x1, Pallas kernels, axis_reduce(): pl.pallas_call(kernel, out_shape=jax.ShapeDtypeStruct((lead, out_rows, la...  48.4 us
    pallas_call x1, Pallas kernels, pair_reduce(): pl.pallas_call(functools.partial(pair_reduce_kernel, band=band, chips=chi...  26.5 us
    pallas_call x2, Pallas kernels, pair_scatter(): pl.pallas_call(functools.partial(pair_scatter_kernel, chips=chips), out_s...  19.4 us
    ppermute x4, starting transfers between devices, body(): rounds.append(lax.ppermute(chunk_rows, ('leaf', 'row', 'col'), pairs))  18.3 us
    pallas_call x1, Pallas kernels, pair_gather(): pl.pallas_call(functools.partial(pair_gather_kernel, chips=chips, rows=ro...  13.5 us
    pallas_call x2, Pallas kernels, level_products(): pl.pallas_call(kernel, out_shape=tuple(shapes), in_specs=[pl.BlockSpec(me...  13.3 us
    dot_general x7, matrix products, mm(): jnp.matmul(a, b, precision=HIGHEST, preferred_element_type=jnp.float32)  13 us
  transfers between devices with their start and end apart: 8, of which 5 were waited for; matrix products, arithmetic and copies ran while one was open for 9% of the time, Pallas kernels for 8%

profile of v20, /device:TPU:1, one launch (start us, length us, event | category | flops | bytes accessed | tf_op | source)
XLA Modules:
  0.0 284.6 jit_solution(3045484840529998357)
XLA Ops:
  9.5 3.9 %fusion.2.x_ref = f32[7,128,512]{2,1,0:T(8,128)} fusion(f32[1,7,128,512]{3,2,1,0:T(8,128)S(1)} %copy-done, f32[1,7,128,128]{3,2,1,0:T(8,128)} %param.8), kind=kOutput, calls=%fused_computation.6 | convolution fusion | flops 704643072 | bytes 4128768 | tf_op jit(solution)/shard_map/dot_general | solution.py:15
  13.4 48.4 %shard_map.68 = f32[7,128,512]{2,1,0:T(8,128)} custom-call(f32[7,128,512]{2,1,0:T(8,128)} %fusion.2.x_ref), custom_call_target="tpu_custom_call" | custom-call | tf_op jit(solution)/shard_map/pallas_call | solution.py:220
  61.8 1.8 broadcast_multiply_fusion
  65.8 9.8 %all_gather.18 = f32[32,1024]{1,0:T(8,128)S(1)} all-gather(f32[32,256]{1,0:T(8,128)S(1)} %copy-done.7), channel_id=1, replica_groups=mesh['leaf'=4,'row'=8,'col'=4] {'col'}, dimensions={1}, use_global_device_ids=true | all-gather | bytes 163840 | tf_op jit(solution)/shard_map/all_gather | solution.py:567
  75.6 7.0 %collective-permute-start.3 = (f32[32,1024]{1,0:T(8,128)S(1)}, f32[32,1024]{1,0:T(8,128)S(1)}, u32[]{:S(2)}, u32[]{:S(2)}) collective-permute-start(f32[32,1024]{1,0:T(8,128)S(1)} %all_gather.18), channel_id=1, source_target_pairs={{0,96},{1,97},{2,98},{3,99},{4,0},{5,1},{6,2},{7,3},{8,32},{9,33},... | collective-permute-start | bytes 393224 | tf_op jit(solution)/shard_map/ppermute | solution.py:582
  82.6 6.7 %collective-permute-start.2 = (f32[32,1024]{1,0:T(8,128)S(1)}, f32[32,1024]{1,0:T(8,128)S(1)}, u32[]{:S(2)}, u32[]{:S(2)}) collective-permute-start(f32[32,1024]{1,0:T(8,128)S(1)} %all_gather.18), channel_id=1, source_target_pairs={{0,64},{1,65},{2,66},{3,67},{4,96},{5,97},{6,98},{7,99},{8,0},{9,1... | collective-permute-start | bytes 393224 | tf_op jit(solution)/shard_map/ppermute | solution.py:582
  89.3 2.7 collective-permute-start.1
  92.0 1.9 collective-permute-start
  93.9 2.2 fusion
  101.8 2.6 all-gather.6.cloned.1.call-done
  107.2 8.6 %shard_map.69 = f32[1,64,128]{2,1,0:T(8,128)} custom-call(f32[1,4,2,64,128]{4,3,2,1,0:T(8,128)} %convolution_bitcast_fusion.x_ref), custom_call_target="tpu_custom_call" | custom-call | tf_op jit(solution)/shard_map/pallas_call | solution.py:446
  115.8 2.1 fusion.15
  124.6 13.5 %shard_map.70.low_ref = f32[2,1024,128]{2,1,0:T(8,128)} custom-call(f32[2,128,128]{2,1,0:T(8,128)} %pad_maximum_fusion.1.x_ref), custom_call_target="tpu_custom_call" | custom-call | tf_op jit(solution)/shard_map/pallas_call | solution.py:525
  138.1 2.3 slice.90.fac_ref
  140.5 30.0 %all-gather.8.cloned.1.call-done = f32[32,192,128]{2,1,0:T(8,128)} async-done(((f32[1,192,128]{2,1,0:T(8,128)}), f32[32,192,128]{2,1,0:T(8,128)}) %all-gather.8.cloned.1.call-update) | async-done | bytes 3145744 | tf_op jit(solution)/shard_map/all_gather | solution.py:598
  170.5 4.6 %shard_map.71 = (f32[2,128,128]{2,1,0:T(8,128)}, f32[2,64,128]{2,1,0:T(8,128)}) custom-call(s32[20]{0:T(128)} %pad_add_fusion.info_ref, f32[8,4,1,192,128]{4,3,2,1,0:T(8,128)} %bitcast.71, f32[2,1024,128]{2,1,0:T(8,128)} %shard_map.70.low_ref, f32[2,1024,128]{2,1,0:T(8,128)} %slice.90.fac_ref), custom_call_target="tpu_custom_call" | custom-call | tf_op jit(solution)/shard_map/pallas_call | solution.py:138
  175.1 2.9 %fusion.16 = f32[2,512,128]{2,1,0:T(8,128)} fusion(f32[7,128,512]{2,1,0:T(8,128)} %copy-done.1, f32[2,128,128]{2,1,0:T(8,128)} %get-tuple-element.15), kind=kOutput, calls=%fused_computation.66 | convolution fusion | flops 201326592 | bytes 2490368 | tf_op jit(solution)/shard_map/dot_general | solution.py:15
  178.0 10.7 %shard_map.72 = f32[2,64,128]{2,1,0:T(8,128)} custom-call(f32[2,4,2,64,128]{4,3,2,1,0:T(8,128)} %bitcast.82), custom_call_target="tpu_custom_call" | custom-call | tf_op jit(solution)/shard_map/pallas_call | solution.py:446
  190.3 2.3 slice.93.rest_0_
  194.0 3.1 %slice.92.fac_ref = f32[4,1024,128]{2,1,0:T(8,128)} slice(f32[7,1024,128]{2,1,0:T(8,128)} %all-gather.6.cloned.1.call-done), slice={[3:7], [0:1024], [0:128]} | slice | bytes 4194304 | tf_op jit(solution)/shard_map/slice | solution.py:649
  198.5 38.1 %all-gather.10.cloned.1.call-done = f32[64,128,128]{2,1,0:T(8,128)} async-done(((f32[2,128,128]{2,1,0:T(8,128)}), f32[64,128,128]{2,1,0:T(8,128)}) %all-gather.10.cloned.1.call-update) | async-done | bytes 4194320 | tf_op jit(solution)/shard_map/all_gather | solution.py:598
  238.4 8.6 %shard_map.73 = (f32[4,128,128]{2,1,0:T(8,128)}, f32[4,512,128]{2,1,0:T(8,128)}) custom-call(s32[38]{0:T(128)} %pad_add_fusion.1.info_ref, f32[8,4,2,128,128]{4,3,2,1,0:T(8,128)} %bitcast.75, f32[8,4,1,192,128]{4,3,2,1,0:T(8,128)} %bitcast.73, f32[4,1024,128]{2,1,0:T(8,128)} %slice.92.fac_ref, f32[4,128,512]{2,1,0:T(8,128)} %slice.93.rest_0_, ...), custom_call_target="tpu_custom_call" | custom-call | tf_op jit(solution)/shard_map/pallas_call | solution.py:138
  247.0 26.5 %shard_map.74 = f32[4,512,128]{2,1,0:T(8,128)} custom-call(f32[4,512,128]{2,1,0:T(8,128)} %get-tuple-element.18.x_ref), custom_call_target="tpu_custom_call" | custom-call | tf_op jit(solution)/shard_map/pallas_call | solution.py:383
  274.4 2.6 maximum_bitcast_fusion
  (80 shorter events, 25.6 us)
Async XLA Ops:
  8.0 1.5 copy-start
  8.0 96.4 %all-gather.6.cloned.1.call-start = ((), (), s32[]{:S(2)}) async-start(), calls=%async_computation.1 | async-start | bytes 4128768 | tf_op jit(solution)/shard_map/all_gather | solution.py:559
  61.8 3.9 %copy-start.7 = (f32[32,256]{1,0:T(8,128)S(1)}, f32[32,256]{1,0:T(8,128)}, u32[]{:S(2)}) copy-start(f32[32,256]{1,0:T(8,128)} %param.7) | copy-start | bytes 98308
  63.6 1.2 copy-start.1
  65.7 56.7 %reduce-scatter.2.cloned.1.call-start = ((), (), s32[]{:S(2)}) async-start(), calls=%async_computation.2 | async-start | bytes 1146880 | tf_op jit(solution)/shard_map/reduce_scatter | solution.py:563
  75.6 23.3 %collective-permute-start.3 = (f32[32,1024]{1,0:T(8,128)S(1)}, f32[32,1024]{1,0:T(8,128)S(1)}, u32[]{:S(2)}, u32[]{:S(2)}) collective-permute-start(f32[32,1024]{1,0:T(8,128)S(1)} %all_gather.18), channel_id=1, source_target_pairs={{0,96},{1,97},{2,98},{3,99},{4,0},{5,1},{6,2},{7,3},{8,32},{9,33},... | collective-permute-start | bytes 393224 | tf_op jit(solution)/shard_map/ppermute | solution.py:582
  82.6 16.2 %collective-permute-start.2 = (f32[32,1024]{1,0:T(8,128)S(1)}, f32[32,1024]{1,0:T(8,128)S(1)}, u32[]{:S(2)}, u32[]{:S(2)}) collective-permute-start(f32[32,1024]{1,0:T(8,128)S(1)} %all_gather.18), channel_id=1, source_target_pairs={{0,64},{1,65},{2,66},{3,67},{4,96},{5,97},{6,98},{7,99},{8,0},{9,1... | collective-permute-start | bytes 393224 | tf_op jit(solution)/shard_map/ppermute | solution.py:582
  89.3 10.2 %collective-permute-start.1 = (f32[32,1024]{1,0:T(8,128)S(1)}, f32[32,1024]{1,0:T(8,128)S(1)}, u32[]{:S(2)}, u32[]{:S(2)}) collective-permute-start(f32[32,1024]{1,0:T(8,128)S(1)} %all_gather.18), channel_id=1, source_target_pairs={{0,32},{1,33},{2,34},{3,35},{4,64},{5,65},{6,66},{7,67},{8,96},{9,... | collective-permute-start | bytes 393224 | tf_op jit(solution)/shard_map/ppermute | solution.py:582
  92.0 9.1 %collective-permute-start = (f32[32,1024]{1,0:T(8,128)S(1)}, f32[32,1024]{1,0:T(8,128)S(1)}, u32[]{:S(2)}, u32[]{:S(2)}) collective-permute-start(f32[32,1024]{1,0:T(8,128)S(1)} %all_gather.18), channel_id=1, source_target_pairs={{0,0},{1,1},{2,2},{3,3},{4,32},{5,33},{6,34},{7,35},{8,64},{9,65},... | collective-permute-start | bytes 393224 | tf_op jit(solution)/shard_map/ppermute | solution.py:582
  93.9 2.3 copy-start.8
  96.2 74.3 %all-gather.8.cloned.1.call-start = ((), (), s32[]{:S(2)}) async-start(), calls=%async_computation.3 | async-start | bytes 3244032 | tf_op jit(solution)/shard_map/all_gather | solution.py:598
  120.3 2.1 copy-start.5
  123.8 112.8 %all-gather.10.cloned.1.call-start = ((), (), s32[]{:S(2)}) async-start(), calls=%async_computation.4 | async-start | bytes 4325376 | tf_op jit(solution)/shard_map/all_gather | solution.py:598
  175.1 13.6 %copy-start.4 = (f32[7,64,128]{2,1,0:T(8,128)S(1)}, f32[7,64,128]{2,1,0:T(8,128)}, u32[]{:S(2)}) copy-start(f32[7,64,128]{2,1,0:T(8,128)} %reduce-scatter.2.cloned.1.call-done) | copy-start | bytes 688132
  175.1 14.5 %copy-start.6 = (f32[2,64,128]{2,1,0:T(8,128)S(1)}, f32[2,64,128]{2,1,0:T(8,128)}, u32[]{:S(2)}) copy-start(f32[2,64,128]{2,1,0:T(8,128)} %get-tuple-element.16) | copy-start | bytes 196612
  178.0 14.7 %copy-start.9 = (s32[1,4]{1,0:T(1,128)S(1)}, s32[1,4]{1,0:T(1,128)}, u32[]{:S(2)}) copy-start(s32[1,4]{1,0:T(1,128)} %param.11) | copy-start | bytes 52
  247.0 26.6 %copy-start.2 = (f32[2,128,128]{2,1,0:T(8,128)S(1)}, f32[2,128,128]{2,1,0:T(8,128)}, u32[]{:S(2)}) copy-start(f32[2,128,128]{2,1,0:T(8,128)} %get-tuple-element.15) | copy-start | bytes 393220
  247.0 26.6 %copy-start.3 = (f32[4,128,128]{2,1,0:T(8,128)S(1)}, f32[4,128,128]{2,1,0:T(8,128)}, u32[]{:S(2)}) copy-start(f32[4,128,128]{2,1,0:T(8,128)} %get-tuple-element.17) | copy-start | bytes 786436
Sparse Core Ops, SparseCore 0:
  65.8 38.5 all-gather.5
Sparse Core Ops, SparseCore 1:
  96.3 22.2 reduce-scatter.1
  123.9 46.5 all-gather.7
  190.4 46.1 all-gather.9
